TPU v7x, 128 devices: a whole 4x4x4 slice. The times are simulated.
128 devices in a mesh: req: 16 (over z, y), tp: 8 (over x, core).
Axes of the slice: x: 4, y: 4, z: 4, core: 2. Of those that a mesh axis runs over, the one named last changes fastest.
Arguments:
- hidden_in: bfloat16 [4096, 1024], P('req'), may hold values from -42 to 42
- prompt_kv: bfloat16 [2, 128, 512, 1024], P(None, 'req', None, 'tp'), may hold values from -9 to 9
- tail_kv: bfloat16 [2, 4096, 64, 1024], P(None, 'req', None, 'tp'), may hold values from -9 to 9
- group_of: int32 [4096], P('req'), may hold values from 0 to 7
- prompt_len: int32 [128], P('req'), may hold values from 64 to 512, as said below
- tail_len: int32 [4096], P('req'), may hold values from 0 to 63, as said below
- bucket_of: int32 [577], replicated, may hold values from 0 to 31, never falling along the last dimension, each value on 1 to 38 neighbouring positions
- bias_table: float32 [32, 16], P(None, 'tp'), may hold values from -6 to 302
- attn_gain: float32 [1024], replicated, may hold values from 0.1 to 1.9
- w_query: bfloat16 [1024, 1024], P(None, 'tp'), may hold values from -0.1875 to 0.1875
- w_key: bfloat16 [1024, 1024], P(None, 'tp'), may hold values from -0.1875 to 0.1875
- w_value: bfloat16 [1024, 1024], P(None, 'tp'), may hold values from -0.1875 to 0.1875
- w_out: bfloat16 [1024, 1024], P('tp'), may hold values from -0.75 to 0.75
- ffn_gain: float32 [1024], replicated, may hold values from 0.1 to 1.9
- router_weight: bfloat16 [1024, 16], replicated, may hold values from -0.1875 to 0.1875
- expert_ids: int32 [4096, 2], P('req'), may hold values from 0 to 15, all different within a row; in each aligned block of 256 rows (0 to 255, 256 to 511, ...) at most 40 rows name the same one
- w_gate: bfloat16 [16, 1024, 2816], P('req', None, 'tp'), may hold values from -0.1875 to 0.1875
- w_up: bfloat16 [16, 1024, 2816], P('req', None, 'tp'), may hold values from -0.1875 to 0.1875
- w_down: bfloat16 [16, 2816, 1024], P('req', 'tp'), may hold values from -0.109375 to 0.109375
- new_slot: int32 [4096], replicated, may hold values from 0 to 4095, as said below
Outputs:
- out_hidden: bfloat16 [4096, 1024], P('req')
- new_tail_kv: bfloat16 [2, 4096, 64, 1024], P(None, 'req', None, 'tp')
Inputs may be any that keep to these rules, and one draw needn't show every extreme that they name: `expert_ids`: in each replica's aligned block of 256 tokens no expert is named by more than 40 of them, a bound that some block reaches. `new_slot`: A permutation. Exactly 4 requests of each replica are movers; all movers of one replica go to one replica (possibly itself), each taking a slot that a mover of that replica leaves; every other request keeps its slot. `prompt_len`: each replica has a group of 512 rows. `tail_len`: each replica has a request of 63 own rows and one of none.
All inputs are finite; a program needn't handle non-finite values.
Results may differ from a plain program's by a relative error of at most 0.013.
Values may be sent and summed in bfloat16 or wider, within the bound.
A program may use at most 128 MiB of HBM per device.

v0:
```python
import jax
import jax.numpy as jnp
from jax import lax
from jax.sharding import PartitionSpec as P

HD = 64
TOP = 2
MIG = 4


EPS = 1e-06


def rms_scale(values, gain):
    v = values.astype(jnp.float32)
    return (v * lax.rsqrt(jnp.mean(v * v, axis=-1, keepdims=True) + EPS) * gain).astype(
        jnp.bfloat16
    )


def bias_lookup(distance, starts, finish, bias_table):
    within = (distance[..., None] >= starts) & (distance[..., None] < finish)
    return jnp.einsum(
        "rjk,kh->hrj", within.astype(jnp.float32), bias_table, precision=lax.Precision.HIGHEST
    )


def attention(
    hidden_in,
    prompt_kv,
    tail_kv,
    group_of,
    prompt_len,
    tail_len,
    bucket_of,
    bias_table,
    attn_gain,
    w_query,
    w_key,
    w_value,
):
    normed = rms_scale(hidden_in, attn_gain)
    query = jnp.dot(normed, w_query, preferred_element_type=jnp.float32).astype(jnp.bfloat16)
    key_new = jnp.dot(normed, w_key, preferred_element_type=jnp.float32).astype(jnp.bfloat16)
    value_new = jnp.dot(normed, w_value, preferred_element_type=jnp.float32).astype(jnp.bfloat16)
    rows = hidden_in.shape[0]
    heads_here = w_query.shape[1] // HD
    groups_here = prompt_kv.shape[1]
    prompt_rows = prompt_kv.shape[2]
    tail_rows = tail_kv.shape[2]
    span = bucket_of.shape[0]
    buckets = bias_table.shape[0]
    bucket_ids = jnp.arange(buckets, dtype=jnp.int32)
    starts = jnp.sum((bucket_of[:, None] < bucket_ids[None, :]).astype(jnp.int32), axis=0)
    finish = jnp.concatenate([starts[1:], jnp.full((1,), span, jnp.int32)])
    first_bias = jnp.sum(jnp.where((bucket_ids == bucket_of[0])[:, None], bias_table, 0.0), axis=0)
    scale = HD ** (-0.5)
    q = query.reshape(rows, heads_here, HD)
    pk = prompt_kv[0].reshape(groups_here, prompt_rows, heads_here, HD)
    pv = prompt_kv[1].reshape(groups_here, prompt_rows, heads_here, HD)
    tk = tail_kv[0].reshape(rows, tail_rows, heads_here, HD)
    tv = tail_kv[1].reshape(rows, tail_rows, heads_here, HD)
    kn = key_new.reshape(rows, heads_here, HD)
    vn = value_new.reshape(rows, heads_here, HD)
    group_hit = group_of[:, None] == jnp.arange(groups_here, dtype=jnp.int32)[None, :]
    own_len = jnp.sum(jnp.where(group_hit, prompt_len[None, :], 0), axis=1)
    pos = own_len + tail_len
    jpos = jnp.arange(prompt_rows, dtype=jnp.int32)
    pidx = jnp.clip(pos[:, None] - jpos[None, :], 0, span - 1)
    pbias = bias_lookup(pidx, starts, finish, bias_table)
    pmask = group_hit[:, :, None] & (jpos[None, None, :] < own_len[:, None, None])
    ps = (
        jnp.einsum("rhd,gjhd->hrgj", q, pk, preferred_element_type=jnp.float32) * scale
        + pbias[:, :, None, :]
    )
    ps = jnp.where(pmask[None], ps, -jnp.inf)
    tpos = jnp.arange(tail_rows, dtype=jnp.int32)
    tidx = jnp.clip(tail_len[:, None] - tpos[None, :], 0, span - 1)
    tbias = bias_lookup(tidx, starts, finish, bias_table)
    tmask = tpos[None, :] < tail_len[:, None]
    ts = jnp.einsum("rhd,rthd->hrt", q, tk, preferred_element_type=jnp.float32) * scale + tbias
    ts = jnp.where(tmask[None], ts, -jnp.inf)
    ns = (
        jnp.einsum("rhd,rhd->hr", q, kn, preferred_element_type=jnp.float32) * scale
        + first_bias[:, None]
    )
    top = jnp.maximum(jnp.maximum(jnp.max(ps, axis=(2, 3)), jnp.max(ts, axis=2)), ns)
    pe = jnp.exp(ps - top[:, :, None, None])
    te = jnp.exp(ts - top[:, :, None])
    ne = jnp.exp(ns - top)
    total = jnp.sum(pe, axis=(2, 3)) + jnp.sum(te, axis=2) + ne
    pw = (pe / total[:, :, None, None]).astype(jnp.bfloat16)
    tw = (te / total[:, :, None]).astype(jnp.bfloat16)
    nw = (ne / total).astype(jnp.bfloat16)
    head = jnp.einsum("hrgj,gjhd->rhd", pw, pv, preferred_element_type=jnp.float32)
    head = head + jnp.einsum("hrt,rthd->rhd", tw, tv, preferred_element_type=jnp.float32)
    head = head + jnp.einsum("hr,rhd->rhd", nw, vn, preferred_element_type=jnp.float32)
    head_out = head.reshape(rows, heads_here * HD).astype(jnp.bfloat16)
    return (head_out, key_new, value_new, tmask)


def body(
    hidden_in,
    prompt_kv,
    tail_kv,
    group_of,
    prompt_len,
    tail_len,
    bucket_of,
    bias_table,
    attn_gain,
    w_query,
    w_key,
    w_value,
    w_out,
    ffn_gain,
    router_weight,
    expert_ids,
    w_gate,
    w_up,
    w_down,
    new_slot,
):
    head_out, key_new, value_new, tmask = attention(
        hidden_in,
        prompt_kv,
        tail_kv,
        group_of,
        prompt_len,
        tail_len,
        bucket_of,
        bias_table,
        attn_gain,
        w_query,
        w_key,
        w_value,
    )
    rows = hidden_in.shape[0]
    width = hidden_in.shape[1]
    local_idx = jnp.arange(rows, dtype=jnp.int32)
    tail_rows = tail_kv.shape[2]
    write_row = jnp.arange(tail_rows, dtype=jnp.int32)[None, :] == tail_len[:, None]
    fresh = jnp.stack([key_new, value_new])[:, :, None, :]
    tail_new = jnp.where(write_row[None, :, :, None], fresh, tail_kv)
    partial_attn = jnp.dot(head_out, w_out, preferred_element_type=jnp.float32)
    attn = lax.psum(partial_attn, "tp")
    resid = (hidden_in.astype(jnp.float32) + attn).astype(jnp.bfloat16)
    normed2 = rms_scale(resid, ffn_gain)
    logits = jnp.dot(normed2, router_weight, preferred_element_type=jnp.float32)
    experts = router_weight.shape[1]
    expert_range = jnp.arange(experts, dtype=jnp.int32)
    first_hit = expert_ids[:, 0:1] == expert_range[None, :]
    second_hit = expert_ids[:, 1:2] == expert_range[None, :]
    picked_first = jnp.sum(jnp.where(first_hit, logits, 0.0), axis=1)
    picked_second = jnp.sum(jnp.where(second_hit, logits, 0.0), axis=1)
    gate_first = jax.nn.sigmoid(picked_first - picked_second)
    capacity = 5 * rows * TOP // (4 * experts)
    flat_e = expert_ids.reshape(-1)
    onehot = (flat_e[:, None] == expert_range[None, :]).astype(jnp.int32)
    slot_pos = jnp.sum((jnp.cumsum(onehot, axis=0) - 1) * onehot, axis=1)
    target = flat_e * capacity + slot_pos
    placed = (target[:, None] == jnp.arange(experts * capacity, dtype=jnp.int32)[None, :]).astype(
        jnp.bfloat16
    )
    doubled = jnp.repeat(normed2, TOP, axis=0)
    outgoing = (
        jnp.dot(placed.T, doubled, preferred_element_type=jnp.float32)
        .astype(jnp.bfloat16)
        .reshape(experts, capacity, width)
    )
    gate_mat = w_gate[0]
    up_mat = w_up[0]
    down_mat = w_down[0]
    received = lax.all_to_all(outgoing, "req", split_axis=0, concat_axis=0, tiled=True)
    flat = received.reshape(-1, received.shape[-1])
    gate_h = jnp.dot(flat, gate_mat, preferred_element_type=jnp.float32)
    up_h = jnp.dot(flat, up_mat, preferred_element_type=jnp.float32)
    act = (jax.nn.gelu(gate_h, approximate=True) * up_h).astype(jnp.bfloat16)
    summed = lax.psum(
        jnp.dot(act, down_mat, preferred_element_type=jnp.float32).astype(jnp.bfloat16), "tp"
    )
    back = summed.reshape(received.shape)
    result = lax.all_to_all(back, "req", split_axis=0, concat_axis=0, tiled=True)
    pair_out = jnp.dot(
        placed, result.reshape(experts * capacity, width), preferred_element_type=jnp.float32
    ).reshape(rows, TOP, width)
    mixed = (
        resid.astype(jnp.float32)
        + gate_first[:, None] * pair_out[:, 0]
        + (1.0 - gate_first)[:, None] * pair_out[:, 1]
    ).astype(jnp.bfloat16)
    replicas = lax.axis_size("req")
    me = lax.axis_index("req")
    total_reqs = new_slot.shape[0]
    everyone = jnp.arange(total_reqs, dtype=jnp.int32)
    leaving_all = new_slot // rows != everyone // rows
    rank_all = (
        jnp.cumsum(leaving_all.reshape(replicas, rows).astype(jnp.int32), axis=1) - 1
    ).reshape(-1)
    source_of = jnp.zeros((total_reqs,), jnp.int32).at[new_slot].set(everyone)
    first_slot = me * rows
    leaving = lax.dynamic_slice_in_dim(leaving_all, first_slot, rows, 0)
    my_rank = lax.dynamic_slice_in_dim(rank_all, first_slot, rows, 0)
    send_idx = (
        jnp.zeros((MIG,), jnp.int32)
        .at[jnp.where(leaving, my_rank, MIG)]
        .set(local_idx, mode="drop")
    )
    send_rows = mixed[send_idx]
    send_tail = jnp.swapaxes(tail_new[:, send_idx], 0, 1)
    got_rows, got_tail = (
        lax.all_gather(send_rows, "req", axis=0, tiled=True),
        lax.all_gather(send_tail, "req", axis=0, tiled=True),
    )
    count = jnp.sum(leaving.astype(jnp.int32))
    vacated = jnp.where(jnp.arange(MIG, dtype=jnp.int32) < count, send_idx, rows)
    source = source_of[first_slot + jnp.minimum(vacated, rows - 1)]
    position = source // rows * MIG + rank_all[source]
    position = jnp.clip(position, 0, got_rows.shape[0] - 1)
    out_hidden = mixed.at[vacated].set(got_rows[position], mode="drop")
    new_tail_kv = tail_new.at[:, vacated].set(jnp.swapaxes(got_tail[position], 0, 1), mode="drop")
    return (out_hidden, new_tail_kv)


def solution(mesh):
    return jax.shard_map(
        body,
        mesh=mesh,
        in_specs=(
            P("req", None),
            P(None, "req", None, "tp"),
            P(None, "req", None, "tp"),
            P("req"),
            P("req"),
            P("req"),
            P(),
            P(None, "tp"),
            P(),
            P(None, "tp"),
            P(None, "tp"),
            P(None, "tp"),
            P("tp", None),
            P(),
            P(),
            P("req", None),
            P("req", None, "tp"),
            P("req", None, "tp"),
            P("req", "tp", None),
            P(),
        ),
        out_specs=(P("req", None), P(None, "req", None, "tp")),
        check_vma=False,
    )
```

profile of v0, /device:TPU:6, one launch (start us, length us, event | category | flops | bytes accessed | tf_op | source)
XLA Modules:
  0.0 309.5 jit_solution(10653071250375701447)
XLA Ops:
  10.9 1.3 iota_compare_fusion.5
  12.2 1.3 subtract_clamp_fusion.1
  15.9 6.9 %fusion.8 = f32[2,256,512]{2,0,1:T(2,128)S(1)} fusion(s32[256,512]{1,0:T(8,128)S(1)} %subtract_clamp_fusion, s32[32]{0:T(128)S(1)} %pad_add_fusion, s32[32]{0:T(128)S(1)} %convert_reduce_fusion, f32[32,2]{0,1:T(2,128)} %param.27), kind=kOutput, calls=%fused_computation.35 | convolution fusion | flops 113246208 | bytes 1573376 | tf_op jit(solution)/shard_map/rjk,kh->hrj/dot_general | solution.py:23
  24.5 1.3 copy.113
  25.8 6.5 %fusion.89 = (bf16[1,256,64,128]{3,2,1,0:T(8,128)(2,1)}, bf16[1,256,64,128]{3,2,1,0:T(8,128)(2,1)}) fusion(bf16[2,256,64,128]{3,2,1,0:T(8,128)(2,1)} %param.22), kind=kLoop, calls=%fused_computation.187 | loop fusion | bytes 16777216 | tf_op jit(solution)/shard_map/slice | solution.py:61
  32.3 7.0 %copy.114 = bf16[1,256,64,128]{1,3,2,0:T(8,128)(2,1)} copy(bf16[1,256,64,128]{3,2,1,0:T(8,128)(2,1)} %get-tuple-element.12) | data formatting | bytes 8388608
  42.9 3.7 %multiply_reduce_fusion.1 = f32[2,256,64]{1,0,2:T(2,128)S(1)} fusion(bf16[2,256,64,64]{1,2,0,3:T(8,128)(2,1)} %bitcast.145, f32[2,256,64]{1,2,0:T(8,128)S(1)} %get-tuple-element.27), kind=kLoop, calls=%fused_computation.13 | loop fusion | flops 6258688 | bytes 4456448 | tf_op jit(solution)/shard_map/rhd,rthd->hrt/dot_general | solution.py:81
  47.6 2.2 fusion.5
  49.9 2.7 fusion.4
  54.7 6.9 %copy.116 = bf16[1,256,64,128]{1,3,2,0:T(8,128)(2,1)} copy(bf16[1,256,64,128]{3,2,1,0:T(8,128)(2,1)} %get-tuple-element.13) | data formatting | bytes 8388608
  61.6 2.0 convolution_convert_fusion.2
  63.6 2.3 copy.115
  65.9 3.2 %multiply_reduce_fusion = f32[256,2,64]{0,2,1:T(8,128)S(1)} fusion(bf16[256,2,64,64]{0,3,1,2:T(8,128)(2,1)} %bitcast.146, f32[256,2,64]{0,1,2:T(2,128)S(1)} %bitcast_convert_fusion), kind=kLoop, calls=%fused_computation.12 | loop fusion | flops 6258688 | bytes 4456448 | tf_op jit(solution)/shard_map/hrt,rthd->rhd/dot_general | solution.py:96
  69.2 5.1 %fusion.19 = bf16[256,2,64]{0,2,1:T(8,128)(2,1)S(1)} fusion(f32[256,2,64]{0,2,1:T(8,128)S(1)} %multiply_reduce_fusion, f32[2,256,8,512]{3,1,2,0:T(8,128)} %copy-done.1, f32[2,256]{1,0:T(2,128)S(1)} %copy-done.18, f32[2,256]{1,0:T(2,128)S(1)} %copy-done.13, f32[2,256,512]{2,1,0:T(8,128)S(1)} %copy.78, pred[256,8,512]{2,0,1:T(8,128)(4,1)S(1)} %broadcast_and_fusion, ...), kind=kOutput, calls=%fused_computation.52 | convolution fusion | flops 281182208 | bytes 11802624 | tf_op jit(solution)/shard_map/hrgj,gjhd->rhd/dot_general | solution.py:95
  74.3 1.3 fusion.93
  77.6 60.5 %all-reduce.3.cloned.1.call-done = f32[256,1024]{1,0:T(8,128)} async-done(((f32[256,1024]{1,0:T(8,128)}), f32[256,1024]{1,0:T(8,128)}) %all-reduce.3.cloned.1.call-update) | async-done | bytes 1048592 | tf_op jit(solution)/shard_map/psum | solution.py:146
  138.1 1.5 fusion.24
  141.6 3.2 %convolution_convert_fusion.1 = bf16[640,1024]{1,0:T(8,128)(2,1)} fusion(bf16[512,1024]{1,0:T(8,128)(2,1)} %reshape.353, s32[512]{0:T(512)S(1)} %multiply_add_fusion), kind=kOutput, calls=%fused_computation.28 | convolution fusion | flops 672071680 | bytes 2361344 | tf_op jit(solution)/shard_map/dot_general | solution.py:167
  144.9 7.0 %all-to-all-start = ((bf16[16,40,1024]{2,1,0:T(8,128)(2,1)}), bf16[16,40,1024]{2,1,0:T(8,128)(2,1)S(1)}, u32[]{:S(2)}, u32[]{:S(2)}) async-start(bf16[16,40,1024]{2,1,0:T(8,128)(2,1)} %bitcast.149), calls=%async_computation | async-start | bytes 2621440 | tf_op jit(solution)/shard_map/all_to_all | solution.py:174
  153.9 1.4 scatter_custom_fusion
  156.0 20.2 %all-to-all-done = bf16[16,40,1024]{2,1,0:T(8,128)(2,1)S(1)} async-done(((bf16[16,40,1024]{2,1,0:T(8,128)(2,1)}), bf16[16,40,1024]{2,1,0:T(8,128)(2,1)S(1)}, u32[]{:S(2)}, u32[]{:S(2)}) %all-to-all-start) | async-done | bytes 1310752 | tf_op jit(solution)/shard_map/all_to_all | solution.py:174
  176.1 2.8 fusion.48
  178.9 4.3 %convolution_convert_fusion = bf16[640,1024]{1,0:T(8,128)(2,1)} fusion(bf16[640,1024]{1,0:T(8,128)(2,1)S(1)} %bitcast.148, f32[640,352]{0,1:T(8,128)} %fusion.48, bf16[1,352,1024]{2,1,0:T(8,128)(2,1)S(1)} %copy-done, bf16[1,1024,352]{1,2,0:T(8,128)(2,1)} %param.37), kind=kOutput, calls=%fused_computation.27 | convolution fusion | flops 925655040 | bytes 4964352 | tf_op jit(solution)/shard_map/dot_general | solution.py:180
  183.3 8.3 %broadcast_select_fusion = bf16[2,256,64,128]{3,2,1,0:T(8,128)(2,1)} fusion(bf16[2,256,64,128]{3,2,1,0:T(8,128)(2,1)} %param.22, pred[256,64]{1,0:T(8,128)(4,1)S(1)} %copy.89, bf16[2,256,128]{2,1,0:T(8,128)(2,1)S(1)} %copy.90), kind=kLoop, calls=%fused_computation.20 | loop fusion | flops 4194304 | bytes 16924672 | tf_op jit(solution)/shard_map/jit(_where)/select_n | solution.py:144
  191.5 4.7 %gather_fusion.3 = bf16[4,2,64,128]{3,2,1,0:T(8,128)(2,1)} fusion(bf16[2,256,64,128]{3,2,1,0:T(8,128)(2,1)} %broadcast_select_fusion, s32[1024]{0:T(1024)S(1)} %pad_clamp_fusion.3), kind=kCustom, calls=%fused_computation.4 | custom fusion | bytes 262160 | tf_op jit(solution)/shard_map/gather | solution.py:210
  196.5 15.5 %scatter_custom_fusion.1 = s32[4096]{0:T(1024)S(1)} fusion(s32[4096]{0:T(1024)S(1)} %add_select_fusion.1, s32[4096]{0:T(1024)S(1)} %iota.80, s32[]{:T(128)} %constant.36.clone.1), kind=kCustom, calls=%fused_computation.136 | custom fusion | bytes 16388 | tf_op jit(solution)/shard_map/scatter | solution.py:200
  212.7 28.9 %all-reduce.5.cloned.1.call-done = bf16[16,40,1024]{2,1,0:T(8,128)(2,1)} async-done(((bf16[16,40,1024]{2,1,0:T(8,128)(2,1)}), bf16[16,40,1024]{2,1,0:T(8,128)(2,1)}) %all-reduce.5.cloned.1.call-update) | async-done | bytes 1310736 | tf_op jit(solution)/shard_map/psum | solution.py:179
  241.6 7.0 %all-to-all-start.1 = ((bf16[16,40,1024]{2,1,0:T(8,128)(2,1)}), bf16[16,40,1024]{2,1,0:T(8,128)(2,1)S(1)}, u32[]{:S(2)}, u32[]{:S(2)}) async-start(bf16[16,40,1024]{2,1,0:T(8,128)(2,1)} %all-reduce.5.cloned.1.call-done), calls=%async_computation.1 | async-start | bytes 2621440 | tf_op jit(solution)/shard_map/all_to_all | solution.py:183
  249.6 23.0 %all-to-all-done.1 = bf16[16,40,1024]{2,1,0:T(8,128)(2,1)S(1)} async-done(((bf16[16,40,1024]{2,1,0:T(8,128)(2,1)}), bf16[16,40,1024]{2,1,0:T(8,128)(2,1)S(1)}, u32[]{:S(2)}, u32[]{:S(2)}) %all-to-all-start.1) | async-done | bytes 1310752 | tf_op jit(solution)/shard_map/all_to_all | solution.py:183
  274.5 22.0 %all-gather.1 = bf16[16,4,1024]{2,1,0:T(4,128)(2,1)S(1)} all-gather(bf16[1,4,1024]{2,1,0:T(4,128)(2,1)S(1)} %bitcast.160), channel_id=2, replica_groups=mesh['req'=16,'tp'=8] {'req'}, dimensions={0}, use_global_device_ids=true | all-gather | bytes 139264 | tf_op jit(solution)/shard_map/all_gather | solution.py:212
  297.7 2.3 gather_fusion.4
  300.0 2.0 scatter_fusion
  (142 shorter events, 24.8 us)
Async XLA Ops:
  8.0 170.9 %copy-start = (bf16[1,352,1024]{2,1,0:T(8,128)(2,1)S(1)}, bf16[1,352,1024]{2,1,0:T(8,128)(2,1)}, u32[]{:S(2)}) copy-start(bf16[1,352,1024]{2,1,0:T(8,128)(2,1)} %param.38) | copy-start | bytes 2162692
  8.0 130.1 %all-reduce.3.cloned.1.call-start = ((), (), s32[]{:S(2)}) async-start(), calls=%async_computation.2 | async-start | bytes 2097152 | tf_op jit(solution)/shard_map/psum | solution.py:146
  14.4 8.4 %copy-start.24 = (s32[32]{0:T(128)}, s32[32]{0:T(128)S(1)}, u32[]{:S(2)}) copy-start(s32[32]{0:T(128)S(1)} %convert_reduce_fusion) | copy-start | bytes 388
  15.9 6.9 %copy-start.29 = (s32[32]{0:T(128)}, s32[32]{0:T(128)S(1)}, u32[]{:S(2)}) copy-start(s32[32]{0:T(128)S(1)} %pad_add_fusion) | copy-start | bytes 388
  15.9 7.1 %copy-start.3 = (bf16[256,1024]{1,0:T(8,128)(2,1)S(1)}, bf16[256,1024]{1,0:T(8,128)(2,1)}, u32[]{:S(2)}) copy-start(bf16[256,1024]{1,0:T(8,128)(2,1)} %param.20) | copy-start | bytes 1572868
  15.9 7.3 %copy-start.2 = (bf16[2,8,512,128]{3,2,1,0:T(8,128)(2,1)S(1)}, bf16[2,8,512,128]{3,2,1,0:T(8,128)(2,1)}, u32[]{:S(2)}) copy-start(bf16[2,8,512,128]{3,2,1,0:T(8,128)(2,1)} %param.21) | copy-start | bytes 6291460
  23.2 16.1 %copy-start.23 = (f32[256]{0:T(256)}, f32[256]{0:T(256)S(1)}, u32[]{:S(2)}) copy-start(f32[256]{0:T(256)S(1)} %add_rsqrt_fusion.1) | copy-start | bytes 3076
  32.3 7.0 %copy-start.26 = (bf16[1024,128]{1,0:T(8,128)(2,1)S(1)}, bf16[1024,128]{1,0:T(8,128)(2,1)}, u32[]{:S(2)}) copy-start(bf16[1024,128]{1,0:T(8,128)(2,1)} %param.29) | copy-start | bytes 786436
  32.3 7.0 %copy-start.28 = (f32[1024]{0:T(1024)S(1)}, f32[1024]{0:T(1024)}, u32[]{:S(2)}) copy-start(f32[1024]{0:T(1024)} %param.28) | copy-start | bytes 12292
  32.3 7.5 %copy-start.27 = (bf16[1024,128]{1,0:T(8,128)(2,1)S(1)}, bf16[1024,128]{1,0:T(8,128)(2,1)}, u32[]{:S(2)}) copy-start(bf16[1024,128]{1,0:T(8,128)(2,1)} %param.30) | copy-start | bytes 786436
  32.3 9.2 %copy-start.21 = (f32[32,2]{0,1:T(2,128)S(1)}, f32[32,2]{0,1:T(2,128)}, u32[]{:S(2)}) copy-start(f32[32,2]{0,1:T(2,128)} %param.27) | copy-start | bytes 772
  39.3 7.3 %copy-start.8 = (s32[256,64]{0,1:T(8,128)S(1)}, s32[256,64]{0,1:T(8,128)}, u32[]{:S(2)}) copy-start(s32[256,64]{0,1:T(8,128)} %subtract_clamp_fusion.1) | copy-start | bytes 196612
  39.3 7.3 %copy-start.16 = (pred[256,64]{0,1:T(8,128)(4,1)S(1)}, pred[256,64]{0,1:T(8,128)(4,1)}, u32[]{:S(2)}) copy-start(pred[256,64]{0,1:T(8,128)(4,1)} %get-tuple-element.21) | copy-start | bytes 49156
  39.3 7.3 %copy-start.22 = (f32[32,2]{0,1:T(2,128)S(1)}, f32[32,2]{0,1:T(2,128)}, u32[]{:S(2)}) copy-start(f32[32,2]{0,1:T(2,128)} %param.27) | copy-start | bytes 772
  39.3 7.3 %copy-start.25 = (s32[32]{0:T(128)S(1)}, s32[32]{0:T(128)}, u32[]{:S(2)}) copy-start(s32[32]{0:T(128)} %copy-done.24) | copy-start | bytes 388
  39.4 7.3 %copy-start.30 = (s32[32]{0:T(128)S(1)}, s32[32]{0:T(128)}, u32[]{:S(2)}) copy-start(s32[32]{0:T(128)} %copy-done.29) | copy-start | bytes 388
  40.8 6.8 %copy-start.4 = (bf16[1,8,512,128]{2,3,1,0:T(8,128)(2,1)S(1)}, bf16[1,8,512,128]{2,3,1,0:T(8,128)(2,1)}, u32[]{:S(2)}) copy-start(bf16[1,8,512,128]{2,3,1,0:T(8,128)(2,1)} %copy.113) | copy-start | bytes 3145732
  49.9 3.4 %copy-start.1 = (f32[2,256,8,512]{3,1,2,0:T(8,128)}, f32[2,256,8,512]{3,1,2,0:T(8,128)S(1)}, u32[]{:S(2)}) copy-start(f32[2,256,8,512]{3,1,2,0:T(8,128)S(1)} %get-tuple-element.26) | copy-start | bytes 25165828
  49.9 4.1 %copy-start.12 = (f32[2,256]{1,0:T(2,128)}, f32[2,256]{1,0:T(2,128)S(1)}, u32[]{:S(2)}) copy-start(f32[2,256]{1,0:T(2,128)S(1)} %maximum_maximum_fusion) | copy-start | bytes 6148
  65.8 3.3 %copy-start.18 = (f32[2,256]{1,0:T(2,128)S(1)}, f32[2,256]{1,0:T(2,128)}, u32[]{:S(2)}) copy-start(f32[2,256]{1,0:T(2,128)} %copy-done.17) | copy-start | bytes 6148
  65.9 3.3 %copy-start.20 = (f32[256,2]{0,1:T(2,128)S(1)}, f32[256,2]{0,1:T(2,128)}, u32[]{:S(2)}) copy-start(f32[256,2]{0,1:T(2,128)} %get-tuple-element.10) | copy-start | bytes 6148
  69.1 5.2 %copy-start.7 = (bf16[128,1024]{1,0:T(8,128)(2,1)S(1)}, bf16[128,1024]{1,0:T(8,128)(2,1)}, u32[]{:S(2)}) copy-start(bf16[128,1024]{1,0:T(8,128)(2,1)} %param.32) | copy-start | bytes 786436
  69.1 6.5 %copy-start.15 = (s32[256,2]{0,1:T(2,128)S(1)}, s32[256,2]{0,1:T(2,128)}, u32[]{:S(2)}) copy-start(s32[256,2]{0,1:T(2,128)} %param.35) | copy-start | bytes 6148
  74.3 65.3 %copy-start.19 = (f32[1024]{0:T(1024)S(1)}, f32[1024]{0:T(1024)}, u32[]{:S(2)}) copy-start(f32[1024]{0:T(1024)} %param.33) | copy-start | bytes 12292
  140.4 11.6 %copy-start.9 = (s32[4096]{0:T(1024)S(1)}, s32[4096]{0:T(1024)}, u32[]{:S(2)}) copy-start(s32[4096]{0:T(1024)} %param.39) | copy-start | bytes 49156
  140.4 12.5 %copy-start.11 = (bf16[256,128]{0,1:T(8,128)(2,1)S(1)}, bf16[256,128]{0,1:T(8,128)(2,1)}, u32[]{:S(2)}) copy-start(bf16[256,128]{0,1:T(8,128)(2,1)} %convolution_convert_fusion.2) | copy-start | bytes 196612
  144.9 31.2 %all-to-all-start = ((bf16[16,40,1024]{2,1,0:T(8,128)(2,1)}), bf16[16,40,1024]{2,1,0:T(8,128)(2,1)S(1)}, u32[]{:S(2)}, u32[]{:S(2)}) async-start(bf16[16,40,1024]{2,1,0:T(8,128)(2,1)} %bitcast.149), calls=%async_computation | async-start | bytes 2621440 | tf_op jit(solution)/shard_map/all_to_all | solution.py:174
  151.9 89.7 %all-reduce.5.cloned.1.call-start = ((), (), s32[]{:S(2)}) async-start(), calls=%async_computation.3 | async-start | bytes 2621440 | tf_op jit(solution)/shard_map/psum | solution.py:179
  183.2 114.4 %all-gather.4.cloned.1.call-start = ((), (), s32[]{:S(2)}) async-start(), calls=%async_computation.4 | async-start | bytes 2228224 | tf_op jit(solution)/shard_map/all_gather | solution.py:213
  191.5 57.8 %copy-start.14 = (bf16[1024,16]{0,1:T(8,128)(2,1)S(1)}, bf16[1024,16]{0,1:T(8,128)(2,1)}, u32[]{:S(2)}) copy-start(bf16[1024,16]{0,1:T(8,128)(2,1)} %param.34) | copy-start | bytes 98308
  241.6 31.1 %all-to-all-start.1 = ((bf16[16,40,1024]{2,1,0:T(8,128)(2,1)}), bf16[16,40,1024]{2,1,0:T(8,128)(2,1)S(1)}, u32[]{:S(2)}, u32[]{:S(2)}) async-start(bf16[16,40,1024]{2,1,0:T(8,128)(2,1)} %all-reduce.5.cloned.1.call-done), calls=%async_computation.1 | async-start | bytes 2621440 | tf_op jit(solution)/shard_map/all_to_all | solution.py:183
  297.6 4.4 %copy-start.6 = (bf16[256,1024]{1,0:T(8,128)(2,1)}, bf16[256,1024]{1,0:T(8,128)(2,1)S(1)}, u32[]{:S(2)}) copy-start(bf16[256,1024]{1,0:T(8,128)(2,1)S(1)} %scatter_custom_fusion.2) | copy-start | bytes 1572868
  (4 other events, 10.3 us)
Sparse Core Ops, SparseCore 0:
  75.7 62.3 all-reduce.2
  183.3 58.1 all-reduce.4
Sparse Core Ops, SparseCore 1:
  196.3 42.1 all-gather.3
where the time goes:
time: 311 us; the launch traced here: 309 us
  waiting for transfers between devices  133 us (43%)
  local copies, waits for them, and re-layouts  59.9 us (19%)
  other arithmetic  33 us (11%)
  matrix products  31.5 us (10%)
  blocking collectives  22 us (7%)
  between operations  16.2 us (5%)
  starting transfers between devices  14.1 us (5%)
    psum x1, waiting for transfers between devices, body(): attn = lax.psum(partial_attn, 'tp')  60.5 us
    psum x1, waiting for transfers between devices, body(): lax.psum(jnp.dot(act, down_mat, preferred_element_type=jnp.float32).astyp...  28.9 us
    all_to_all x1, waiting for transfers between devices, body(): lax.all_to_all(back, 'req', split_axis=0, concat_axis=0, tiled=True)  23 us
    all_gather x1, blocking collectives, body(): lax.all_gather(send_rows, 'req', axis=0, tiled=True)  22 us
    all_to_all x1, waiting for transfers between devices, body(): lax.all_to_all(outgoing, 'req', split_axis=0, concat_axis=0, tiled=True)  20.2 us
    unnamed x68, local copies, waits for them, and re-layouts  18.9 us
    scatter x1, local copies, waits for them, and re-layouts, body(): source_of = jnp.zeros((total_reqs,), jnp.int32).at[new_slot].set(everyone)  15.5 us
    select_n x1, other arithmetic, body(): tail_new = jnp.where(write_row[None, :, :, None], fresh, tail_kv)  8.26 us
  transfers between devices with their start and end apart: 5, of which 4 were waited for; matrix products, arithmetic and copies ran while one was open for 13% of the time, Pallas kernels for 0%

commit v1 on v0

v1 whole, which is shorter than its diff:
```python
import functools
import jax
import jax.numpy as jnp
from jax import lax
from jax.experimental import pallas as pl
from jax.experimental.pallas import tpu as pltpu
from jax.sharding import PartitionSpec as P

F32 = jnp.float32
BF16 = jnp.bfloat16
EPS = 1e-06
NEG = -1e30
RB = 32
TOP = 2
MIG = 4


def col_form(row):
    n = row.shape[1]
    return jnp.transpose(jnp.broadcast_to(row.astype(F32), (128, n)))


def attn_kernel(
    tl_s, st_s, tab_s, plen_s, send_s,
    hid_ref, gain_ref, wq_ref, wk_ref, wv_ref, grp_ref, tlr_ref, ids_ref, pkv_ref, tail_ref, tail_any,
    tail_out, head_ref, send_ref, slot_ref,
    q16, kvn, lhs, kcat, sco, prob, posb, plb, tlb, tbias, opart, mpart, lpart, sems,
):
    step = pl.program_id(0)
    nsteps = pl.num_programs(0)
    rows = hid_ref.shape[0]
    nb = rows // 8
    groups = pkv_ref.shape[1]
    pre = pkv_ref.shape[2]
    nbuck = st_s.shape[0]
    mig = send_ref.shape[0]

    @pl.when(step == 0)
    def _():
        for m in range(mig):
            for kv in range(2):
                pltpu.make_async_copy(
                    tail_any.at[kv, send_s[m]], send_ref.at[m, kv], sems.at[m, kv]
                ).start()
        h = hid_ref[...].astype(F32)
        ms = jnp.mean(h * h, axis=-1, keepdims=True)
        n1 = (h * lax.rsqrt(ms + EPS) * gain_ref[...]).astype(BF16)
        q = jnp.dot(n1, wq_ref[...], preferred_element_type=F32).astype(BF16).astype(F32)
        kvn[0] = jnp.dot(n1, wk_ref[...], preferred_element_type=F32).astype(BF16).astype(F32)
        kvn[1] = jnp.dot(n1, wv_ref[...], preferred_element_type=F32).astype(BF16).astype(F32)
        g = col_form(grp_ref[...])
        tl = col_form(tlr_ref[...])
        pln = jnp.zeros_like(g)
        for i in range(groups):
            pln = jnp.where(g == float(i), plen_s[i].astype(F32), pln)
        posb[...] = pln + tl
        plb[...] = pln
        tlb[...] = tl
        lane = lax.broadcasted_iota(jnp.int32, (nb, 2, 8, 128), 3)
        head = lax.broadcasted_iota(jnp.int32, (nb, 2, 8, 128), 1)
        qh = jnp.broadcast_to((q * 0.125).reshape(nb, 1, 8, 128), (nb, 2, 8, 128))
        qh = jnp.where((lane // 64) == head, qh, 0.0).reshape(2 * rows, 128)
        q16[...] = qh.astype(BF16)
        g2 = jnp.broadcast_to(g.reshape(nb, 1, 8, 128), (nb, 2, 8, 128)).reshape(2 * rows, 128)
        for i in range(groups):
            lhs[:, i * 128 : (i + 1) * 128] = jnp.where(g2 == float(i), qh, 0.0).astype(BF16)
            kcat[:, i * 128 : (i + 1) * 128] = pkv_ref[0, i]
        for c in range(2):
            sco[pl.ds(c * rows, rows), :] = lax.dot_general(
                lhs[pl.ds(c * rows, rows), :], kcat[...], (((1,), (1,)), ((), ())),
                preferred_element_type=F32,
            )

        @pl.loop(0, nb)
        def _(b):
            pos = posb[pl.ds(b * 8, 8), :]
            pb = plb[pl.ds(b * 8, 8), :]
            tb = tlb[pl.ds(b * 8, 8), :]
            ln = lax.broadcasted_iota(jnp.int32, (8, 128), 1)
            lnf = ln.astype(F32)
            nch = pre // 128
            idx = [pos - (lnf + float(c * 128)) for c in range(nch)]
            idx.append(tb - (ln % 64).astype(F32))
            acc = [[jnp.full((8, 128), tab_s[0, hh], F32) for _ in idx] for hh in range(2)]
            for k in range(1, nbuck):
                th = st_s[k].astype(F32)
                t0 = tab_s[k, 0]
                t1 = tab_s[k, 1]
                for c in range(len(idx)):
                    ge = idx[c] >= th
                    acc[0][c] = jnp.where(ge, t0, acc[0][c])
                    acc[1][c] = jnp.where(ge, t1, acc[1][c])
            sub = lax.broadcasted_iota(jnp.int32, (8, 128), 0)
            tvalid = (idx[nch] >= 0.0) & ((ln // 64) == (sub % 2))
            for hh in range(2):
                rs = pl.ds(b * 16 + hh * 8, 8)
                tbias[rs, :] = jnp.where(tvalid, acc[hh][nch], NEG)
                s = [
                    jnp.where(lnf + float(c * 128) < pb, sco[rs, c * 128 : (c + 1) * 128] + acc[hh][c], NEG)
                    for c in range(nch)
                ]
                mx = functools.reduce(jnp.maximum, s)
                mx = jnp.max(mx, axis=1, keepdims=True)
                e = [jnp.exp(x - mx) for x in s]
                tot = jnp.sum(functools.reduce(jnp.add, e), axis=1, keepdims=True)
                mpart[rs, :] = jnp.broadcast_to(mx, (8, 128))
                lpart[rs, :] = jnp.broadcast_to(tot, (8, 128))
                for c in range(nch):
                    sco[rs, c * 128 : (c + 1) * 128] = e[c]

        prob[...] = sco[...].astype(BF16)
        acc = jnp.zeros((2 * rows, 128), F32)
        for i in range(groups):
            o = jnp.dot(prob[...], pkv_ref[1, i], preferred_element_type=F32)
            acc = jnp.where(g2 == float(i), o, acc)
        opart[...] = acc

        ids = ids_ref[...]
        e0 = ids[:, 0:1]
        e1 = ids[:, 1:2]
        ln = lax.broadcasted_iota(jnp.int32, (rows, 128), 1)
        hit0 = ln == e0
        hit1 = ln == e1
        ri = lax.broadcasted_iota(jnp.int32, (rows, rows), 0)
        ci = lax.broadcasted_iota(jnp.int32, (rows, rows), 1)
        lower = (ci < ri).astype(F32).astype(BF16)
        o0 = hit0.astype(F32)
        o1 = hit1.astype(F32)
        cum0 = jnp.dot(lower, o0.astype(BF16), preferred_element_type=F32)
        cum1 = jnp.dot(lower, o1.astype(BF16), preferred_element_type=F32)
        tot0 = jnp.sum(o0, axis=0, keepdims=True)
        p0 = jnp.sum(jnp.where(hit0, cum0, 0.0), axis=1, keepdims=True)
        p1 = jnp.sum(jnp.where(hit1, cum1 + tot0, 0.0), axis=1, keepdims=True)
        cap = float(slot_stride(5 * rows * TOP // (4 * 16)))
        slot_ref[0] = jnp.broadcast_to(e0.astype(F32) * cap + p0, (rows, 128))
        slot_ref[1] = jnp.broadcast_to(e1.astype(F32) * cap + p1, (rows, 128))

    def put_row(ref, lead, r, kv, length):
        base = pl.multiple_of((length // 16) * 16, 16)
        w = ref[(*lead, pl.ds(base, 16), slice(None))].astype(F32)
        sub = lax.broadcasted_iota(jnp.int32, (16, 128), 0)
        row = kvn[kv, pl.ds(r, 1), :]
        ref[(*lead, pl.ds(base, 16), slice(None))] = jnp.where(sub == length - base, row, w).astype(BF16)

    tail_out[...] = tail_ref[...]
    for i in range(RB):
        r = step * RB + i
        length = tl_s[r]
        for kv in range(2):
            put_row(tail_out, (kv, i), r, kv, length)

    sub = lax.broadcasted_iota(jnp.int32, (2, 8, 128), 1).reshape(16, 128)
    pair = sub // 2
    for bb in range(RB // 8):
        b = step * (RB // 8) + bb
        rs = pl.ds(pl.multiple_of(b * 16, 16), 16)
        kb = tail_out[0, bb * 8 : (bb + 1) * 8].reshape(512, 128)
        vb = tail_out[1, bb * 8 : (bb + 1) * 8].reshape(512, 128)
        s4 = lax.dot_general(q16[rs, :], kb, (((1,), (1,)), ((), ())), preferred_element_type=F32)
        s = s4[:, 0:128]
        for c in range(1, 4):
            s = jnp.where(pair == c, s4[:, c * 128 : (c + 1) * 128], s)
        s = s + tbias[rs, :]
        mt = jnp.max(s, axis=1, keepdims=True)
        mp = mpart[rs, :]
        mx = jnp.maximum(mt, mp)
        e = jnp.exp(s - mx)
        ap = jnp.exp(mp - mx)
        tot = jnp.sum(e, axis=1, keepdims=True) + lpart[rs, :] * ap
        p4 = jnp.concatenate([jnp.where(pair == c, e, 0.0) for c in range(4)], axis=1).astype(BF16)
        o = jnp.dot(p4, vb, preferred_element_type=F32) + opart[rs, :] * ap
        o = (o / tot).reshape(2, 8, 128)
        lane8 = lax.broadcasted_iota(jnp.int32, (8, 128), 1)
        head_ref[pl.ds(pl.multiple_of(b * 8, 8), 8), :] = jnp.where(lane8 < 64, o[0], o[1])

    @pl.when(step == nsteps - 1)
    def _():
        for m in range(mig):
            for kv in range(2):
                pltpu.make_async_copy(
                    tail_any.at[kv, send_s[m]], send_ref.at[m, kv], sems.at[m, kv]
                ).wait()
        for m in range(mig):
            r = send_s[m]
            length = tl_s[r]
            for kv in range(2):
                put_row(send_ref, (m, kv), r, kv, length)


def attention_call(hidden_in, gain, wq, wk, wv, group_of, prompt_len, tail_len, starts, table, send_idx, expert_ids, prompt_kv, tail_kv):
    rows = hidden_in.shape[0]
    smem = pl.BlockSpec(memory_space=pltpu.SMEM)
    once = pl.Buffered(1)

    def whole(shape):
        return pl.BlockSpec(shape, lambda s: (0,) * len(shape), pipeline_mode=once)

    def wholeo(shape):
        return pl.BlockSpec(shape, lambda s: (0,) * len(shape))

    _, groups, pre, wd = prompt_kv.shape
    tail_rows = tail_kv.shape[2]
    tail_spec = pl.BlockSpec((2, RB, tail_rows, wd), lambda s: (0, s, 0, 0))
    return pl.pallas_call(
        attn_kernel,
        grid=(rows // RB,),
        out_shape=(
            jax.ShapeDtypeStruct(tail_kv.shape, BF16),
            jax.ShapeDtypeStruct((rows, wd), F32),
            jax.ShapeDtypeStruct((send_idx.shape[0], 2, tail_rows, wd), BF16),
            jax.ShapeDtypeStruct((2, rows, 128), F32),
        ),
        in_specs=[smem] * 5
        + [
            whole(hidden_in.shape), whole((1, hidden_in.shape[1])), whole(wq.shape), whole(wk.shape), whole(wv.shape),
            whole((1, rows)), whole((1, rows)), whole(expert_ids.shape), whole(prompt_kv.shape), tail_spec,
            pl.BlockSpec(memory_space=pl.ANY),
        ],
        out_specs=(
            tail_spec, wholeo((rows, wd)), wholeo((send_idx.shape[0], 2, tail_rows, wd)), wholeo((2, rows, 128)),
        ),
        scratch_shapes=[
            pltpu.VMEM((2 * rows, 128), BF16),
            pltpu.VMEM((2, rows, 128), F32),
            pltpu.VMEM((2 * rows, groups * 128), BF16),
            pltpu.VMEM((pre, groups * 128), BF16),
            pltpu.VMEM((2 * rows, pre), F32),
            pltpu.VMEM((2 * rows, pre), BF16),
            pltpu.VMEM((rows, 128), F32),
            pltpu.VMEM((rows, 128), F32),
            pltpu.VMEM((rows, 128), F32),
            pltpu.VMEM((2 * rows, 128), F32),
            pltpu.VMEM((2 * rows, 128), F32),
            pltpu.VMEM((2 * rows, 128), F32),
            pltpu.VMEM((2 * rows, 128), F32),
            pltpu.SemaphoreType.DMA((send_idx.shape[0], 2)),
        ],
        compiler_params=pltpu.CompilerParams(vmem_limit_bytes=60 << 20, dimension_semantics=("arbitrary",)),
        cost_estimate=pl.CostEstimate(flops=2_000_000_000, bytes_accessed=22_000_000, transcendentals=400_000),
        name="attention_tails",
    )(
        tail_len, starts, table, prompt_len, send_idx,
        hidden_in, gain.reshape(1, -1), wq, wk, wv, group_of.reshape(1, -1), tail_len.reshape(1, -1), expert_ids,
        prompt_kv, tail_kv, tail_kv,
    )


MESH = pl.DeviceIdType.MESH


def moe_kernel(
    src_s, send_s, vac_s,
    hid_ref, head_ref, wout_ref, gain_ref, router_ref, ids_ref, slot_ref, wg_ref, wu_ref, wd_ref, tail_ref,
    out_ref, got_ref,
    t1, t2, t2r, part, psib, psend, precv, stat, statr, dsend, drecv, xall, ypart, ysib, ysend, yrecv, rsend, rrecv, mvs, mvr, mix,
    s_t1, r_t1, s_t2, r_t2, s_psib, r_psib, s_px, r_px, s_st, r_st, s_d, r_d, s_gx, r_gx, s_gs, r_gs,
    s_ysib, r_ysib, s_yx, r_yx, s_r, r_r, s_mv, r_mv, s_ox, r_ox, s_os, r_os,
):
    r = lax.axis_index("req")
    t = lax.axis_index("tp")
    n_req = t1.shape[0]
    n_tp = mix.shape[0]
    n_x = n_tp // 2
    rows = hid_ref.shape[0]
    cap = xall.shape[1] // n_req
    capp = dsend.shape[0] // n_req
    c = lax.rem(t, 2)
    x = t // 2
    sib = x * 2 + 1 - c
    width = hid_ref.shape[1]

    def tp_copy(src, dst, ss, rs, peer):
        return pltpu.make_async_remote_copy(
            src_ref=src, dst_ref=dst, send_sem=ss, recv_sem=rs, device_id=(r, peer), device_id_type=MESH
        )

    def req_copy(src, dst, ss, rs, peer):
        return pltpu.make_async_remote_copy(
            src_ref=src, dst_ref=dst, send_sem=ss, recv_sem=rs, device_id=(peer, t), device_id_type=MESH
        )

    def xpeer(d):
        return lax.rem(x + d, n_x) * 2 + c

    def xfrom(d):
        return lax.rem(x + n_x - d, n_x) * 2 + c

    barrier = pltpu.get_barrier_semaphore()

    @pl.loop(1, n_tp)
    def _(d):
        pl.semaphore_signal(barrier, inc=1, device_id=(r, lax.rem(t + d, n_tp)), device_id_type=MESH)

    @pl.loop(1, n_req)
    def _(d):
        pl.semaphore_signal(barrier, inc=1, device_id=(lax.rem(r + d, n_req), t), device_id_type=MESH)

    head = head_ref[...].astype(BF16)
    for tt in range(n_tp):
        part[tt % 2, tt // 2] = jnp.dot(
            head, wout_ref[:, tt * 128 : (tt + 1) * 128], preferred_element_type=F32
        ).astype(BF16)

    pl.semaphore_wait(barrier, n_tp - 1 + n_req - 1)

    def rs_sib(d, buf, dst, ss, rs):
        xx = lax.rem(x + d, n_x)
        return tp_copy(buf.at[1 - c, xx], dst.at[xx], ss.at[d], rs.at[d], sib)

    def rs_x(d, buf, dst, ss, rs):
        return tp_copy(buf.at[d], dst.at[d], ss.at[d], rs.at[d], xpeer(d))

    def reduce_scatter(buf, bsib, bsend, brecv, ss1, rs1, ss2, rs2):
        for d in (1, 2, 3, 0):
            rs_sib(d, buf, bsib, ss1, rs1).start()
        for d in (1, 2, 3):
            xx = lax.rem(x + d, n_x)
            rs_sib(d, buf, bsib, ss1, rs1).wait_recv()
            bsend[d] = (buf[c, xx].astype(F32) + bsib[xx].astype(F32)).astype(BF16)
            rs_x(d, bsend, brecv, ss2, rs2).start()
        rs_sib(0, buf, bsib, ss1, rs1).wait_recv()
        for d in (1, 2, 3):
            rs_x(d, bsend, brecv, ss2, rs2).wait_recv()

    def rs_total(buf, bsib, brecv, sl):
        tot = buf[c, x, sl, :].astype(F32) + bsib[x, sl, :].astype(F32)
        for d in (1, 2, 3):
            tot = tot + brecv[d, sl, :].astype(F32)
        return tot

    def rs_finish(buf, bsib, bsend, brecv, ss1, rs1, ss2, rs2):
        for d in (0, 1, 2, 3):
            rs_sib(d, buf, bsib, ss1, rs1).wait_send()
        for d in (1, 2, 3):
            rs_x(d, bsend, brecv, ss2, rs2).wait_send()

    def ag_x(d, buf, ss, rs):
        return tp_copy(buf.at[t], buf.at[t], ss.at[d], rs.at[d], xpeer(d))

    def ag_s(d, buf, ss, rs):
        who = xfrom(d)
        return tp_copy(buf.at[who], buf.at[who], ss.at[d], rs.at[d], sib)

    def all_gather(buf, ss1, rs1, ss2, rs2):
        for d in (1, 2, 3):
            ag_x(d, buf, ss1, rs1).start()
        ag_s(0, buf, ss2, rs2).start()
        for d in (1, 3, 2):
            who = xfrom(d)
            tp_copy(buf.at[who], buf.at[who], ss1.at[d], rs1.at[d], xpeer(d)).wait_recv()
            ag_s(d, buf, ss2, rs2).start()
        for d in (0, 1, 3, 2):
            mine = xfrom(d)
            other = lax.rem(x + n_x - d, n_x) * 2 + 1 - c
            tp_copy(buf.at[mine], buf.at[other], ss2.at[d], rs2.at[d], sib).wait_recv()

    def ag_finish(buf, ss1, rs1, ss2, rs2):
        for d in (1, 2, 3):
            ag_x(d, buf, ss1, rs1).wait_send()
        for d in (0, 1, 2, 3):
            ag_s(d, buf, ss2, rs2).wait_send()

    reduce_scatter(part, psib, psend, precv, s_psib, r_psib, s_px, r_px)

    def t1_copy(d):
        j = lax.rem(r + d, n_req)
        return req_copy(tail_ref.at[j], t1.at[r], s_t1.at[d], r_t1.at[d], j)

    @pl.loop(1, n_req)
    def _(d):
        t1_copy(d).start()

    t1[r] = tail_ref[r]

    attn = rs_total(part, psib, precv, slice(None))
    lanes = pl.ds(pl.multiple_of(t * 128, 128), 128)
    resid = (hid_ref[:, lanes].astype(F32) + attn).astype(BF16).astype(F32)
    u = resid * gain_ref[:, lanes]
    lg = jnp.dot(
        u.astype(BF16), router_ref[pl.ds(pl.multiple_of(t * 128, 128), 128), :], preferred_element_type=F32
    )
    ex = lax.broadcasted_iota(jnp.int32, lg.shape, 1)
    diff = jnp.sum(
        jnp.where(ex == ids_ref[:, 0:1], lg, 0.0) - jnp.where(ex == ids_ref[:, 1:2], lg, 0.0), axis=1, keepdims=True
    )
    sq = jnp.sum(resid * resid, axis=1, keepdims=True)
    ln = lax.broadcasted_iota(jnp.int32, (rows, 128), 1)
    packed = jnp.where(ln == 0, sq, jnp.where(ln == 1, diff, 0.0))
    stat[...] = jnp.transpose(packed)[0:8]

    def st_copy(d):
        return tp_copy(stat, statr.at[d], s_st.at[d], r_st.at[d], lax.rem(t + d, n_tp))

    for d in range(1, n_tp):
        st_copy(d).start()
    tot = stat[...]
    for d in range(1, n_tp):
        st_copy(d).wait_recv()
        tot = tot + statr[d]
    tot = jnp.transpose(jnp.concatenate([tot, jnp.zeros((120, rows), F32)], axis=0))
    rs = lax.rsqrt(tot[:, 0:1] * (1.0 / width) + EPS)
    gate = jax.nn.sigmoid(tot[:, 1:2] * rs)
    n2 = (u * rs).astype(BF16)

    s0 = slot_ref[0]
    s1 = slot_ref[1]
    nsl = n_req * cap
    nslp = n_req * capp
    lnf = ln.astype(F32)
    for k in range(nslp // 128):
        pick = (s0 == lnf + float(k * 128)) | (s1 == lnf + float(k * 128))
        dsend[k * 128 : (k + 1) * 128, :] = lax.dot_general(
            pick.astype(F32).astype(BF16), n2, (((0,), (0,)), ((), ())), preferred_element_type=F32
        ).astype(BF16)

    def block(j):
        return pl.ds(pl.multiple_of(j * capp, 16), capp)

    def d_copy(d):
        j = lax.rem(r + d, n_req)
        return req_copy(dsend.at[block(j)], drecv.at[block(r)], s_d.at[d], r_d.at[d], j)

    @pl.loop(1, n_req)
    def _(d):
        d_copy(d).start()

    drecv[block(r), :] = dsend[block(r), :]

    @pl.loop(1, n_req)
    def _(d):
        t1_copy(d).wait_recv()

    @pl.loop(0, n_req)
    def _(j):
        t2[j] = t1[src_s[j]]

    def t2_copy(d):
        j = lax.rem(r + d, n_req)
        return req_copy(t2.at[j], t2r.at[r], s_t2.at[d], r_t2.at[d], j)

    @pl.loop(1, n_req)
    def _(d):
        d_copy(d).wait_recv()

    xall[t] = jnp.concatenate(
        [drecv[j * capp : (j + 1) * capp, :].astype(F32)[0:cap] for j in range(n_req)], axis=0
    ).astype(BF16)
    all_gather(xall, s_gx, r_gx, s_gs, r_gs)

    @pl.loop(1, n_req)
    def _(d):
        t2_copy(d).start()

    t2r[r] = t2[r]

    @pl.loop(0, nsl // 128)
    def _(m):
        sl = pl.ds(pl.multiple_of(m * 128, 128), 128)
        xm = jnp.concatenate([xall[tt, sl, :] for tt in range(n_tp)], axis=1)
        gh = jnp.dot(xm, wg_ref[...], preferred_element_type=F32)
        uh = jnp.dot(xm, wu_ref[...], preferred_element_type=F32)
        act = (jax.nn.gelu(gh, approximate=True) * uh).astype(BF16)
        y = jnp.dot(act, wd_ref[...], preferred_element_type=F32).astype(BF16)
        for tt in range(n_tp):
            ypart[tt % 2, tt // 2, sl, :] = y[:, tt * 128 : (tt + 1) * 128]

    reduce_scatter(ypart, ysib, ysend, yrecv, s_ysib, r_ysib, s_yx, r_yx)
    tot = rs_total(ypart, ysib, yrecv, slice(None))
    pad = jnp.zeros((capp - cap, 128), F32)
    for j in range(n_req):
        rsend[j * capp : (j + 1) * capp, :] = jnp.concatenate([tot[j * cap : (j + 1) * cap], pad], axis=0).astype(BF16)

    def r_copy(d):
        j = lax.rem(r + d, n_req)
        return req_copy(rsend.at[block(j)], rrecv.at[block(r)], s_r.at[d], r_r.at[d], j)

    @pl.loop(1, n_req)
    def _(d):
        r_copy(d).start()

    rrecv[block(r), :] = rsend[block(r), :]

    @pl.loop(1, n_req)
    def _(d):
        r_copy(d).wait_recv()

    p0 = jnp.zeros((rows, 128), F32)
    p1 = jnp.zeros((rows, 128), F32)
    for k in range(nslp // 128):
        got = rrecv[k * 128 : (k + 1) * 128, :]
        p0 = p0 + jnp.dot((s0 == lnf + float(k * 128)).astype(F32).astype(BF16), got, preferred_element_type=F32)
        p1 = p1 + jnp.dot((s1 == lnf + float(k * 128)).astype(F32).astype(BF16), got, preferred_element_type=F32)
    mixed = (resid + gate * p0 + (1.0 - gate) * p1).astype(BF16)

    n_mig = send_s.shape[0]
    kk = lax.broadcasted_iota(jnp.int32, (16, rows), 0)
    rr = lax.broadcasted_iota(jnp.int32, (16, rows), 1)
    pick = jnp.zeros((16, rows), F32)
    for k in range(n_mig):
        pick = jnp.where((kk == k) & (rr == send_s[k]), 1.0, pick)
    mvs[...] = jnp.dot(pick.astype(BF16), mixed, preferred_element_type=F32).astype(BF16)

    def mv_copy(d):
        j = lax.rem(r + d, n_req)
        return req_copy(mvs, mvr.at[r], s_mv.at[d], r_mv.at[d], j)

    @pl.loop(1, n_req)
    def _(d):
        mv_copy(d).start()

    mvr[r] = mvs[...]

    @pl.loop(1, n_req)
    def _(d):
        mv_copy(d).wait_recv()

    came = mvr[src_s[r]].astype(F32)
    ri = lax.broadcasted_iota(jnp.int32, (rows, 128), 0)
    new = mixed.astype(F32)
    for k in range(n_mig):
        new = jnp.where(ri == vac_s[k], came[k : k + 1, :], new)
    mix[t] = new.astype(BF16)
    all_gather(mix, s_ox, r_ox, s_os, r_os)
    for tt in range(n_tp):
        out_ref[:, tt * 128 : (tt + 1) * 128] = mix[tt]

    @pl.loop(1, n_req)
    def _(d):
        t2_copy(d).wait_recv()

    got_ref[...] = t2r[...]

    rs_finish(part, psib, psend, precv, s_psib, r_psib, s_px, r_px)
    rs_finish(ypart, ysib, ysend, yrecv, s_ysib, r_ysib, s_yx, r_yx)
    ag_finish(xall, s_gx, r_gx, s_gs, r_gs)
    ag_finish(mix, s_ox, r_ox, s_os, r_os)
    for d in range(1, n_tp):
        st_copy(d).wait_send()

    @pl.loop(1, n_req)
    def _(d):
        t1_copy(d).wait_send()
        d_copy(d).wait_send()
        t2_copy(d).wait_send()
        r_copy(d).wait_send()
        mv_copy(d).wait_send()


def slot_stride(cap):
    return -(-cap // 16) * 16


def moe_call(n_req, n_tp, src, send_idx, vac, hidden, head, w_out, gain, router, ids, slots, wg, wu, wd, send_tail):
    rows, width = hidden.shape
    cap = 5 * rows * TOP // (4 * n_req)
    nsl = n_req * cap
    nslp = n_req * slot_stride(cap)
    chunk = send_tail.shape[1]
    smem = pl.BlockSpec(memory_space=pltpu.SMEM)
    vmem = pl.BlockSpec(memory_space=pltpu.VMEM)
    dma = pltpu.SemaphoreType.DMA
    n_x = n_tp // 2

    def bf(*shape):
        return pltpu.VMEM(shape, BF16)

    return pl.pallas_call(
        moe_kernel,
        out_shape=(
            jax.ShapeDtypeStruct((rows, width), BF16),
            jax.ShapeDtypeStruct((n_req, chunk, 128), BF16),
        ),
        in_specs=[smem] * 3 + [vmem] * 11,
        out_specs=(vmem, vmem),
        scratch_shapes=[
            bf(n_req, chunk, 128), bf(n_req, chunk, 128), bf(n_req, chunk, 128),
            bf(2, n_x, rows, 128), bf(n_x, rows, 128), bf(n_x, rows, 128), bf(n_x, rows, 128),
            pltpu.VMEM((8, rows), F32), pltpu.VMEM((n_tp, 8, rows), F32),
            bf(nslp, 128), bf(nslp, 128), bf(n_tp, nsl, 128),
            bf(2, n_x, nsl, 128), bf(n_x, nsl, 128), bf(n_x, nsl, 128), bf(n_x, nsl, 128),
            bf(nslp, 128), bf(nslp, 128),
            bf(16, 128), bf(n_req, 16, 128), bf(n_tp, rows, 128),
        ]
        + [dma((n_req,))] * 4
        + [dma((n_x,))] * 4
        + [dma((n_tp,))] * 2
        + [dma((n_req,))] * 2
        + [dma((n_x,))] * 4
        + [dma((n_x,))] * 4
        + [dma((n_req,))] * 4
        + [dma((n_x,))] * 4,
        compiler_params=pltpu.CompilerParams(
            collective_id=0, has_side_effects=True, vmem_limit_bytes=56 << 20
        ),
        name="moe_exchange",
    )(src, send_idx, vac, hidden, head, w_out, gain.reshape(1, -1), router, ids, slots, wg, wu, wd, send_tail)


def place_kernel(vac_s, got_ref, tail_in, tail_out, sems):
    rows = tail_out.shape[1]
    n_mig = got_ref.shape[0]
    for k in range(n_mig):
        for kv in range(2):

            @pl.when(vac_s[k] < rows)
            def _():
                pltpu.make_async_copy(got_ref.at[k, kv], tail_out.at[kv, vac_s[k]], sems.at[k, kv]).start()

    for k in range(n_mig):
        for kv in range(2):

            @pl.when(vac_s[k] < rows)
            def _():
                pltpu.make_async_copy(got_ref.at[k, kv], tail_out.at[kv, vac_s[k]], sems.at[k, kv]).wait()


def place_call(vac, got, tail):
    return pl.pallas_call(
        place_kernel,
        out_shape=jax.ShapeDtypeStruct(tail.shape, tail.dtype),
        in_specs=[
            pl.BlockSpec(memory_space=pltpu.SMEM),
            pl.BlockSpec(memory_space=pltpu.VMEM),
            pl.BlockSpec(memory_space=pl.ANY),
        ],
        out_specs=pl.BlockSpec(memory_space=pl.ANY),
        scratch_shapes=[pltpu.SemaphoreType.DMA((got.shape[0], 2))],
        input_output_aliases={2: 0},
        name="place_tails",
    )(vac, got, tail)


def body(
    hidden_in, prompt_kv, tail_kv, group_of, prompt_len, tail_len, bucket_of, bias_table, attn_gain, w_query, w_key,
    w_value, w_out, ffn_gain, router_weight, expert_ids, w_gate, w_up, w_down, new_slot,
):
    rows = hidden_in.shape[0]
    n_req = lax.axis_size("req")
    n_tp = lax.axis_size("tp")
    me = lax.axis_index("req")
    buckets = bias_table.shape[0]
    starts = jnp.sum((bucket_of[:, None] < jnp.arange(buckets, dtype=jnp.int32)[None, :]).astype(jnp.int32), axis=0)
    local = jnp.arange(rows, dtype=jnp.int32)
    kth = jnp.arange(MIG, dtype=jnp.int32)
    slots2 = new_slot.reshape(n_req, rows)
    moved2 = slots2 != jnp.arange(n_req * rows, dtype=jnp.int32).reshape(n_req, rows)
    replica = jnp.arange(n_req, dtype=jnp.int32)
    goes = jnp.max(jnp.where(moved2, slots2 // rows, -1), axis=1)
    goes = jnp.where(goes < 0, replica, goes)
    src = jnp.sum(jnp.where(goes[None, :] == replica[:, None], replica[None, :], 0), axis=1)
    mine = lax.dynamic_slice_in_dim(new_slot, me * rows, rows, 0)
    moved = mine != me * rows + local
    order = jnp.sum((moved[None, :] & (mine[None, :] < mine[:, None])).astype(jnp.int32), axis=1)
    place = jnp.sum((moved[None, :] & (local[None, :] < local[:, None])).astype(jnp.int32), axis=1)
    is_kth = moved[None, :] & (order[None, :] == kth[:, None])
    send_idx = jnp.sum(jnp.where(is_kth, local[None, :], 0), axis=1)
    at_kth = moved[None, :] & (place[None, :] == kth[:, None])
    vac = jnp.min(jnp.where(at_kth, local[None, :], rows), axis=1)
    tail_new, head, send_tail, slots = attention_call(
        hidden_in, attn_gain, w_query, w_key, w_value, group_of, prompt_len, tail_len, starts, bias_table, send_idx,
        expert_ids, prompt_kv, tail_kv,
    )
    pieces = send_tail.reshape(n_req, -1, send_tail.shape[-1])
    out_hidden, got = moe_call(
        n_req, n_tp, src, send_idx, vac, hidden_in, head, w_out, ffn_gain, router_weight, expert_ids, slots,
        w_gate[0], w_up[0], w_down[0], pieces,
    )
    new_tail = place_call(vac, got.reshape(send_tail.shape), tail_new)
    return (out_hidden, new_tail)


def solution(mesh):
    return jax.shard_map(
        body,
        mesh=mesh,
        in_specs=(
            P("req", None), P(None, "req", None, "tp"), P(None, "req", None, "tp"), P("req"), P("req"), P("req"), P(),
            P(None, "tp"), P(), P(None, "tp"), P(None, "tp"), P(None, "tp"), P("tp", None), P(), P(), P("req", None),
            P("req", None, "tp"), P("req", None, "tp"), P("req", "tp", None), P(),
        ),
        out_specs=(P("req", None), P(None, "req", None, "tp")),
        check_vma=False,
    )
```

time: 311 us -> 117 us (0.38)
  the two profiles are of different devices: /device:TPU:6 before, /device:TPU:1 now
where the time goes in v1:
time: 117 us; the launch traced here: 116 us
  Pallas kernels  101 us (86%)
  local copies, waits for them, and re-layouts  10.5 us (9%)
  other arithmetic  3.87 us (3%)
    pallas_call x1, Pallas kernels, moe_call(): pl.pallas_call(moe_kernel, out_shape=(jax.ShapeDtypeStruct((rows, width),...  71.1 us
    pallas_call x1, Pallas kernels, attention_call(): pl.pallas_call(attn_kernel, grid=(rows // RB,), out_shape=(jax.ShapeDtype...  28 us
    unnamed x8, local copies, waits for them, and re-layouts  9.79 us

profile of v1, /device:TPU:1, one launch (start us, length us, event | category | flops | bytes accessed | tf_op | source)
XLA Modules:
  0.0 115.8 jit_solution(774730908772425896)
XLA Ops:
  0.6 1.4 %convert_reduce_fusion.2.st_s = s32[32]{0:T(128)} fusion(s32[577]{0:T(1024)} %param.26), kind=kLoop, calls=%fused_computation.4 | loop fusion | flops 55360 | bytes 2436 | tf_op jit(solution)/shard_map/reduce_sum | solution.py:642
  2.0 0.8 add_compare_fusion.1
  2.8 0.2 convert_reduce_fusion
  3.0 0.7 select_reduce_fusion.1
  3.7 1.4 %copy.29.tab_s = f32[32,2]{1,0:T(8,128)} copy(f32[32,2]{0,1:T(2,128)} %param.27) | data formatting | bytes 512 | tf_op args[7]
  5.0 0.7 reshape.45
  5.8 0.1 fusion.3
  5.9 0.7 select_reduce_fusion.src_s
  6.6 1.5 %copy.30.ids_ref = s32[256,2]{1,0:T(8,128)} copy(s32[256,2]{0,1:T(2,128)} %param.35) | data formatting | bytes 4096 | tf_op args[15]
  8.1 1.6 %copy.33.router_ref = bf16[1024,16]{1,0:T(8,128)(2,1)} copy(bf16[1024,16]{0,1:T(8,128)(2,1)} %param.34) | data formatting | bytes 65536 | tf_op args[14]
  9.7 2.3 %copy.31 = bf16[1,1024,352]{2,1,0:T(8,128)(2,1)} copy(bf16[1,1024,352]{1,2,0:T(8,128)(2,1)} %param.36) | data formatting | bytes 1441792 | tf_op args[16]
  11.9 2.3 %copy.32 = bf16[1,1024,352]{2,1,0:T(8,128)(2,1)} copy(bf16[1,1024,352]{1,2,0:T(8,128)(2,1)} %param.37) | data formatting | bytes 1441792 | tf_op args[17]
  14.2 28.0 %attention_tails.1 = (bf16[2,256,64,128]{3,2,1,0:T(8,128)(2,1)}, f32[256,128]{1,0:T(8,128)}, bf16[4,2,64,128]{3,2,1,0:T(8,128)(2,1)}, f32[2,256,128]{2,1,0:T(8,128)}) custom-call(s32[256]{0:T(256)} %tl_s.1, s32[32]{0:T(128)} %convert_reduce_fusion.2.st_s, f32[32,2]{1,0:T(8,128)} %copy.29.tab_s, s32[8]{0:T(128)} %plen_s.1, s32[4]{0:T(128)} %get-tuple-element.15.send_s, ...), custom_call_target="tpu_custom_call" | custom-call | flops 2000000000 | bytes 22000000 | tf_op jit(solution)/shard_map/attention_tails/pallas_call | solution.py:204
  42.2 71.1 %moe_exchange.1 = (bf16[256,1024]{1,0:T(8,128)(2,1)}, bf16[16,32,128]{2,1,0:T(8,128)(2,1)}) custom-call(s32[16]{0:T(128)} %select_reduce_fusion.src_s, s32[4]{0:T(128)} %get-tuple-element.15.send_s, s32[4]{0:T(128)} %get-tuple-element.14.vac_s, bf16[256,1024]{1,0:T(8,128)(2,1)} %hid_ref.3, f32[256,128]{1,0:T(8,128)} %get-tuple-element.8.head_ref, ...), custom_call_target="tpu_custom_call" | custom-call | tf_op jit(solution)/shard_map/moe_exchange/pallas_call | solution.py:567
  113.3 0.0 copy-start
  113.3 1.7 %place_tails.1 = bf16[2,256,64,128]{3,2,1,0:T(8,128)(2,1)} custom-call(s32[4]{0:T(128)} %get-tuple-element.14.vac_s, bf16[4,2,64,128]{3,2,1,0:T(8,128)(2,1)} %bitcast.12, bf16[2,256,64,128]{3,2,1,0:T(8,128)(2,1)} %get-tuple-element.13.tail_in), custom_call_target="tpu_custom_call", output_to_operand_aliasing={{}: (2, {})} | custom-call | tf_op jit(solution)/shard_map/place_tails/pallas_call | solution.py:618
  115.0 0.0 copy-done
  115.1 0.8 copy.37
  (1 shorter events, 0.0 us)
Async XLA Ops:
  113.3 1.7 %copy-start = (bf16[256,1024]{1,0:T(8,128)(2,1)S(1)}, bf16[256,1024]{1,0:T(8,128)(2,1)}, u32[]{:S(2)}) copy-start(bf16[256,1024]{1,0:T(8,128)(2,1)} %get-tuple-element.22) | copy-start | bytes 1572868

commit v2 on v1

v2 whole, which is shorter than its diff:
```python
import functools

import jax
import jax.numpy as jnp
from jax import lax
from jax.experimental import pallas as pl
from jax.experimental.pallas import tpu as pltpu
from jax.sharding import PartitionSpec as P

F32 = jnp.float32
BF16 = jnp.bfloat16
EPS = 1e-06
NEG = -1e30
RB = 32
TOP = 2
MIG = 4


def slot_stride(cap):
    return -(-cap // 16) * 16


def col_form(row):
    n = row.shape[1]
    return jnp.transpose(jnp.broadcast_to(row.astype(F32), (128, n)))


def attn_kernel(
    tl_s, tab_s, plen_s, idx_s,
    gain_ref, grp_ref, tlr_ref, ids_ref, bkt_ref, hid_any, wq_any, wk_any, wv_any, pkv_any, tail_any,
    tail_out, head_ref, send_ref, slot_ref,
    hid_v, wcat, pkv_v, buf, q16, kvn, lhs, kcat, sco, prob, posb, plb, tlb, bkt, dtab, tbias, opart, mpart, lpart,
    s_in, s_tin, s_tout,
):
    rows = hid_v.shape[0]
    nb = rows // 8
    groups = pkv_v.shape[1]
    pre = pkv_v.shape[2]
    nbuck = tab_s.shape[1]
    mig = send_ref.shape[0]
    span = bkt_ref.shape[1]
    nblk = rows // RB
    loads = [
        pltpu.make_async_copy(hid_any, hid_v, s_in.at[0]),
        pltpu.make_async_copy(wq_any, wcat.at[:, 0:128], s_in.at[1]),
        pltpu.make_async_copy(wk_any, wcat.at[:, 128:256], s_in.at[2]),
        pltpu.make_async_copy(wv_any, wcat.at[:, 256:384], s_in.at[3]),
        pltpu.make_async_copy(pkv_any.at[0], pkv_v.at[0], s_in.at[4]),
        pltpu.make_async_copy(pkv_any.at[1], pkv_v.at[1], s_in.at[5]),
    ]
    for cp in loads:
        cp.start()

    def t_in(s, kv):
        sl = pl.ds(s * RB, RB)
        return pltpu.make_async_copy(tail_any.at[kv, sl], buf.at[kv, sl], s_tin.at[s, kv])

    def t_out(s, kv):
        sl = pl.ds(s * RB, RB)
        return pltpu.make_async_copy(buf.at[kv, sl], tail_out.at[kv, sl], s_tout.at[s, kv])

    @pl.loop(0, nblk)
    def _(s):
        t_in(s, 0).start()
        t_in(s, 1).start()

    bkt[...] = jnp.zeros_like(bkt)
    bkt[:, 0:span] = jnp.broadcast_to(bkt_ref[...], (8, span))
    nd = bkt.shape[1] // 128
    for c in range(nd):
        bk = bkt[:, c * 128 : (c + 1) * 128]
        d0 = jnp.zeros((8, 128), F32)
        d1 = d0
        for k in range(nbuck):
            hit = bk == k
            d0 = jnp.where(hit, tab_s[0, k], d0)
            d1 = jnp.where(hit, tab_s[1, k], d1)
        dtab[0, :, c * 128 : (c + 1) * 128] = d0
        dtab[1, :, c * 128 : (c + 1) * 128] = d1

    g = col_form(grp_ref[...])
    tl = col_form(tlr_ref[...])
    pln = jnp.zeros_like(g)
    for i in range(groups):
        pln = jnp.where(g == float(i), plen_s[i].astype(F32), pln)
    posb[...] = (pln + tl).astype(jnp.int32)
    plb[...] = pln.astype(jnp.int32)
    tlb[...] = tl.astype(jnp.int32)
    g2 = jnp.broadcast_to(g.reshape(nb, 1, 8, 128), (nb, 2, 8, 128)).reshape(2 * rows, 128)

    e0 = col_form(ids_ref[0:1, :])
    e1 = col_form(ids_ref[1:2, :])
    ln = lax.broadcasted_iota(jnp.int32, (rows, 128), 1).astype(F32)
    hit0 = ln == e0
    hit1 = ln == e1
    ri = lax.broadcasted_iota(jnp.int32, (rows, rows), 0)
    ci = lax.broadcasted_iota(jnp.int32, (rows, rows), 1)
    lower = (ci < ri).astype(F32).astype(BF16)
    o0 = hit0.astype(F32)
    o1 = hit1.astype(F32)
    cum0 = jnp.dot(lower, o0.astype(BF16), preferred_element_type=F32)
    cum1 = jnp.dot(lower, o1.astype(BF16), preferred_element_type=F32)
    tot0 = jnp.sum(o0, axis=0, keepdims=True)
    p0 = jnp.sum(jnp.where(hit0, cum0, 0.0), axis=1, keepdims=True)
    p1 = jnp.sum(jnp.where(hit1, cum1 + tot0, 0.0), axis=1, keepdims=True)
    stride = float(slot_stride(5 * rows * TOP // (4 * 16)))
    slot_ref[0] = e0 * stride + p0
    slot_ref[1] = e1 * stride + p1

    for cp in loads[:4]:
        cp.wait()
    h = hid_v[...].astype(F32)
    ms = jnp.mean(h * h, axis=-1, keepdims=True)
    n1 = (h * lax.rsqrt(ms + EPS) * gain_ref[...]).astype(BF16)
    qkv = jnp.dot(n1, wcat[...], preferred_element_type=F32).astype(BF16).astype(F32)
    q = qkv[:, 0:128]
    kvn[0] = qkv[:, 128:256]
    kvn[1] = qkv[:, 256:384]
    lane = lax.broadcasted_iota(jnp.int32, (nb, 2, 8, 128), 3)
    head = lax.broadcasted_iota(jnp.int32, (nb, 2, 8, 128), 1)
    qh = jnp.broadcast_to((q * 0.125).reshape(nb, 1, 8, 128), (nb, 2, 8, 128))
    qh = jnp.where((lane // 64) == head, qh, 0.0).reshape(2 * rows, 128)
    q16[...] = qh.astype(BF16)
    loads[4].wait()
    for i in range(groups):
        lhs[:, i * 128 : (i + 1) * 128] = jnp.where(g2 == float(i), qh, 0.0).astype(BF16)
        kcat[:, i * 128 : (i + 1) * 128] = pkv_v[0, i]
    sco[...] = lax.dot_general(lhs[...], kcat[...], (((1,), (1,)), ((), ())), preferred_element_type=F32)

    def take(tab, i):
        return jnp.take_along_axis(tab, i, axis=1, mode="promise_in_bounds")

    nch = pre // 128

    def prompt_softmax(b):
        pos = posb[pl.ds(b * 8, 8), :]
        pb = plb[pl.ds(b * 8, 8), :]
        tb = tlb[pl.ds(b * 8, 8), :]
        ln = lax.broadcasted_iota(jnp.int32, (8, 128), 1)
        sub = lax.broadcasted_iota(jnp.int32, (8, 128), 0)
        low = pos & 127
        gi = (low - ln) & 127
        blk = (pos >> 7) - (ln > low).astype(jnp.int32)
        at = [blk == k for k in range(nd)]
        td = tb - (ln & 63)
        tvalid = (td >= 0) & ((ln >> 6) == (sub & 1))
        td = jnp.maximum(td, 0)
        es = [[], []]
        for hh in range(2):
            rs = pl.ds(b * 16 + hh * 8, 8)
            tbias[rs, :] = jnp.where(tvalid, take(dtab[hh, :, 0:128], td), NEG)
            gs = [take(dtab[hh, :, k * 128 : (k + 1) * 128], gi) for k in range(nd)]
            s = []
            for c in range(nch):
                bias = gs[0]
                for k in range(1, nd - c):
                    bias = jnp.where(at[k + c], gs[k], bias)
                s.append(jnp.where(ln + c * 128 < pb, sco[rs, c * 128 : (c + 1) * 128] + bias, NEG))
            mx = jnp.max(functools.reduce(jnp.maximum, s), axis=1, keepdims=True)
            e = [jnp.exp(v - mx) for v in s]
            tot = jnp.sum(functools.reduce(jnp.add, e), axis=1, keepdims=True)
            mpart[rs, :] = jnp.broadcast_to(mx, (8, 128))
            lpart[rs, :] = jnp.broadcast_to(tot, (8, 128))
            es[hh] = e
        for c in range(nch):
            prob[pl.ds(b * 16, 16), c * 128 : (c + 1) * 128] = jnp.concatenate(
                [es[0][c], es[1][c]], axis=0
            ).astype(BF16)

    @pl.loop(0, nb // 2)
    def _(i):
        prompt_softmax(pl.multiple_of(i * 2, 2))
        prompt_softmax(i * 2 + 1)

    loads[5].wait()
    acc = jnp.zeros((2 * rows, 128), F32)
    for i in range(0, groups, 2):
        rhs = jnp.concatenate([pkv_v[1, i], pkv_v[1, i + 1]], axis=1)
        o = jnp.dot(prob[...], rhs, preferred_element_type=F32)
        acc = jnp.where(g2 == float(i), o[:, 0:128], acc)
        acc = jnp.where(g2 == float(i + 1), o[:, 128:256], acc)
    opart[...] = acc

    sub16 = lax.broadcasted_iota(jnp.int32, (16, 128), 0)
    pair = lax.rem(sub16, 8) // 2
    lane8 = lax.broadcasted_iota(jnp.int32, (8, 128), 1)

    @pl.loop(0, nblk)
    def _(s):
        t_in(s, 0).wait()
        t_in(s, 1).wait()
        for i in range(RB):
            r = s * RB + i
            length = tl_s[r]
            base = pl.multiple_of((length >> 4) << 4, 16)
            for kv in range(2):
                w = buf[kv, r, pl.ds(base, 16), :].astype(F32)
                row = kvn[kv, pl.ds(r, 1), :]
                buf[kv, r, pl.ds(base, 16), :] = jnp.where(sub16 == length - base, row, w).astype(BF16)
        t_out(s, 0).start()
        t_out(s, 1).start()
        for bb in range(RB // 8):
            b = s * (RB // 8) + bb
            rs = pl.ds(pl.multiple_of(b * 16, 16), 16)
            own = pl.ds(b * 8, 8)
            kb = buf[0, own].reshape(512, 128)
            vb = buf[1, own].reshape(512, 128)
            s4 = lax.dot_general(q16[rs, :], kb, (((1,), (1,)), ((), ())), preferred_element_type=F32)
            sc = s4[:, 0:128]
            for c in range(1, 4):
                sc = jnp.where(pair == c, s4[:, c * 128 : (c + 1) * 128], sc)
            sc = sc + tbias[rs, :]
            mt = jnp.max(sc, axis=1, keepdims=True)
            mp = mpart[rs, :]
            mx = jnp.maximum(mt, mp)
            e = jnp.exp(sc - mx)
            ap = jnp.exp(mp - mx)
            tot = jnp.sum(e, axis=1, keepdims=True) + lpart[rs, :] * ap
            p4 = jnp.concatenate([jnp.where(pair == c, e, 0.0) for c in range(4)], axis=1).astype(BF16)
            o = jnp.dot(p4, vb, preferred_element_type=F32) + opart[rs, :] * ap
            o = (o / tot).reshape(2, 8, 128)
            head_ref[pl.ds(pl.multiple_of(b * 8, 8), 8), :] = jnp.where(lane8 < 64, o[0], o[1])

    for m in range(mig):
        for kv in range(2):
            send_ref[m, kv] = buf[kv, idx_s[m]]

    @pl.loop(0, nblk)
    def _(s):
        t_out(s, 0).wait()
        t_out(s, 1).wait()


def attention_call(
    hidden_in, gain, wq, wk, wv, group_of, prompt_len, tail_len, bucket_of, table_t, idx, ids_t, prompt_kv, tail_kv
):
    rows, width = hidden_in.shape
    smem = pl.BlockSpec(memory_space=pltpu.SMEM)
    vmem = pl.BlockSpec(memory_space=pltpu.VMEM)
    anym = pl.BlockSpec(memory_space=pl.ANY)
    _, groups, pre, wd = prompt_kv.shape
    tail_rows = tail_kv.shape[2]
    nd = -(-bucket_of.shape[0] // 128)
    nblk = rows // RB
    dma = pltpu.SemaphoreType.DMA
    return pl.pallas_call(
        attn_kernel,
        out_shape=(
            jax.ShapeDtypeStruct(tail_kv.shape, BF16),
            jax.ShapeDtypeStruct((rows, wd), F32),
            jax.ShapeDtypeStruct((MIG, 2, tail_rows, wd), BF16),
            jax.ShapeDtypeStruct((2, rows, 128), F32),
        ),
        in_specs=[smem] * 4 + [vmem] * 5 + [anym] * 6,
        out_specs=(anym, vmem, vmem, vmem),
        scratch_shapes=[
            pltpu.VMEM((rows, width), BF16),
            pltpu.VMEM((width, 3 * wd), BF16),
            pltpu.VMEM(prompt_kv.shape, BF16),
            pltpu.VMEM(tail_kv.shape, BF16),
            pltpu.VMEM((2 * rows, wd), BF16),
            pltpu.VMEM((2, rows, wd), F32),
            pltpu.VMEM((2 * rows, groups * wd), BF16),
            pltpu.VMEM((pre, groups * wd), BF16),
            pltpu.VMEM((2 * rows, pre), F32),
            pltpu.VMEM((2 * rows, pre), BF16),
            pltpu.VMEM((rows, 128), jnp.int32),
            pltpu.VMEM((rows, 128), jnp.int32),
            pltpu.VMEM((rows, 128), jnp.int32),
            pltpu.VMEM((8, nd * 128), jnp.int32),
            pltpu.VMEM((2, 8, nd * 128), F32),
            pltpu.VMEM((2 * rows, 128), F32),
            pltpu.VMEM((2 * rows, 128), F32),
            pltpu.VMEM((2 * rows, 128), F32),
            pltpu.VMEM((2 * rows, 128), F32),
            dma((6,)),
            dma((nblk, 2)),
            dma((nblk, 2)),
        ],
        compiler_params=pltpu.CompilerParams(vmem_limit_bytes=60 << 20),
        name="attention_tails",
    )(
        tail_len, table_t, prompt_len, idx,
        gain.reshape(1, -1), group_of.reshape(1, -1), tail_len.reshape(1, -1), ids_t, bucket_of.reshape(1, -1),
        hidden_in, wq, wk, wv, prompt_kv, tail_kv,
    )


MESH = pl.DeviceIdType.MESH
NCH = 2


def moe_kernel(
    src_s, idx_s,
    head_ref, gain_ref, router_ref, ids_ref, slot_ref, tail_ref, hid_any, wout_any, wg_any, wu_any, wd_any,
    mix, came, got,
    hid_v, wout_v, wg_v, wu_v, wd_v,
    t1, t2, part, psib, psend, precv, stat, statr, dsend, drecv, xall, ypart, ysib, ysend, yrecv, rsend, rrecv, mvs, mvr,
    s_in, s_t1, r_t1, s_t2, r_t2, s_ps, r_ps, s_px, r_px, s_st, r_st, s_d, r_d, s_gx, r_gx, s_gs, r_gs,
    s_ys, r_ys, s_yx, r_yx, s_r, r_r, s_mv, r_mv, s_ox, r_ox, s_os, r_os, s_cm, r_cm,
):
    r = lax.axis_index("req")
    t = lax.axis_index("tp")
    n_req = t1.shape[0]
    n_tp = mix.shape[0]
    n_x = n_tp // 2
    rows = hid_v.shape[0]
    width = wout_v.shape[1]
    crows = xall.shape[2]
    per = n_req // NCH
    cap = crows // per
    nslp = dsend.shape[0]
    capp = nslp // n_req
    c = lax.rem(t, 2)
    x = t // 2
    sib = x * 2 + 1 - c
    lanes = pl.ds(pl.multiple_of(t * 128, 128), 128)

    loads = [
        pltpu.make_async_copy(wout_any, wout_v, s_in.at[0]),
        pltpu.make_async_copy(hid_any.at[:, lanes], hid_v, s_in.at[1]),
        pltpu.make_async_copy(wg_any, wg_v, s_in.at[2]),
        pltpu.make_async_copy(wu_any, wu_v, s_in.at[3]),
        pltpu.make_async_copy(wd_any, wd_v, s_in.at[4]),
    ]
    for cp in loads:
        cp.start()

    def tp_copy(src, dst, ss, rs, peer):
        return pltpu.make_async_remote_copy(
            src_ref=src, dst_ref=dst, send_sem=ss, recv_sem=rs, device_id=(r, peer), device_id_type=MESH
        )

    def req_copy(src, dst, ss, rs, peer):
        return pltpu.make_async_remote_copy(
            src_ref=src, dst_ref=dst, send_sem=ss, recv_sem=rs, device_id=(peer, t), device_id_type=MESH
        )

    def xpeer(d):
        return lax.rem(x + d, n_x) * 2 + c

    def xfrom(d):
        return lax.rem(x + n_x - d, n_x) * 2 + c

    barrier = pltpu.get_barrier_semaphore()

    @pl.loop(1, n_tp)
    def _(d):
        pl.semaphore_signal(barrier, inc=1, device_id=(r, lax.rem(t + d, n_tp)), device_id_type=MESH)

    @pl.loop(1, n_req)
    def _(d):
        pl.semaphore_signal(barrier, inc=1, device_id=(lax.rem(r + d, n_req), t), device_id_type=MESH)

    head = head_ref[...].astype(BF16)
    loads[0].wait()
    for tt in range(n_tp):
        part[tt % 2, tt // 2] = jnp.dot(
            head, wout_v[:, tt * 128 : (tt + 1) * 128], preferred_element_type=F32
        ).astype(BF16)

    pl.semaphore_wait(barrier, n_tp - 1 + n_req - 1)

    def rs_sib(d, buf, dst, ss, rs):
        xx = lax.rem(x + d, n_x)
        return tp_copy(buf.at[1 - c, xx], dst.at[xx], ss.at[d], rs.at[d], sib)

    def rs_x(d, buf, dst, ss, rs):
        return tp_copy(buf.at[d], dst.at[d], ss.at[d], rs.at[d], xpeer(d))

    def rs_start(buf, bsib, ss1, rs1):
        for d in (2, 1, 3, 0):
            rs_sib(d, buf, bsib, ss1, rs1).start()

    def rs_send(buf, bsib, bsend, brecv, ss1, rs1, ss2, rs2):
        for d in (2, 1, 3):
            xx = lax.rem(x + d, n_x)
            rs_sib(d, buf, bsib, ss1, rs1).wait_recv()
            bsend[d] = (buf[c, xx].astype(F32) + bsib[xx].astype(F32)).astype(BF16)
            rs_x(d, bsend, brecv, ss2, rs2).start()

    def rs_total(buf, bsib, bsend, brecv, ss1, rs1, ss2, rs2):
        rs_sib(0, buf, bsib, ss1, rs1).wait_recv()
        tot = buf[c, x].astype(F32) + bsib[x].astype(F32)
        for d in (1, 3, 2):
            rs_x(d, bsend, brecv, ss2, rs2).wait_recv()
            tot = tot + brecv[d].astype(F32)
        return tot

    def rs_finish(buf, bsib, bsend, brecv, ss1, rs1, ss2, rs2):
        for d in (0, 1, 2, 3):
            rs_sib(d, buf, bsib, ss1, rs1).wait_send()
        for d in (1, 2, 3):
            rs_x(d, bsend, brecv, ss2, rs2).wait_send()

    def ag_x(d, buf, ss, rs):
        return tp_copy(buf.at[t], buf.at[t], ss.at[d], rs.at[d], xpeer(d))

    def ag_s(d, buf, ss, rs):
        who = xfrom(d)
        return tp_copy(buf.at[who], buf.at[who], ss.at[d], rs.at[d], sib)

    def ag_start(buf, ss1, rs1, ss2, rs2):
        for d in (2, 1, 3):
            ag_x(d, buf, ss1, rs1).start()
        ag_s(0, buf, ss2, rs2).start()

    def ag_pass(buf, ss1, rs1, ss2, rs2):
        for d in (1, 3, 2):
            who = xfrom(d)
            tp_copy(buf.at[who], buf.at[who], ss1.at[d], rs1.at[d], xpeer(d)).wait_recv()
            ag_s(d, buf, ss2, rs2).start()

    def ag_wait(buf, ss1, rs1, ss2, rs2):
        for d in (0, 1, 3, 2):
            mine = xfrom(d)
            other = lax.rem(x + n_x - d, n_x) * 2 + 1 - c
            tp_copy(buf.at[mine], buf.at[other], ss2.at[d], rs2.at[d], sib).wait_recv()

    def ag_finish(buf, ss1, rs1, ss2, rs2):
        for d in (1, 2, 3):
            ag_x(d, buf, ss1, rs1).wait_send()
        for d in (0, 1, 2, 3):
            ag_s(d, buf, ss2, rs2).wait_send()

    attn_rs = (part, psib, psend, precv, s_ps, r_ps, s_px, r_px)
    rs_start(part, psib, s_ps, r_ps)
    rs_send(*attn_rs)

    def t1_copy(d):
        j = lax.rem(r + d, n_req)
        return req_copy(tail_ref.at[j], t1.at[r], s_t1.at[d], r_t1.at[d], j)

    @pl.loop(1, n_req)
    def _(d):
        t1_copy(d).start()

    t1[r] = tail_ref[r]
    loads[1].wait()
    resid = (hid_v[...].astype(F32) + rs_total(*attn_rs)).astype(BF16)

    s0 = slot_ref[0]
    s1 = slot_ref[1]
    lnf = lax.broadcasted_iota(jnp.int32, (rows, 128), 1).astype(F32)
    for k in range(nslp // 128):
        pick = (s0 == lnf + float(k * 128)) | (s1 == lnf + float(k * 128))
        dsend[k * 128 : (k + 1) * 128, :] = lax.dot_general(
            pick.astype(F32).astype(BF16), resid, (((0,), (0,)), ((), ())), preferred_element_type=F32
        ).astype(BF16)

    def block(j):
        return pl.ds(pl.multiple_of(j * capp, 16), capp)

    def d_copy(d):
        j = lax.rem(r + d, n_req)
        return req_copy(dsend.at[block(j)], drecv.at[block(r)], s_d.at[d], r_d.at[d], j)

    @pl.loop(1, n_req)
    def _(d):
        d_copy(d).start()

    drecv[block(r), :] = dsend[block(r), :]

    rf = resid.astype(F32)
    u = rf * gain_ref[:, lanes]
    lg = lax.dot_general(
        u.astype(BF16), router_ref[:, lanes], (((1,), (1,)), ((), ())), preferred_element_type=F32
    )
    e0 = col_form(ids_ref[0:1, :])
    e1 = col_form(ids_ref[1:2, :])
    n_e = lg.shape[1]
    ex = lnf[:, 0:n_e]
    diff = jnp.sum(
        jnp.where(ex == e0[:, 0:n_e], lg, 0.0) - jnp.where(ex == e1[:, 0:n_e], lg, 0.0), axis=1, keepdims=True
    )
    sq = jnp.sum(rf * rf, axis=1, keepdims=True)
    stat[...] = jnp.transpose(jnp.where(lnf == 0.0, sq, jnp.where(lnf == 1.0, diff, 0.0)))[0:8]

    def st_copy(d):
        return tp_copy(stat, statr.at[d], s_st.at[d], r_st.at[d], lax.rem(t + d, n_tp))

    for d in range(1, n_tp):
        st_copy(d).start()

    @pl.loop(1, n_req)
    def _(d):
        d_copy(d).wait_recv()

    def x_ag(h):
        return (xall.at[h], s_gx.at[h], r_gx.at[h], s_gs.at[h], r_gs.at[h])

    for h in range(NCH):
        xall[h, t] = jnp.concatenate(
            [drecv[j * capp : (j + 1) * capp, :].astype(F32)[0:cap] for j in range(h * per, (h + 1) * per)], axis=0
        ).astype(BF16)
        ag_start(*x_ag(h))

    @pl.loop(1, n_req)
    def _(d):
        t1_copy(d).wait_recv()

    @pl.loop(0, n_req)
    def _(j):
        t2[j] = t1[src_s[j]]

    def t2_copy(d):
        j = lax.rem(r + d, n_req)
        return req_copy(t2.at[j], got.at[r], s_t2.at[d], r_t2.at[d], j)

    @pl.loop(1, n_req)
    def _(d):
        t2_copy(d).start()

    got[r] = t2[r]

    tot = stat[...]
    for d in range(1, n_tp):
        st_copy(d).wait_recv()
        tot = tot + statr[d]
    tot = jnp.transpose(jnp.concatenate([tot, jnp.zeros((120, rows), F32)], axis=0))
    gate = jax.nn.sigmoid(tot[:, 1:2] * lax.rsqrt(tot[:, 0:1] * (1.0 / width) + EPS))

    for cp in loads[2:]:
        cp.wait()

    def ffn(h):
        xm = jnp.concatenate([xall[h, tt] for tt in range(n_tp)], axis=1).astype(F32)
        ms = jnp.mean(xm * xm, axis=-1, keepdims=True)
        nm = (xm * lax.rsqrt(ms + EPS) * gain_ref[...]).astype(BF16)
        gh = lax.dot_general(nm, wg_v[...], (((1,), (1,)), ((), ())), preferred_element_type=F32)
        uh = lax.dot_general(nm, wu_v[...], (((1,), (1,)), ((), ())), preferred_element_type=F32)
        act = (jax.nn.gelu(gh, approximate=True) * uh).astype(BF16)
        y = jnp.dot(act, wd_v[...], preferred_element_type=F32).astype(BF16)
        for tt in range(n_tp):
            ypart[h, tt % 2, tt // 2] = y[:, tt * 128 : (tt + 1) * 128]

    def y_rs(h):
        return (
            ypart.at[h], ysib.at[h], ysend.at[h], yrecv.at[h], s_ys.at[h], r_ys.at[h], s_yx.at[h], r_yx.at[h]
        )

    ag_pass(*x_ag(0))
    for h in range(NCH):
        ag_wait(*x_ag(h))
        ffn(h)
        rs_start(ypart.at[h], ysib.at[h], s_ys.at[h], r_ys.at[h])
        if h + 1 < NCH:
            ag_pass(*x_ag(h + 1))
        rs_send(*y_rs(h))

    def r_copy(d):
        j = lax.rem(r + d, n_req)
        return req_copy(rsend.at[block(j)], rrecv.at[block(r)], s_r.at[d], r_r.at[d], j)

    pad = jnp.zeros((capp - cap, 128), F32)
    for h in range(NCH):
        tot = rs_total(*y_rs(h))
        for i in range(per):
            j = h * per + i
            rsend[j * capp : (j + 1) * capp, :] = jnp.concatenate(
                [tot[i * cap : (i + 1) * cap], pad], axis=0
            ).astype(BF16)

        @pl.loop(h * per, (h + 1) * per)
        def _(j):
            @pl.when(j != r)
            def _():
                r_copy(lax.rem(j + n_req - r, n_req)).start()

    rrecv[block(r), :] = rsend[block(r), :]

    @pl.loop(1, n_req)
    def _(d):
        r_copy(d).wait_recv()

    p0 = jnp.zeros((rows, 128), F32)
    p1 = jnp.zeros((rows, 128), F32)
    for k in range(nslp // 128):
        res = rrecv[k * 128 : (k + 1) * 128, :]
        p0 = p0 + jnp.dot((s0 == lnf + float(k * 128)).astype(F32).astype(BF16), res, preferred_element_type=F32)
        p1 = p1 + jnp.dot((s1 == lnf + float(k * 128)).astype(F32).astype(BF16), res, preferred_element_type=F32)
    mixed = (rf + gate * p0 + (1.0 - gate) * p1).astype(BF16)

    kk = lax.broadcasted_iota(jnp.int32, (16, rows), 0)
    rr = lax.broadcasted_iota(jnp.int32, (16, rows), 1)
    pick = jnp.zeros((16, rows), F32)
    for k in range(MIG):
        pick = jnp.where((kk == k) & (rr == idx_s[k]), 1.0, pick)
    mvs[...] = jnp.dot(pick.astype(BF16), mixed, preferred_element_type=F32).astype(BF16)

    def mv_copy(d):
        j = lax.rem(r + d, n_req)
        return req_copy(mvs, mvr.at[r], s_mv.at[d], r_mv.at[d], j)

    @pl.loop(1, n_req)
    def _(d):
        mv_copy(d).start()

    mvr[r] = mvs[...]
    mix[t] = mixed
    o_ag = (mix, s_ox, r_ox, s_os, r_os)
    ag_start(*o_ag)
    ag_pass(*o_ag)

    @pl.loop(1, n_req)
    def _(d):
        mv_copy(d).wait_recv()

    came[t] = mvr[src_s[r]]

    def cm_copy(d):
        return tp_copy(came.at[t], came.at[t], s_cm.at[d], r_cm.at[d], lax.rem(t + d, n_tp))

    for d in range(1, n_tp):
        cm_copy(d).start()

    ag_wait(*o_ag)
    for d in range(1, n_tp):
        who = lax.rem(t + n_tp - d, n_tp)
        tp_copy(came.at[who], came.at[who], s_cm.at[d], r_cm.at[d], who).wait_recv()

    @pl.loop(1, n_req)
    def _(d):
        t2_copy(d).wait_recv()

    rs_finish(*attn_rs)
    for h in range(NCH):
        rs_finish(*y_rs(h))
        ag_finish(*x_ag(h))
    ag_finish(*o_ag)
    for d in range(1, n_tp):
        st_copy(d).wait_send()
        cm_copy(d).wait_send()

    @pl.loop(1, n_req)
    def _(d):
        t1_copy(d).wait_send()
        d_copy(d).wait_send()
        t2_copy(d).wait_send()
        r_copy(d).wait_send()
        mv_copy(d).wait_send()


def moe_call(n_req, n_tp, src, idx, head, gain, router_t, ids_t, slots, send_tail, hidden, w_out, wg_t, wu_t, wd):
    rows, width = hidden.shape
    cap = 5 * rows * TOP // (4 * n_req)
    nsl = n_req * cap
    crows = nsl // NCH
    nslp = n_req * slot_stride(cap)
    chunk = send_tail.shape[1]
    smem = pl.BlockSpec(memory_space=pltpu.SMEM)
    vmem = pl.BlockSpec(memory_space=pltpu.VMEM)
    anym = pl.BlockSpec(memory_space=pl.ANY)
    dma = pltpu.SemaphoreType.DMA
    n_x = n_tp // 2

    def bf(*shape):
        return pltpu.VMEM(shape, BF16)

    return pl.pallas_call(
        moe_kernel,
        out_shape=(
            jax.ShapeDtypeStruct((n_tp, rows, 128), BF16),
            jax.ShapeDtypeStruct((n_tp, 16, 128), BF16),
            jax.ShapeDtypeStruct((n_req, chunk, 128), BF16),
        ),
        in_specs=[smem] * 2 + [vmem] * 6 + [anym] * 5,
        out_specs=(vmem, vmem, vmem),
        scratch_shapes=[
            bf(rows, 128), bf(*w_out.shape), bf(*wg_t.shape), bf(*wu_t.shape), bf(*wd.shape),
            bf(n_req, chunk, 128), bf(n_req, chunk, 128),
            bf(2, n_x, rows, 128), bf(n_x, rows, 128), bf(n_x, rows, 128), bf(n_x, rows, 128),
            pltpu.VMEM((8, rows), F32), pltpu.VMEM((n_tp, 8, rows), F32),
            bf(nslp, 128), bf(nslp, 128), bf(NCH, n_tp, crows, 128),
            bf(NCH, 2, n_x, crows, 128), bf(NCH, n_x, crows, 128), bf(NCH, n_x, crows, 128), bf(NCH, n_x, crows, 128),
            bf(nslp, 128), bf(nslp, 128),
            bf(16, 128), bf(n_req, 16, 128),
        ]
        + [dma((5,))]
        + [dma((n_req,))] * 4
        + [dma((n_x,))] * 4
        + [dma((n_tp,))] * 2
        + [dma((n_req,))] * 2
        + [dma((NCH, n_x))] * 8
        + [dma((n_req,))] * 4
        + [dma((n_x,))] * 4
        + [dma((n_tp,))] * 2,
        compiler_params=pltpu.CompilerParams(collective_id=0, has_side_effects=True, vmem_limit_bytes=56 << 20),
        name="moe_exchange",
    )(src, idx, head, gain.reshape(1, -1), router_t, ids_t, slots, send_tail, hidden, w_out, wg_t, wu_t, wd)


def place_kernel(idx_s, mix_ref, came_ref, got_ref, tail_in, out_ref, tail_out, sems):
    rows = tail_out.shape[1]

    def put(k, kv):
        return pltpu.make_async_copy(got_ref.at[k, kv], tail_out.at[kv, idx_s[MIG + k]], sems.at[k, kv])

    for k in range(MIG):
        for kv in range(2):

            @pl.when(idx_s[MIG + k] < rows)
            def _():
                put(k, kv).start()

    for tt in range(mix_ref.shape[0]):
        out_ref[:, tt * 128 : (tt + 1) * 128] = mix_ref[tt]
    sub = lax.broadcasted_iota(jnp.int32, (16, 128), 0)
    for k in range(MIG):
        slot = idx_s[MIG + k]

        @pl.when(slot < rows)
        def _():
            base = pl.multiple_of((slot >> 4) << 4, 16)
            for tt in range(mix_ref.shape[0]):
                cols = slice(tt * 128, (tt + 1) * 128)
                row = came_ref[tt].astype(F32)[k : k + 1, :]
                w = out_ref[pl.ds(base, 16), cols].astype(F32)
                out_ref[pl.ds(base, 16), cols] = jnp.where(sub == slot - base, row, w).astype(BF16)

    for k in range(MIG):
        for kv in range(2):

            @pl.when(idx_s[MIG + k] < rows)
            def _():
                put(k, kv).wait()


def place_call(idx, mix, came, got, tail):
    n_tp, rows, wd = mix.shape
    vmem = pl.BlockSpec(memory_space=pltpu.VMEM)
    return pl.pallas_call(
        place_kernel,
        out_shape=(
            jax.ShapeDtypeStruct((rows, n_tp * wd), BF16),
            jax.ShapeDtypeStruct(tail.shape, tail.dtype),
        ),
        in_specs=[pl.BlockSpec(memory_space=pltpu.SMEM), vmem, vmem, vmem, pl.BlockSpec(memory_space=pl.ANY)],
        out_specs=(vmem, pl.BlockSpec(memory_space=pl.ANY)),
        scratch_shapes=[pltpu.SemaphoreType.DMA((MIG, 2))],
        input_output_aliases={4: 1},
        name="place_rows",
    )(idx, mix, came, got, tail)


def body(
    hidden_in, prompt_kv, tail_kv, group_of, prompt_len, tail_len, bucket_of, bias_table, attn_gain, w_query, w_key,
    w_value, w_out, ffn_gain, router_weight, expert_ids, w_gate, w_up, w_down, new_slot,
):
    rows = hidden_in.shape[0]
    n_req = lax.axis_size("req")
    n_tp = lax.axis_size("tp")
    me = lax.axis_index("req")
    local = jnp.arange(rows, dtype=jnp.int32)
    kth = jnp.arange(MIG, dtype=jnp.int32)
    tiles = new_slot.reshape(n_req * rows // 128, 128)
    moved_t = tiles != jnp.arange(n_req * rows, dtype=jnp.int32).reshape(tiles.shape)
    goes = jnp.max(jnp.where(moved_t, tiles // rows, -1), axis=1).reshape(n_req, rows // 128)
    goes = jnp.max(goes, axis=1)
    replica = jnp.arange(n_req, dtype=jnp.int32)
    goes = jnp.where(goes < 0, replica, goes)
    src = jnp.sum(jnp.where(goes[None, :] == replica[:, None], replica[None, :], 0), axis=1)
    mine = lax.dynamic_slice_in_dim(new_slot, me * rows, rows, 0)
    moved = mine != me * rows + local
    key = jnp.concatenate([mine, local])
    both = jnp.concatenate([moved, moved])
    part = jnp.concatenate([jnp.zeros_like(local), jnp.ones_like(local)])
    rank = jnp.sum(
        (both[None, :] & (part[None, :] == part[:, None]) & (key[None, :] < key[:, None])).astype(jnp.int32), axis=1
    )
    want = jnp.arange(2 * MIG, dtype=jnp.int32)
    hit = both[None, :] & (rank + part * MIG == want[:, None])
    idx = jnp.min(jnp.where(hit, jnp.concatenate([local, local])[None, :], rows), axis=1)
    idx = jnp.where(want < MIG, jnp.minimum(idx, rows - 1), idx)
    ids_t = expert_ids.T
    tail_new, head, send_tail, slots = attention_call(
        hidden_in, attn_gain, w_query, w_key, w_value, group_of, prompt_len, tail_len, bucket_of, bias_table.T, idx,
        ids_t, prompt_kv, tail_kv,
    )
    pieces = send_tail.reshape(n_req, -1, send_tail.shape[-1])
    mix, came, got = moe_call(
        n_req, n_tp, src, idx, head, ffn_gain, router_weight.T, ids_t, slots, pieces, hidden_in, w_out,
        w_gate[0].T, w_up[0].T, w_down[0],
    )
    return place_call(idx, mix, came, got.reshape(send_tail.shape), tail_new)


def solution(mesh):
    return jax.shard_map(
        body,
        mesh=mesh,
        in_specs=(
            P("req", None), P(None, "req", None, "tp"), P(None, "req", None, "tp"), P("req"), P("req"), P("req"), P(),
            P(None, "tp"), P(), P(None, "tp"), P(None, "tp"), P(None, "tp"), P("tp", None), P(), P(), P("req", None),
            P("req", None, "tp"), P("req", None, "tp"), P("req", "tp", None), P(),
        ),
        out_specs=(P("req", None), P(None, "req", None, "tp")),
        check_vma=False,
    )
```

time: 117 us -> 88.5 us (0.76)
  Pallas kernels: 101 us -> 81.1 us
  local copies, waits for them, and re-layouts: 10.5 us -> 1.36 us
    pallas_call x3, Pallas kernels: 101 us -> 81.1 us  [the longest x1 58.1 us: moe_call(): pl.pallas_call(moe_kernel, out_shape=(jax.ShapeDtypeStruct((n_tp, rows, 1...]
    unnamed x8 -> x0, local copies, waits for them, and re-layouts: 9.79 us -> none
where the time goes in v2:
time: 88.5 us; the launch traced here: 88.2 us
  Pallas kernels  81.1 us (92%)
  other arithmetic  5 us (6%)
  local copies, waits for them, and re-layouts  1.36 us (2%)
    pallas_call x1, Pallas kernels, moe_call(): pl.pallas_call(moe_kernel, out_shape=(jax.ShapeDtypeStruct((n_tp, rows, 1...  58.1 us
    pallas_call x1, Pallas kernels, attention_call(): pl.pallas_call(attn_kernel, out_shape=(jax.ShapeDtypeStruct(tail_kv.shape...  20.4 us
    pallas_call x1, Pallas kernels, place_call(): pl.pallas_call(place_kernel, out_shape=(jax.ShapeDtypeStruct((rows, n_tp...  2.61 us

profile of v2, /device:TPU:1, one launch (start us, length us, event | category | flops | bytes accessed | tf_op | source)
XLA Modules:
  0.0 88.2 jit_solution(13676148760888230674)
XLA Ops:
  0.6 0.8 fusion.2
  1.5 0.8 add_compare_fusion
  2.3 1.2 %convert_reduce_fusion = s32[512]{0:T(512)S(1)} fusion(s32[512]{0:T(512)S(1)} %get-tuple-element.18, s32[512]{0:T(512)} %constant.39.clone.1, pred[512]{0:T(512)(128)(4,1)S(1)} %pad_add_fusion.2), kind=kLoop, calls=%fused_computation | loop fusion | flops 1572352 | bytes 6656 | tf_op jit(solution)/shard_map/reduce_sum | solution.py:768
  3.5 0.7 add.21
  4.2 0.1 select_reduce_fusion
  4.3 0.6 compare_select_fusion.1.idx_s
  4.9 1.3 %reshape.60.bkt_ref = s32[1,577]{1,0:T(1,128)} reshape(s32[577]{0:T(1024)} %param.26) | data formatting | bytes 4616 | tf_op jit(solution)/shard_map/reshape | solution.py:284
  6.1 0.1 reshape.56
  6.2 0.1 reduce_max.19
  6.4 0.7 select_reduce_fusion.1.src_s
  7.0 20.4 %attention_tails.1 = (bf16[2,256,64,128]{3,2,1,0:T(8,128)(2,1)}, f32[256,128]{1,0:T(8,128)}, bf16[4,2,64,128]{3,2,1,0:T(8,128)(2,1)}, f32[2,256,128]{2,1,0:T(8,128)}) custom-call(s32[256]{0:T(256)} %tl_s.1, f32[2,32]{1,0:T(2,128)} %bitcast.46, s32[8]{0:T(128)} %plen_s.1, s32[8]{0:T(128)} %compare_select_fusion.1.idx_s, f32[1,1024]{1,0:T(1,128)} %bitcast.43, ...), custom_call_target="tpu_custom_call" | custom-call | tf_op jit(solution)/shard_map/attention_tails/pallas_call | solution.py:246
  27.5 58.1 %moe_exchange.1 = (bf16[8,256,128]{2,1,0:T(8,128)(2,1)}, bf16[8,16,128]{2,1,0:T(8,128)(2,1)}, bf16[16,32,128]{2,1,0:T(8,128)(2,1)}) custom-call(s32[16]{0:T(128)} %select_reduce_fusion.1.src_s, s32[8]{0:T(128)} %compare_select_fusion.1.idx_s, f32[256,128]{1,0:T(8,128)} %get-tuple-element.9.head_ref, f32[1,1024]{1,0:T(1,128)} %bitcast.44, ...), custom_call_target="tpu_custom_call" | custom-call | tf_op jit(solution)/shard_map/moe_exchange/pallas_call | solution.py:660
  85.6 2.6 %place_rows.1 = (bf16[256,1024]{1,0:T(8,128)(2,1)}, bf16[2,256,64,128]{3,2,1,0:T(8,128)(2,1)}) custom-call(s32[8]{0:T(128)} %compare_select_fusion.1.idx_s, bf16[8,256,128]{2,1,0:T(8,128)(2,1)} %get-tuple-element.12.mix_ref, bf16[8,16,128]{2,1,0:T(8,128)(2,1)} %get-tuple-element.13.came_ref, ...), custom_call_target="tpu_custom_call", output_to_operand_aliasing={{1}: (4, {})} | custom-call | tf_op jit(solution)/shard_map/place_rows/pallas_call | solution.py:732
  (4 shorter events, 0.0 us)

commit v3 on v2

--- a/solution.py
+++ b/solution.py
@@ -25,12 +25,51 @@
     return jnp.transpose(jnp.broadcast_to(row.astype(F32), (128, n)))
 
 
+def migration_tables(ns_ref, meta_ref, rows):
+    me = lax.axis_index("req")
+    per = rows // 128
+    tiles = ns_ref[...].astype(F32)
+    shape = tiles.shape
+    lane = lax.broadcasted_iota(jnp.int32, shape, 1).astype(F32)
+    sub = lax.broadcasted_iota(jnp.int32, shape, 0)
+    moved = tiles != sub.astype(F32) * 128.0 + lane
+    where_to = jnp.floor(tiles * (1.0 / rows))
+    goes = jnp.max(jnp.where(moved, where_to, -1.0), axis=1, keepdims=True)
+    src = jnp.max(jnp.where(goes == lane, (sub // per).astype(F32), -1.0), axis=0, keepdims=True)
+    src = jnp.where(src < 0.0, lane[0:1], src)
+
+    mine = ns_ref[pl.ds(me * per, per), :].astype(F32)
+    row = jnp.concatenate([mine[i : i + 1] for i in range(per)], axis=1)
+    col = col_form(row)
+    base = (me * rows).astype(F32)
+    rid = lax.broadcasted_iota(jnp.int32, (rows, 128), 0).astype(F32)
+    rlane = lax.broadcasted_iota(jnp.int32, (rows, 128), 1).astype(F32)
+    moved_col = col != rid + base
+    order = jnp.zeros((rows, 128), F32)
+    place = jnp.zeros((rows, 128), F32)
+    for i in range(per):
+        part = row[:, i * 128 : (i + 1) * 128]
+        other = rlane + float(i * 128)
+        moved_row = part != other[0:1] + base
+        order = order + jnp.where(moved_row & (part < col), 1.0, 0.0)
+        place = place + jnp.where(moved_row & (other < rid), 1.0, 0.0)
+    order = jnp.sum(order, axis=1, keepdims=True)
+    place = jnp.sum(place, axis=1, keepdims=True)
+    out = float(rows)
+    send = jnp.min(jnp.where(moved_col & (order == rlane), rid, out), axis=0, keepdims=True)
+    send = jnp.minimum(send, out - 1.0)
+    vac = jnp.min(jnp.where(moved_col & (place + float(MIG) == rlane), rid, out), axis=0, keepdims=True)
+    idx = jnp.where(rlane[0:1] < float(MIG), send, vac)
+    s8 = lax.broadcasted_iota(jnp.int32, (8, 128), 0)
+    meta_ref[...] = jnp.where(s8 == 0, idx, jnp.where(s8 == 1, src, 0.0)).astype(jnp.int32)
+
+
 def attn_kernel(
-    tl_s, tab_s, plen_s, idx_s,
-    gain_ref, grp_ref, tlr_ref, ids_ref, bkt_ref, hid_any, wq_any, wk_any, wv_any, pkv_any, tail_any,
-    tail_out, head_ref, send_ref, slot_ref,
-    hid_v, wcat, pkv_v, buf, q16, kvn, lhs, kcat, sco, prob, posb, plb, tlb, bkt, dtab, tbias, opart, mpart, lpart,
-    s_in, s_tin, s_tout,
+    tl_s, tab_s, plen_s, bkt_s,
+    gain_ref, grp_ref, tlr_ref, ids_ref, ns_ref, hid_any, wq_any, wk_any, wv_any, pkv_any, tail_any,
+    tail_out, head_ref, send_ref, slot_ref, meta_ref,
+    hid_v, wcat, pkv_v, buf, q16, kvn, lhs, kcat, sco, prob, posb, plb, tlb, dtab, tbias, opart, mpart, lpart,
+    first_s, meta_s, s_in, s_tin, s_tout, s_meta,
 ):
     rows = hid_v.shape[0]
     nb = rows // 8
@@ -38,7 +77,7 @@
     pre = pkv_v.shape[2]
     nbuck = tab_s.shape[1]
     mig = send_ref.shape[0]
-    span = bkt_ref.shape[1]
+    span = bkt_s.shape[0]
     nblk = rows // RB
     loads = [
         pltpu.make_async_copy(hid_any, hid_v, s_in.at[0]),
@@ -64,19 +103,30 @@
         t_in(s, 0).start()
         t_in(s, 1).start()
 
-    bkt[...] = jnp.zeros_like(bkt)
-    bkt[:, 0:span] = jnp.broadcast_to(bkt_ref[...], (8, span))
-    nd = bkt.shape[1] // 128
+    for k in range(nbuck):
+        first_s[k] = span
+
+    @pl.loop(0, span, unroll=8)
+    def _(i):
+        d = span - 1 - i
+        first_s[bkt_s[d]] = d
+
+    nd = dtab.shape[2] // 128
+    dist = [lax.broadcasted_iota(jnp.int32, (8, 128), 1) + c * 128 for c in range(nd)]
+    d0 = [jnp.full((8, 128), tab_s[0, 0], F32) for _ in range(nd)]
+    d1 = [jnp.full((8, 128), tab_s[1, 0], F32) for _ in range(nd)]
+    for k in range(1, nbuck):
+        for c in range(nd):
+            ge = dist[c] >= first_s[k]
+            d0[c] = jnp.where(ge, tab_s[0, k], d0[c])
+            d1[c] = jnp.where(ge, tab_s[1, k], d1[c])
     for c in range(nd):
-        bk = bkt[:, c * 128 : (c + 1) * 128]
-        d0 = jnp.zeros((8, 128), F32)
-        d1 = d0
-        for k in range(nbuck):
-            hit = bk == k
-            d0 = jnp.where(hit, tab_s[0, k], d0)
-            d1 = jnp.where(hit, tab_s[1, k], d1)
-        dtab[0, :, c * 128 : (c + 1) * 128] = d0
-        dtab[1, :, c * 128 : (c + 1) * 128] = d1
+        dtab[0, :, c * 128 : (c + 1) * 128] = d0[c]
+        dtab[1, :, c * 128 : (c + 1) * 128] = d1[c]
+
+    migration_tables(ns_ref, meta_ref, rows)
+    meta_copy = pltpu.make_async_copy(meta_ref, meta_s, s_meta)
+    meta_copy.start()
 
     g = col_form(grp_ref[...])
     tl = col_form(tlr_ref[...])
@@ -221,9 +271,10 @@
             o = (o / tot).reshape(2, 8, 128)
             head_ref[pl.ds(pl.multiple_of(b * 8, 8), 8), :] = jnp.where(lane8 < 64, o[0], o[1])
 
+    meta_copy.wait()
     for m in range(mig):
         for kv in range(2):
-            send_ref[m, kv] = buf[kv, idx_s[m]]
+            send_ref[m, kv] = buf[kv, meta_s[0, m]]
 
     @pl.loop(0, nblk)
     def _(s):
@@ -232,7 +283,7 @@
 
 
 def attention_call(
-    hidden_in, gain, wq, wk, wv, group_of, prompt_len, tail_len, bucket_of, table_t, idx, ids_t, prompt_kv, tail_kv
+    hidden_in, gain, wq, wk, wv, group_of, prompt_len, tail_len, bucket_of, table_t, new_slot, ids_t, prompt_kv, tail_kv
 ):
     rows, width = hidden_in.shape
     smem = pl.BlockSpec(memory_space=pltpu.SMEM)
@@ -250,9 +301,10 @@
             jax.ShapeDtypeStruct((rows, wd), F32),
             jax.ShapeDtypeStruct((MIG, 2, tail_rows, wd), BF16),
             jax.ShapeDtypeStruct((2, rows, 128), F32),
+            jax.ShapeDtypeStruct((8, 128), jnp.int32),
         ),
         in_specs=[smem] * 4 + [vmem] * 5 + [anym] * 6,
-        out_specs=(anym, vmem, vmem, vmem),
+        out_specs=(anym, vmem, vmem, vmem, vmem),
         scratch_shapes=[
             pltpu.VMEM((rows, width), BF16),
             pltpu.VMEM((width, 3 * wd), BF16),
@@ -267,21 +319,23 @@
             pltpu.VMEM((rows, 128), jnp.int32),
             pltpu.VMEM((rows, 128), jnp.int32),
             pltpu.VMEM((rows, 128), jnp.int32),
-            pltpu.VMEM((8, nd * 128), jnp.int32),
             pltpu.VMEM((2, 8, nd * 128), F32),
             pltpu.VMEM((2 * rows, 128), F32),
             pltpu.VMEM((2 * rows, 128), F32),
             pltpu.VMEM((2 * rows, 128), F32),
             pltpu.VMEM((2 * rows, 128), F32),
+            pltpu.SMEM((table_t.shape[1],), jnp.int32),
+            pltpu.SMEM((8, 128), jnp.int32),
             dma((6,)),
             dma((nblk, 2)),
             dma((nblk, 2)),
+            dma,
         ],
         compiler_params=pltpu.CompilerParams(vmem_limit_bytes=60 << 20),
         name="attention_tails",
     )(
-        tail_len, table_t, prompt_len, idx,
-        gain.reshape(1, -1), group_of.reshape(1, -1), tail_len.reshape(1, -1), ids_t, bucket_of.reshape(1, -1),
+        tail_len, table_t, prompt_len, bucket_of,
+        gain.reshape(1, -1), group_of.reshape(1, -1), tail_len.reshape(1, -1), ids_t, new_slot.reshape(-1, 128),
         hidden_in, wq, wk, wv, prompt_kv, tail_kv,
     )
 
@@ -291,7 +345,7 @@
 
 
 def moe_kernel(
-    src_s, idx_s,
+    meta_s,
     head_ref, gain_ref, router_ref, ids_ref, slot_ref, tail_ref, hid_any, wout_any, wg_any, wu_any, wd_any,
     mix, came, got,
     hid_v, wout_v, wg_v, wu_v, wd_v,
@@ -431,11 +485,6 @@
         j = lax.rem(r + d, n_req)
         return req_copy(tail_ref.at[j], t1.at[r], s_t1.at[d], r_t1.at[d], j)
 
-    @pl.loop(1, n_req)
-    def _(d):
-        t1_copy(d).start()
-
-    t1[r] = tail_ref[r]
     loads[1].wait()
     resid = (hid_v[...].astype(F32) + rs_total(*attn_rs)).astype(BF16)
 
@@ -460,6 +509,12 @@
         d_copy(d).start()
 
     drecv[block(r), :] = dsend[block(r), :]
+
+    @pl.loop(1, n_req)
+    def _(d):
+        t1_copy(d).start()
+
+    t1[r] = tail_ref[r]
 
     rf = resid.astype(F32)
     u = rf * gain_ref[:, lanes]
@@ -501,7 +556,7 @@
 
     @pl.loop(0, n_req)
     def _(j):
-        t2[j] = t1[src_s[j]]
+        t2[j] = t1[meta_s[1, j]]
 
     def t2_copy(d):
         j = lax.rem(r + d, n_req)
@@ -585,7 +640,7 @@
     rr = lax.broadcasted_iota(jnp.int32, (16, rows), 1)
     pick = jnp.zeros((16, rows), F32)
     for k in range(MIG):
-        pick = jnp.where((kk == k) & (rr == idx_s[k]), 1.0, pick)
+        pick = jnp.where((kk == k) & (rr == meta_s[0, k]), 1.0, pick)
     mvs[...] = jnp.dot(pick.astype(BF16), mixed, preferred_element_type=F32).astype(BF16)
 
     def mv_copy(d):
@@ -606,7 +661,7 @@
     def _(d):
         mv_copy(d).wait_recv()
 
-    came[t] = mvr[src_s[r]]
+    came[t] = mvr[meta_s[1, r]]
 
     def cm_copy(d):
         return tp_copy(came.at[t], came.at[t], s_cm.at[d], r_cm.at[d], lax.rem(t + d, n_tp))
@@ -641,7 +696,7 @@
         mv_copy(d).wait_send()
 
 
-def moe_call(n_req, n_tp, src, idx, head, gain, router_t, ids_t, slots, send_tail, hidden, w_out, wg_t, wu_t, wd):
+def moe_call(n_req, n_tp, meta, head, gain, router_t, ids_t, slots, send_tail, hidden, w_out, wg_t, wu_t, wd):
     rows, width = hidden.shape
     cap = 5 * rows * TOP // (4 * n_req)
     nsl = n_req * cap
@@ -664,7 +719,7 @@
             jax.ShapeDtypeStruct((n_tp, 16, 128), BF16),
             jax.ShapeDtypeStruct((n_req, chunk, 128), BF16),
         ),
-        in_specs=[smem] * 2 + [vmem] * 6 + [anym] * 5,
+        in_specs=[smem] + [vmem] * 6 + [anym] * 5,
         out_specs=(vmem, vmem, vmem),
         scratch_shapes=[
             bf(rows, 128), bf(*w_out.shape), bf(*wg_t.shape), bf(*wu_t.shape), bf(*wd.shape),
@@ -687,19 +742,19 @@
         + [dma((n_tp,))] * 2,
         compiler_params=pltpu.CompilerParams(collective_id=0, has_side_effects=True, vmem_limit_bytes=56 << 20),
         name="moe_exchange",
-    )(src, idx, head, gain.reshape(1, -1), router_t, ids_t, slots, send_tail, hidden, w_out, wg_t, wu_t, wd)
-
-
-def place_kernel(idx_s, mix_ref, came_ref, got_ref, tail_in, out_ref, tail_out, sems):
+    )(meta, head, gain.reshape(1, -1), router_t, ids_t, slots, send_tail, hidden, w_out, wg_t, wu_t, wd)
+
+
+def place_kernel(meta_s, mix_ref, came_ref, got_ref, tail_in, out_ref, tail_out, sems):
     rows = tail_out.shape[1]
 
     def put(k, kv):
-        return pltpu.make_async_copy(got_ref.at[k, kv], tail_out.at[kv, idx_s[MIG + k]], sems.at[k, kv])
+        return pltpu.make_async_copy(got_ref.at[k, kv], tail_out.at[kv, meta_s[0, MIG + k]], sems.at[k, kv])
 
     for k in range(MIG):
         for kv in range(2):
 
-            @pl.when(idx_s[MIG + k] < rows)
+            @pl.when(meta_s[0, MIG + k] < rows)
             def _():
                 put(k, kv).start()
 
@@ -707,7 +762,7 @@
         out_ref[:, tt * 128 : (tt + 1) * 128] = mix_ref[tt]
     sub = lax.broadcasted_iota(jnp.int32, (16, 128), 0)
     for k in range(MIG):
-        slot = idx_s[MIG + k]
+        slot = meta_s[0, MIG + k]
 
         @pl.when(slot < rows)
         def _():
@@ -721,12 +776,12 @@
     for k in range(MIG):
         for kv in range(2):
 
-            @pl.when(idx_s[MIG + k] < rows)
+            @pl.when(meta_s[0, MIG + k] < rows)
             def _():
                 put(k, kv).wait()
 
 
-def place_call(idx, mix, came, got, tail):
+def place_call(meta, mix, came, got, tail):
     n_tp, rows, wd = mix.shape
     vmem = pl.BlockSpec(memory_space=pltpu.VMEM)
     return pl.pallas_call(
@@ -740,49 +795,26 @@
         scratch_shapes=[pltpu.SemaphoreType.DMA((MIG, 2))],
         input_output_aliases={4: 1},
         name="place_rows",
-    )(idx, mix, came, got, tail)
+    )(meta, mix, came, got, tail)
 
 
 def body(
     hidden_in, prompt_kv, tail_kv, group_of, prompt_len, tail_len, bucket_of, bias_table, attn_gain, w_query, w_key,
     w_value, w_out, ffn_gain, router_weight, expert_ids, w_gate, w_up, w_down, new_slot,
 ):
-    rows = hidden_in.shape[0]
     n_req = lax.axis_size("req")
     n_tp = lax.axis_size("tp")
-    me = lax.axis_index("req")
-    local = jnp.arange(rows, dtype=jnp.int32)
-    kth = jnp.arange(MIG, dtype=jnp.int32)
-    tiles = new_slot.reshape(n_req * rows // 128, 128)
-    moved_t = tiles != jnp.arange(n_req * rows, dtype=jnp.int32).reshape(tiles.shape)
-    goes = jnp.max(jnp.where(moved_t, tiles // rows, -1), axis=1).reshape(n_req, rows // 128)
-    goes = jnp.max(goes, axis=1)
-    replica = jnp.arange(n_req, dtype=jnp.int32)
-    goes = jnp.where(goes < 0, replica, goes)
-    src = jnp.sum(jnp.where(goes[None, :] == replica[:, None], replica[None, :], 0), axis=1)
-    mine = lax.dynamic_slice_in_dim(new_slot, me * rows, rows, 0)
-    moved = mine != me * rows + local
-    key = jnp.concatenate([mine, local])
-    both = jnp.concatenate([moved, moved])
-    part = jnp.concatenate([jnp.zeros_like(local), jnp.ones_like(local)])
-    rank = jnp.sum(
-        (both[None, :] & (part[None, :] == part[:, None]) & (key[None, :] < key[:, None])).astype(jnp.int32), axis=1
-    )
-    want = jnp.arange(2 * MIG, dtype=jnp.int32)
-    hit = both[None, :] & (rank + part * MIG == want[:, None])
-    idx = jnp.min(jnp.where(hit, jnp.concatenate([local, local])[None, :], rows), axis=1)
-    idx = jnp.where(want < MIG, jnp.minimum(idx, rows - 1), idx)
     ids_t = expert_ids.T
-    tail_new, head, send_tail, slots = attention_call(
-        hidden_in, attn_gain, w_query, w_key, w_value, group_of, prompt_len, tail_len, bucket_of, bias_table.T, idx,
-        ids_t, prompt_kv, tail_kv,
+    tail_new, head, send_tail, slots, meta = attention_call(
+        hidden_in, attn_gain, w_query, w_key, w_value, group_of, prompt_len, tail_len, bucket_of, bias_table.T,
+        new_slot, ids_t, prompt_kv, tail_kv,
     )
     pieces = send_tail.reshape(n_req, -1, send_tail.shape[-1])
     mix, came, got = moe_call(
-        n_req, n_tp, src, idx, head, ffn_gain, router_weight.T, ids_t, slots, pieces, hidden_in, w_out,
+        n_req, n_tp, meta, head, ffn_gain, router_weight.T, ids_t, slots, pieces, hidden_in, w_out,
         w_gate[0].T, w_up[0].T, w_down[0],
     )
-    return place_call(idx, mix, came, got.reshape(send_tail.shape), tail_new)
+    return place_call(meta, mix, came, got.reshape(send_tail.shape), tail_new)
 
 
 def solution(mesh):

time: 88.5 us -> 83.2 us (0.940)
  other arithmetic: 5 us -> 0 us
  local copies, waits for them, and re-layouts: 1.36 us -> 0 us
  Pallas kernels: 81.1 us -> 82.3 us
    reduce_sum x2 -> x0, other arithmetic: 1.85 us -> none  [the longest x1 1.19 us: body(): jnp.sum((both[None, :] & (part[None, :] == part[:, None]) & (key[None, :]...]
    reshape x2 -> x0, local copies, waits for them, and re-layouts: 1.36 us -> none  [the longest x1 1.28 us: attention_call(): bucket_of.reshape(1, -1)]
    pallas_call x1, Pallas kernels: 20.4 us -> 21.5 us  [attention_call(): pl.pallas_call(attn_kernel, out_shape=(jax.ShapeDtypeStruct(tail_kv.shape...]
    reduce_max x2 -> x0, other arithmetic: 0.97 us -> none  [the longest x1 0.84 us: body(): jnp.max(jnp.where(moved_t, tiles // rows, -1), axis=1)]
where the time goes in v3:
time: 83.2 us; the launch traced here: 83 us
  Pallas kernels  82.3 us (99%)
    pallas_call x1, Pallas kernels, moe_call(): pl.pallas_call(moe_kernel, out_shape=(jax.ShapeDtypeStruct((n_tp, rows, 1...  58.2 us
    pallas_call x1, Pallas kernels, attention_call(): pl.pallas_call(attn_kernel, out_shape=(jax.ShapeDtypeStruct(tail_kv.shape...  21.5 us
    pallas_call x1, Pallas kernels, place_call(): pl.pallas_call(place_kernel, out_shape=(jax.ShapeDtypeStruct((rows, n_tp...  2.61 us

profile of v3, /device:TPU:1, one launch (start us, length us, event | category | flops | bytes accessed | tf_op | source)
XLA Modules:
  0.0 83.0 jit_solution(13623775295724027099)
XLA Ops:
  0.6 21.5 %attention_tails.1 = (bf16[2,256,64,128]{3,2,1,0:T(8,128)(2,1)}, f32[256,128]{1,0:T(8,128)}, bf16[4,2,64,128]{3,2,1,0:T(8,128)(2,1)}, f32[2,256,128]{2,1,0:T(8,128)}, s32[8,128]{1,0:T(8,128)}) custom-call(s32[256]{0:T(256)} %tl_s.1, f32[2,32]{1,0:T(2,128)} %bitcast.29, s32[8]{0:T(128)} %plen_s.1, s32[577]{0:T(1024)} %bkt_s.1, f32[1,1024]{1,0:T(1,128)} %bitcast.26, ...), custom_call_target="tpu_custom_call" | custom-call | tf_op jit(solution)/shard_map/attention_tails/pallas_call | solution.py:297
  22.1 58.2 %moe_exchange.1 = (bf16[8,256,128]{2,1,0:T(8,128)(2,1)}, bf16[8,16,128]{2,1,0:T(8,128)(2,1)}, bf16[16,32,128]{2,1,0:T(8,128)(2,1)}) custom-call(s32[8,128]{1,0:T(8,128)} %get-tuple-element.10.meta_s, f32[256,128]{1,0:T(8,128)} %get-tuple-element.11.head_ref, f32[1,1024]{1,0:T(1,128)} %bitcast.27, bf16[16,1024]{1,0:T(8,128)(2,1)} %bitcast.22, ...), custom_call_target="tpu_custom_call" | custom-call | tf_op jit(solution)/shard_map/moe_exchange/pallas_call | solution.py:715
  80.4 2.6 %place_rows.1 = (bf16[256,1024]{1,0:T(8,128)(2,1)}, bf16[2,256,64,128]{3,2,1,0:T(8,128)(2,1)}) custom-call(s32[8,128]{1,0:T(8,128)} %get-tuple-element.10.meta_s, bf16[8,256,128]{2,1,0:T(8,128)(2,1)} %get-tuple-element.14.mix_ref, bf16[8,16,128]{2,1,0:T(8,128)(2,1)} %get-tuple-element.15.came_ref, ...), custom_call_target="tpu_custom_call", output_to_operand_aliasing={{1}: (4, {})} | custom-call | tf_op jit(solution)/shard_map/place_rows/pallas_call | solution.py:787

commit v4 on v3

--- a/solution.py
+++ b/solution.py
@@ -12,6 +12,8 @@
 EPS = 1e-06
 NEG = -1e30
 RB = 32
+UB = 4
+TB = 8
 TOP = 2
 MIG = 4
 
@@ -166,74 +168,7 @@
     q = qkv[:, 0:128]
     kvn[0] = qkv[:, 128:256]
     kvn[1] = qkv[:, 256:384]
-    lane = lax.broadcasted_iota(jnp.int32, (nb, 2, 8, 128), 3)
-    head = lax.broadcasted_iota(jnp.int32, (nb, 2, 8, 128), 1)
-    qh = jnp.broadcast_to((q * 0.125).reshape(nb, 1, 8, 128), (nb, 2, 8, 128))
-    qh = jnp.where((lane // 64) == head, qh, 0.0).reshape(2 * rows, 128)
-    q16[...] = qh.astype(BF16)
-    loads[4].wait()
-    for i in range(groups):
-        lhs[:, i * 128 : (i + 1) * 128] = jnp.where(g2 == float(i), qh, 0.0).astype(BF16)
-        kcat[:, i * 128 : (i + 1) * 128] = pkv_v[0, i]
-    sco[...] = lax.dot_general(lhs[...], kcat[...], (((1,), (1,)), ((), ())), preferred_element_type=F32)
-
-    def take(tab, i):
-        return jnp.take_along_axis(tab, i, axis=1, mode="promise_in_bounds")
-
-    nch = pre // 128
-
-    def prompt_softmax(b):
-        pos = posb[pl.ds(b * 8, 8), :]
-        pb = plb[pl.ds(b * 8, 8), :]
-        tb = tlb[pl.ds(b * 8, 8), :]
-        ln = lax.broadcasted_iota(jnp.int32, (8, 128), 1)
-        sub = lax.broadcasted_iota(jnp.int32, (8, 128), 0)
-        low = pos & 127
-        gi = (low - ln) & 127
-        blk = (pos >> 7) - (ln > low).astype(jnp.int32)
-        at = [blk == k for k in range(nd)]
-        td = tb - (ln & 63)
-        tvalid = (td >= 0) & ((ln >> 6) == (sub & 1))
-        td = jnp.maximum(td, 0)
-        es = [[], []]
-        for hh in range(2):
-            rs = pl.ds(b * 16 + hh * 8, 8)
-            tbias[rs, :] = jnp.where(tvalid, take(dtab[hh, :, 0:128], td), NEG)
-            gs = [take(dtab[hh, :, k * 128 : (k + 1) * 128], gi) for k in range(nd)]
-            s = []
-            for c in range(nch):
-                bias = gs[0]
-                for k in range(1, nd - c):
-                    bias = jnp.where(at[k + c], gs[k], bias)
-                s.append(jnp.where(ln + c * 128 < pb, sco[rs, c * 128 : (c + 1) * 128] + bias, NEG))
-            mx = jnp.max(functools.reduce(jnp.maximum, s), axis=1, keepdims=True)
-            e = [jnp.exp(v - mx) for v in s]
-            tot = jnp.sum(functools.reduce(jnp.add, e), axis=1, keepdims=True)
-            mpart[rs, :] = jnp.broadcast_to(mx, (8, 128))
-            lpart[rs, :] = jnp.broadcast_to(tot, (8, 128))
-            es[hh] = e
-        for c in range(nch):
-            prob[pl.ds(b * 16, 16), c * 128 : (c + 1) * 128] = jnp.concatenate(
-                [es[0][c], es[1][c]], axis=0
-            ).astype(BF16)
-
-    @pl.loop(0, nb // 2)
-    def _(i):
-        prompt_softmax(pl.multiple_of(i * 2, 2))
-        prompt_softmax(i * 2 + 1)
-
-    loads[5].wait()
-    acc = jnp.zeros((2 * rows, 128), F32)
-    for i in range(0, groups, 2):
-        rhs = jnp.concatenate([pkv_v[1, i], pkv_v[1, i + 1]], axis=1)
-        o = jnp.dot(prob[...], rhs, preferred_element_type=F32)
-        acc = jnp.where(g2 == float(i), o[:, 0:128], acc)
-        acc = jnp.where(g2 == float(i + 1), o[:, 128:256], acc)
-    opart[...] = acc
-
     sub16 = lax.broadcasted_iota(jnp.int32, (16, 128), 0)
-    pair = lax.rem(sub16, 8) // 2
-    lane8 = lax.broadcasted_iota(jnp.int32, (8, 128), 1)
 
     @pl.loop(0, nblk)
     def _(s):
@@ -249,27 +184,114 @@
                 buf[kv, r, pl.ds(base, 16), :] = jnp.where(sub16 == length - base, row, w).astype(BF16)
         t_out(s, 0).start()
         t_out(s, 1).start()
-        for bb in range(RB // 8):
-            b = s * (RB // 8) + bb
-            rs = pl.ds(pl.multiple_of(b * 16, 16), 16)
-            own = pl.ds(b * 8, 8)
-            kb = buf[0, own].reshape(512, 128)
-            vb = buf[1, own].reshape(512, 128)
-            s4 = lax.dot_general(q16[rs, :], kb, (((1,), (1,)), ((), ())), preferred_element_type=F32)
+
+    lane = lax.broadcasted_iota(jnp.int32, (nb, 2, 8, 128), 3)
+    head = lax.broadcasted_iota(jnp.int32, (nb, 2, 8, 128), 1)
+    qh = jnp.broadcast_to((q * 0.125).reshape(nb, 1, 8, 128), (nb, 2, 8, 128))
+    qh = jnp.where((lane // 64) == head, qh, 0.0).reshape(2 * rows, 128)
+    q16[...] = qh.astype(BF16)
+    loads[4].wait()
+    for i in range(groups):
+        lhs[:, i * 128 : (i + 1) * 128] = jnp.where(g2 == float(i), qh, 0.0).astype(BF16)
+        kcat[:, i * 128 : (i + 1) * 128] = pkv_v[0, i]
+    sco[...] = lax.dot_general(lhs[...], kcat[...], (((1,), (1,)), ((), ())), preferred_element_type=F32)
+
+    def take(tab, i):
+        return jnp.take_along_axis(tab, i, axis=1, mode="promise_in_bounds")
+
+    nch = pre // 128
+
+    ln = lax.broadcasted_iota(jnp.int32, (8, 128), 1)
+    sub = lax.broadcasted_iota(jnp.int32, (8, 128), 0)
+    mine = (ln >> 6) == (sub & 1)
+
+    @pl.loop(0, nb // UB)
+    def _(i):
+        at = [i * UB + n for n in range(UB)]
+        pos = [posb[pl.ds(b * 8, 8), :] for b in at]
+        pb = [plb[pl.ds(b * 8, 8), :] for b in at]
+        tb = [tlb[pl.ds(b * 8, 8), :] for b in at]
+        raw = [
+            [[sco[pl.ds(b * 16 + hh * 8, 8), c * 128 : (c + 1) * 128] for c in range(nch)] for hh in range(2)]
+            for b in at
+        ]
+        tabs = [[dtab[hh, :, k * 128 : (k + 1) * 128] for k in range(nd)] for hh in range(2)]
+        out = []
+        for n in range(UB):
+            low = pos[n] & 127
+            gi = (low - ln) & 127
+            blk = (pos[n] >> 7) - (ln > low).astype(jnp.int32)
+            is_blk = [blk == k for k in range(nd)]
+            td = tb[n] - (ln & 63)
+            valid = (td >= 0) & mine
+            td = jnp.maximum(td, 0)
+            for hh in range(2):
+                tail = jnp.where(valid, take(tabs[hh][0], td), NEG)
+                gs = [take(tabs[hh][k], gi) for k in range(nd)]
+                s = []
+                for c in range(nch):
+                    bias = gs[0]
+                    for k in range(1, nd - c):
+                        bias = jnp.where(is_blk[k + c], gs[k], bias)
+                    s.append(jnp.where(ln + c * 128 < pb[n], raw[n][hh][c] + bias, NEG))
+                mx = jnp.max(functools.reduce(jnp.maximum, s), axis=1, keepdims=True)
+                e = [jnp.exp(v - mx) for v in s]
+                tot = jnp.sum(functools.reduce(jnp.add, e), axis=1, keepdims=True)
+                out.append((tail, mx, e, tot))
+        for n in range(UB):
+            for hh in range(2):
+                tail, mx, e, tot = out[n * 2 + hh]
+                rs = pl.ds(at[n] * 16 + hh * 8, 8)
+                tbias[rs, :] = tail
+                mpart[rs, :] = jnp.broadcast_to(mx, (8, 128))
+                lpart[rs, :] = jnp.broadcast_to(tot, (8, 128))
+            for c in range(nch):
+                prob[pl.ds(at[n] * 16, 16), c * 128 : (c + 1) * 128] = jnp.concatenate(
+                    [out[n * 2][2][c], out[n * 2 + 1][2][c]], axis=0
+                ).astype(BF16)
+
+    loads[5].wait()
+    acc = jnp.zeros((2 * rows, 128), F32)
+    for i in range(0, groups, 2):
+        rhs = jnp.concatenate([pkv_v[1, i], pkv_v[1, i + 1]], axis=1)
+        o = jnp.dot(prob[...], rhs, preferred_element_type=F32)
+        acc = jnp.where(g2 == float(i), o[:, 0:128], acc)
+        acc = jnp.where(g2 == float(i + 1), o[:, 128:256], acc)
+    opart[...] = acc
+
+    pair = lax.rem(sub16, 8) // 2
+    lane4 = lax.broadcasted_iota(jnp.int32, (TB, 8, 128), 2)
+
+    @pl.loop(0, nb // TB)
+    def _(i):
+        rs = pl.ds(pl.multiple_of(i * TB * 16, TB * 16), TB * 16)
+        scs = []
+        for n in range(TB):
+            b = i * TB + n
+            kb = buf[0, pl.ds(b * 8, 8)].reshape(512, 128)
+            qb = q16[pl.ds(pl.multiple_of(b * 16, 16), 16), :]
+            s4 = lax.dot_general(qb, kb, (((1,), (1,)), ((), ())), preferred_element_type=F32)
             sc = s4[:, 0:128]
             for c in range(1, 4):
                 sc = jnp.where(pair == c, s4[:, c * 128 : (c + 1) * 128], sc)
-            sc = sc + tbias[rs, :]
-            mt = jnp.max(sc, axis=1, keepdims=True)
-            mp = mpart[rs, :]
-            mx = jnp.maximum(mt, mp)
-            e = jnp.exp(sc - mx)
-            ap = jnp.exp(mp - mx)
-            tot = jnp.sum(e, axis=1, keepdims=True) + lpart[rs, :] * ap
-            p4 = jnp.concatenate([jnp.where(pair == c, e, 0.0) for c in range(4)], axis=1).astype(BF16)
-            o = jnp.dot(p4, vb, preferred_element_type=F32) + opart[rs, :] * ap
-            o = (o / tot).reshape(2, 8, 128)
-            head_ref[pl.ds(pl.multiple_of(b * 8, 8), 8), :] = jnp.where(lane8 < 64, o[0], o[1])
+            scs.append(sc)
+        sc = jnp.concatenate(scs, axis=0) + tbias[rs, :]
+        mp = mpart[rs, :]
+        mx = jnp.maximum(jnp.max(sc, axis=1, keepdims=True), mp)
+        e = jnp.exp(sc - mx)
+        ap = jnp.exp(mp - mx)
+        tot = jnp.sum(e, axis=1, keepdims=True) + lpart[rs, :] * ap
+        os = []
+        for n in range(TB):
+            b = i * TB + n
+            vb = buf[1, pl.ds(b * 8, 8)].reshape(512, 128)
+            en = e[n * 16 : (n + 1) * 16]
+            p4 = jnp.concatenate([jnp.where(pair == c, en, 0.0) for c in range(4)], axis=1).astype(BF16)
+            os.append(jnp.dot(p4, vb, preferred_element_type=F32))
+        o = (jnp.concatenate(os, axis=0) + opart[rs, :] * ap) / tot
+        o = o.reshape(TB, 2, 8, 128)
+        o = jnp.where(lane4 < 64, o[:, 0], o[:, 1]).reshape(TB * 8, 128)
+        head_ref[pl.ds(pl.multiple_of(i * TB * 8, TB * 8), TB * 8), :] = o
 
     meta_copy.wait()
     for m in range(mig):
@@ -647,28 +669,28 @@
         j = lax.rem(r + d, n_req)
         return req_copy(mvs, mvr.at[r], s_mv.at[d], r_mv.at[d], j)
 
-    @pl.loop(1, n_req)
-    def _(d):
-        mv_copy(d).start()
-
-    mvr[r] = mvs[...]
     mix[t] = mixed
     o_ag = (mix, s_ox, r_ox, s_os, r_os)
     ag_start(*o_ag)
-    ag_pass(*o_ag)
-
-    @pl.loop(1, n_req)
-    def _(d):
-        mv_copy(d).wait_recv()
-
-    came[t] = mvr[meta_s[1, r]]
+
+    @pl.loop(1, n_req)
+    def _(d):
+        mv_copy(d).start()
+
+    mvr[r] = mvs[...]
 
     def cm_copy(d):
         return tp_copy(came.at[t], came.at[t], s_cm.at[d], r_cm.at[d], lax.rem(t + d, n_tp))
 
+    @pl.loop(1, n_req)
+    def _(d):
+        mv_copy(d).wait_recv()
+
+    came[t] = mvr[meta_s[1, r]]
     for d in range(1, n_tp):
         cm_copy(d).start()
 
+    ag_pass(*o_ag)
     ag_wait(*o_ag)
     for d in range(1, n_tp):
         who = lax.rem(t + n_tp - d, n_tp)

time: 83.2 us -> 78.7 us (0.946)
  Pallas kernels: 82.3 us -> 77.8 us
    pallas_call x1, Pallas kernels: 21.5 us -> 16.9 us  [attention_call(): pl.pallas_call(attn_kernel, out_shape=(jax.ShapeDtypeStruct(tail_kv.shape...]
where the time goes in v4:
time: 78.7 us; the launch traced here: 78.4 us
  Pallas kernels  77.8 us (99%)
    pallas_call x1, Pallas kernels, moe_call(): pl.pallas_call(moe_kernel, out_shape=(jax.ShapeDtypeStruct((n_tp, rows, 1...  58.3 us
    pallas_call x1, Pallas kernels, attention_call(): pl.pallas_call(attn_kernel, out_shape=(jax.ShapeDtypeStruct(tail_kv.shape...  16.9 us
    pallas_call x1, Pallas kernels, place_call(): pl.pallas_call(place_kernel, out_shape=(jax.ShapeDtypeStruct((rows, n_tp...  2.61 us

profile of v4, /device:TPU:1, one launch (start us, length us, event | category | flops | bytes accessed | tf_op | source)
XLA Modules:
  0.0 78.4 jit_solution(1750454682309011783)
XLA Ops:
  0.6 16.9 %attention_tails.1 = (bf16[2,256,64,128]{3,2,1,0:T(8,128)(2,1)}, f32[256,128]{1,0:T(8,128)}, bf16[4,2,64,128]{3,2,1,0:T(8,128)(2,1)}, f32[2,256,128]{2,1,0:T(8,128)}, s32[8,128]{1,0:T(8,128)}) custom-call(s32[256]{0:T(256)} %tl_s.1, f32[2,32]{1,0:T(2,128)} %bitcast.29, s32[8]{0:T(128)} %plen_s.1, s32[577]{0:T(1024)} %bkt_s.1, f32[1,1024]{1,0:T(1,128)} %bitcast.26, ...), custom_call_target="tpu_custom_call" | custom-call | tf_op jit(solution)/shard_map/attention_tails/pallas_call | solution.py:319
  17.5 58.3 %moe_exchange.1 = (bf16[8,256,128]{2,1,0:T(8,128)(2,1)}, bf16[8,16,128]{2,1,0:T(8,128)(2,1)}, bf16[16,32,128]{2,1,0:T(8,128)(2,1)}) custom-call(s32[8,128]{1,0:T(8,128)} %get-tuple-element.10.meta_s, f32[256,128]{1,0:T(8,128)} %get-tuple-element.11.head_ref, f32[1,1024]{1,0:T(1,128)} %bitcast.27, bf16[16,1024]{1,0:T(8,128)(2,1)} %bitcast.22, ...), custom_call_target="tpu_custom_call" | custom-call | tf_op jit(solution)/shard_map/moe_exchange/pallas_call | solution.py:737
  75.8 2.6 %place_rows.1 = (bf16[256,1024]{1,0:T(8,128)(2,1)}, bf16[2,256,64,128]{3,2,1,0:T(8,128)(2,1)}) custom-call(s32[8,128]{1,0:T(8,128)} %get-tuple-element.10.meta_s, bf16[8,256,128]{2,1,0:T(8,128)(2,1)} %get-tuple-element.14.mix_ref, bf16[8,16,128]{2,1,0:T(8,128)(2,1)} %get-tuple-element.15.came_ref, ...), custom_call_target="tpu_custom_call", output_to_operand_aliasing={{1}: (4, {})} | custom-call | tf_op jit(solution)/shard_map/place_rows/pallas_call | solution.py:809

commit v5 on v4

--- a/solution.py
+++ b/solution.py
@@ -69,8 +69,8 @@
 def attn_kernel(
     tl_s, tab_s, plen_s, bkt_s,
     gain_ref, grp_ref, tlr_ref, ids_ref, ns_ref, hid_any, wq_any, wk_any, wv_any, pkv_any, tail_any,
-    tail_out, head_ref, send_ref, slot_ref, meta_ref,
-    hid_v, wcat, pkv_v, buf, q16, kvn, lhs, kcat, sco, prob, posb, plb, tlb, dtab, tbias, opart, mpart, lpart,
+    tail_out, send_ref, slot_ref, meta_ref, q16, tbias, mpart, lpart, opart,
+    hid_v, wcat, pkv_v, buf, kvn, lhs, kcat, sco, prob, posb, plb, tlb, dtab,
     first_s, meta_s, s_in, s_tin, s_tout, s_meta,
 ):
     rows = hid_v.shape[0]
@@ -259,40 +259,6 @@
         acc = jnp.where(g2 == float(i + 1), o[:, 128:256], acc)
     opart[...] = acc
 
-    pair = lax.rem(sub16, 8) // 2
-    lane4 = lax.broadcasted_iota(jnp.int32, (TB, 8, 128), 2)
-
-    @pl.loop(0, nb // TB)
-    def _(i):
-        rs = pl.ds(pl.multiple_of(i * TB * 16, TB * 16), TB * 16)
-        scs = []
-        for n in range(TB):
-            b = i * TB + n
-            kb = buf[0, pl.ds(b * 8, 8)].reshape(512, 128)
-            qb = q16[pl.ds(pl.multiple_of(b * 16, 16), 16), :]
-            s4 = lax.dot_general(qb, kb, (((1,), (1,)), ((), ())), preferred_element_type=F32)
-            sc = s4[:, 0:128]
-            for c in range(1, 4):
-                sc = jnp.where(pair == c, s4[:, c * 128 : (c + 1) * 128], sc)
-            scs.append(sc)
-        sc = jnp.concatenate(scs, axis=0) + tbias[rs, :]
-        mp = mpart[rs, :]
-        mx = jnp.maximum(jnp.max(sc, axis=1, keepdims=True), mp)
-        e = jnp.exp(sc - mx)
-        ap = jnp.exp(mp - mx)
-        tot = jnp.sum(e, axis=1, keepdims=True) + lpart[rs, :] * ap
-        os = []
-        for n in range(TB):
-            b = i * TB + n
-            vb = buf[1, pl.ds(b * 8, 8)].reshape(512, 128)
-            en = e[n * 16 : (n + 1) * 16]
-            p4 = jnp.concatenate([jnp.where(pair == c, en, 0.0) for c in range(4)], axis=1).astype(BF16)
-            os.append(jnp.dot(p4, vb, preferred_element_type=F32))
-        o = (jnp.concatenate(os, axis=0) + opart[rs, :] * ap) / tot
-        o = o.reshape(TB, 2, 8, 128)
-        o = jnp.where(lane4 < 64, o[:, 0], o[:, 1]).reshape(TB * 8, 128)
-        head_ref[pl.ds(pl.multiple_of(i * TB * 8, TB * 8), TB * 8), :] = o
-
     meta_copy.wait()
     for m in range(mig):
         for kv in range(2):
@@ -320,19 +286,19 @@
         attn_kernel,
         out_shape=(
             jax.ShapeDtypeStruct(tail_kv.shape, BF16),
-            jax.ShapeDtypeStruct((rows, wd), F32),
             jax.ShapeDtypeStruct((MIG, 2, tail_rows, wd), BF16),
             jax.ShapeDtypeStruct((2, rows, 128), F32),
             jax.ShapeDtypeStruct((8, 128), jnp.int32),
-        ),
+            jax.ShapeDtypeStruct((2 * rows, wd), BF16),
+        )
+        + (jax.ShapeDtypeStruct((2 * rows, 128), F32),) * 4,
         in_specs=[smem] * 4 + [vmem] * 5 + [anym] * 6,
-        out_specs=(anym, vmem, vmem, vmem, vmem),
+        out_specs=(anym,) + (vmem,) * 8,
         scratch_shapes=[
             pltpu.VMEM((rows, width), BF16),
             pltpu.VMEM((width, 3 * wd), BF16),
             pltpu.VMEM(prompt_kv.shape, BF16),
             pltpu.VMEM(tail_kv.shape, BF16),
-            pltpu.VMEM((2 * rows, wd), BF16),
             pltpu.VMEM((2, rows, wd), F32),
             pltpu.VMEM((2 * rows, groups * wd), BF16),
             pltpu.VMEM((pre, groups * wd), BF16),
@@ -342,10 +308,6 @@
             pltpu.VMEM((rows, 128), jnp.int32),
             pltpu.VMEM((rows, 128), jnp.int32),
             pltpu.VMEM((2, 8, nd * 128), F32),
-            pltpu.VMEM((2 * rows, 128), F32),
-            pltpu.VMEM((2 * rows, 128), F32),
-            pltpu.VMEM((2 * rows, 128), F32),
-            pltpu.VMEM((2 * rows, 128), F32),
             pltpu.SMEM((table_t.shape[1],), jnp.int32),
             pltpu.SMEM((8, 128), jnp.int32),
             dma((6,)),
@@ -368,11 +330,11 @@
 
 def moe_kernel(
     meta_s,
-    head_ref, gain_ref, router_ref, ids_ref, slot_ref, tail_ref, hid_any, wout_any, wg_any, wu_any, wd_any,
+    q16, tbias, mpart, lpart, opart, gain_ref, router_ref, ids_ref, slot_ref, tail_ref, kv_any, hid_any, wout_any, wg_any, wu_any, wd_any,
     mix, came, got,
-    hid_v, wout_v, wg_v, wu_v, wd_v,
+    buf, head_v, hid_v, wout_v, wg_v, wu_v, wd_v,
     t1, t2, part, psib, psend, precv, stat, statr, dsend, drecv, xall, ypart, ysib, ysend, yrecv, rsend, rrecv, mvs, mvr,
-    s_in, s_t1, r_t1, s_t2, r_t2, s_ps, r_ps, s_px, r_px, s_st, r_st, s_d, r_d, s_gx, r_gx, s_gs, r_gs,
+    s_in, s_kv, s_t1, r_t1, s_t2, r_t2, s_ps, r_ps, s_px, r_px, s_st, r_st, s_d, r_d, s_gx, r_gx, s_gs, r_gs,
     s_ys, r_ys, s_yx, r_yx, s_r, r_r, s_mv, r_mv, s_ox, r_ox, s_os, r_os, s_cm, r_cm,
 ):
     r = lax.axis_index("req")
@@ -399,6 +361,16 @@
         pltpu.make_async_copy(wu_any, wu_v, s_in.at[3]),
         pltpu.make_async_copy(wd_any, wd_v, s_in.at[4]),
     ]
+    nkv = rows // (TB * 8)
+
+    def kv_load(i):
+        sl = pl.ds(i * TB * 8, TB * 8)
+        return pltpu.make_async_copy(kv_any.at[:, sl], buf.at[:, sl], s_kv.at[i])
+
+    @pl.loop(0, nkv)
+    def _(i):
+        kv_load(i).start()
+
     for cp in loads:
         cp.start()
 
@@ -428,7 +400,43 @@
     def _(d):
         pl.semaphore_signal(barrier, inc=1, device_id=(lax.rem(r + d, n_req), t), device_id_type=MESH)
 
-    head = head_ref[...].astype(BF16)
+    sub16 = lax.broadcasted_iota(jnp.int32, (16, 128), 0)
+    pair = lax.rem(sub16, 8) // 2
+    lane4 = lax.broadcasted_iota(jnp.int32, (TB, 8, 128), 2)
+
+    @pl.loop(0, nkv)
+    def _(i):
+        kv_load(i).wait()
+        rs = pl.ds(pl.multiple_of(i * TB * 16, TB * 16), TB * 16)
+        scs = []
+        for n in range(TB):
+            b = i * TB + n
+            kb = buf[0, pl.ds(b * 8, 8)].reshape(512, 128)
+            qb = q16[pl.ds(pl.multiple_of(b * 16, 16), 16), :]
+            s4 = lax.dot_general(qb, kb, (((1,), (1,)), ((), ())), preferred_element_type=F32)
+            sc = s4[:, 0:128]
+            for j in range(1, 4):
+                sc = jnp.where(pair == j, s4[:, j * 128 : (j + 1) * 128], sc)
+            scs.append(sc)
+        sc = jnp.concatenate(scs, axis=0) + tbias[rs, :]
+        mp = mpart[rs, :]
+        mx = jnp.maximum(jnp.max(sc, axis=1, keepdims=True), mp)
+        e = jnp.exp(sc - mx)
+        ap = jnp.exp(mp - mx)
+        tot = jnp.sum(e, axis=1, keepdims=True) + lpart[rs, :] * ap
+        os = []
+        for n in range(TB):
+            b = i * TB + n
+            vb = buf[1, pl.ds(b * 8, 8)].reshape(512, 128)
+            en = e[n * 16 : (n + 1) * 16]
+            p4 = jnp.concatenate([jnp.where(pair == j, en, 0.0) for j in range(4)], axis=1).astype(BF16)
+            os.append(jnp.dot(p4, vb, preferred_element_type=F32))
+        o = (jnp.concatenate(os, axis=0) + opart[rs, :] * ap) / tot
+        o = o.reshape(TB, 2, 8, 128)
+        o = jnp.where(lane4 < 64, o[:, 0], o[:, 1]).reshape(TB * 8, 128)
+        head_v[pl.ds(pl.multiple_of(i * TB * 8, TB * 8), TB * 8), :] = o.astype(BF16)
+
+    head = head_v[...]
     loads[0].wait()
     for tt in range(n_tp):
         part[tt % 2, tt // 2] = jnp.dot(
@@ -718,7 +726,7 @@
         mv_copy(d).wait_send()
 
 
-def moe_call(n_req, n_tp, meta, head, gain, router_t, ids_t, slots, send_tail, hidden, w_out, wg_t, wu_t, wd):
+def moe_call(n_req, n_tp, meta, parts, gain, router_t, ids_t, slots, send_tail, tail, hidden, w_out, wg_t, wu_t, wd):
     rows, width = hidden.shape
     cap = 5 * rows * TOP // (4 * n_req)
     nsl = n_req * cap
@@ -741,10 +749,10 @@
             jax.ShapeDtypeStruct((n_tp, 16, 128), BF16),
             jax.ShapeDtypeStruct((n_req, chunk, 128), BF16),
         ),
-        in_specs=[smem] + [vmem] * 6 + [anym] * 5,
+        in_specs=[smem] + [vmem] * 10 + [anym] * 6,
         out_specs=(vmem, vmem, vmem),
         scratch_shapes=[
-            bf(rows, 128), bf(*w_out.shape), bf(*wg_t.shape), bf(*wu_t.shape), bf(*wd.shape),
+            bf(*tail.shape), bf(rows, 128), bf(rows, 128), bf(*w_out.shape), bf(*wg_t.shape), bf(*wu_t.shape), bf(*wd.shape),
             bf(n_req, chunk, 128), bf(n_req, chunk, 128),
             bf(2, n_x, rows, 128), bf(n_x, rows, 128), bf(n_x, rows, 128), bf(n_x, rows, 128),
             pltpu.VMEM((8, rows), F32), pltpu.VMEM((n_tp, 8, rows), F32),
@@ -754,6 +762,7 @@
             bf(16, 128), bf(n_req, 16, 128),
         ]
         + [dma((5,))]
+        + [dma((rows // (TB * 8),))]
         + [dma((n_req,))] * 4
         + [dma((n_x,))] * 4
         + [dma((n_tp,))] * 2
@@ -764,7 +773,7 @@
         + [dma((n_tp,))] * 2,
         compiler_params=pltpu.CompilerParams(collective_id=0, has_side_effects=True, vmem_limit_bytes=56 << 20),
         name="moe_exchange",
-    )(meta, head, gain.reshape(1, -1), router_t, ids_t, slots, send_tail, hidden, w_out, wg_t, wu_t, wd)
+    )(meta, *parts, gain.reshape(1, -1), router_t, ids_t, slots, send_tail, tail, hidden, w_out, wg_t, wu_t, wd)
 
 
 def place_kernel(meta_s, mix_ref, came_ref, got_ref, tail_in, out_ref, tail_out, sems):
@@ -827,13 +836,13 @@
     n_req = lax.axis_size("req")
     n_tp = lax.axis_size("tp")
     ids_t = expert_ids.T
-    tail_new, head, send_tail, slots, meta = attention_call(
+    tail_new, send_tail, slots, meta, *parts = attention_call(
         hidden_in, attn_gain, w_query, w_key, w_value, group_of, prompt_len, tail_len, bucket_of, bias_table.T,
         new_slot, ids_t, prompt_kv, tail_kv,
     )
     pieces = send_tail.reshape(n_req, -1, send_tail.shape[-1])
     mix, came, got = moe_call(
-        n_req, n_tp, meta, head, ffn_gain, router_weight.T, ids_t, slots, pieces, hidden_in, w_out,
+        n_req, n_tp, meta, parts, ffn_gain, router_weight.T, ids_t, slots, pieces, tail_new, hidden_in, w_out,
         w_gate[0].T, w_up[0].T, w_down[0],
     )
     return place_call(meta, mix, came, got.reshape(send_tail.shape), tail_new)

time: 78.7 us -> 78.8 us (level)
    pallas_call x1, Pallas kernels: 58.3 us -> 60.4 us  [moe_call(): pl.pallas_call(moe_kernel, out_shape=(jax.ShapeDtypeStruct((n_tp, rows, 1...]
    pallas_call x1, Pallas kernels: 16.9 us -> 14.9 us  [attention_call(): pl.pallas_call(attn_kernel, out_shape=(jax.ShapeDtypeStruct(tail_kv.shape...]
where the time goes in v5:
time: 78.8 us; the launch traced here: 78.6 us
  Pallas kernels  77.9 us (99%)
    pallas_call x1, Pallas kernels, moe_call(): pl.pallas_call(moe_kernel, out_shape=(jax.ShapeDtypeStruct((n_tp, rows, 1...  60.4 us
    pallas_call x1, Pallas kernels, attention_call(): pl.pallas_call(attn_kernel, out_shape=(jax.ShapeDtypeStruct(tail_kv.shape...  14.9 us
    pallas_call x1, Pallas kernels, place_call(): pl.pallas_call(place_kernel, out_shape=(jax.ShapeDtypeStruct((rows, n_tp...  2.61 us

profile of v5, /device:TPU:1, one launch (start us, length us, event | category | flops | bytes accessed | tf_op | source)
XLA Modules:
  0.0 78.6 jit_solution(16253372650394865185)
XLA Ops:
  0.6 14.9 %attention_tails.1 = (bf16[2,256,64,128]{3,2,1,0:T(8,128)(2,1)}, bf16[4,2,64,128]{3,2,1,0:T(8,128)(2,1)}, f32[2,256,128]{2,1,0:T(8,128)}, s32[8,128]{1,0:T(8,128...) custom-call(s32[256]{0:T(256)} %tl_s.1, ...), custom_call_target="tpu_custom_call" | custom-call | tf_op jit(solution)/shard_map/attention_tails/pallas_call | solution.py:285
  15.5 60.4 %moe_exchange.1 = (bf16[8,256,128]{2,1,0:T(8,128)(2,1)}, bf16[8,16,128]{2,1,0:T(8,128)(2,1)}, bf16[16,32,128]{2,1,0:T(8,128)(2,1)}) custom-call(s32[8,128]{1,0:T(8,128)} %get-tuple-element.14.meta_s, bf16[512,128]{1,0:T(8,128)(2,1)} %get-tuple-element.15.q16, f32[512,128]{1,0:T(8,128)} %get-tuple-element.16.tbias, f32[512,128]{1,0:T(8,128)} %get-tuple-element.17.mpart, ...), custom_call_target="tpu_custom_call" | custom-call | tf_op jit(solution)/shard_map/moe_exchange/pallas_call | solution.py:745
  75.9 2.6 %place_rows.1 = (bf16[256,1024]{1,0:T(8,128)(2,1)}, bf16[2,256,64,128]{3,2,1,0:T(8,128)(2,1)}) custom-call(s32[8,128]{1,0:T(8,128)} %get-tuple-element.14.meta_s, bf16[8,256,128]{2,1,0:T(8,128)(2,1)} %get-tuple-element.23.mix_ref, bf16[8,16,128]{2,1,0:T(8,128)(2,1)} %get-tuple-element.24.came_ref, ...), custom_call_target="tpu_custom_call", output_to_operand_aliasing={{1}: (4, {})} | custom-call | tf_op jit(solution)/shard_map/place_rows/pallas_call | solution.py:818

commit v6 on v5

--- a/solution.py
+++ b/solution.py
@@ -68,8 +68,8 @@
 
 def attn_kernel(
     tl_s, tab_s, plen_s, bkt_s,
-    gain_ref, grp_ref, tlr_ref, ids_ref, ns_ref, hid_any, wq_any, wk_any, wv_any, pkv_any, tail_any,
-    tail_out, send_ref, slot_ref, meta_ref, q16, tbias, mpart, lpart, opart,
+    gain_ref, grp_ref, tlr_ref, ns_ref, hid_any, wq_any, wk_any, wv_any, pkv_any, tail_any,
+    tail_out, send_ref, meta_ref, q16, tbias, mpart, lpart, opart,
     hid_v, wcat, pkv_v, buf, kvn, lhs, kcat, sco, prob, posb, plb, tlb, dtab,
     first_s, meta_s, s_in, s_tin, s_tout, s_meta,
 ):
@@ -140,25 +140,6 @@
     tlb[...] = tl.astype(jnp.int32)
     g2 = jnp.broadcast_to(g.reshape(nb, 1, 8, 128), (nb, 2, 8, 128)).reshape(2 * rows, 128)
 
-    e0 = col_form(ids_ref[0:1, :])
-    e1 = col_form(ids_ref[1:2, :])
-    ln = lax.broadcasted_iota(jnp.int32, (rows, 128), 1).astype(F32)
-    hit0 = ln == e0
-    hit1 = ln == e1
-    ri = lax.broadcasted_iota(jnp.int32, (rows, rows), 0)
-    ci = lax.broadcasted_iota(jnp.int32, (rows, rows), 1)
-    lower = (ci < ri).astype(F32).astype(BF16)
-    o0 = hit0.astype(F32)
-    o1 = hit1.astype(F32)
-    cum0 = jnp.dot(lower, o0.astype(BF16), preferred_element_type=F32)
-    cum1 = jnp.dot(lower, o1.astype(BF16), preferred_element_type=F32)
-    tot0 = jnp.sum(o0, axis=0, keepdims=True)
-    p0 = jnp.sum(jnp.where(hit0, cum0, 0.0), axis=1, keepdims=True)
-    p1 = jnp.sum(jnp.where(hit1, cum1 + tot0, 0.0), axis=1, keepdims=True)
-    stride = float(slot_stride(5 * rows * TOP // (4 * 16)))
-    slot_ref[0] = e0 * stride + p0
-    slot_ref[1] = e1 * stride + p1
-
     for cp in loads[:4]:
         cp.wait()
     h = hid_v[...].astype(F32)
@@ -168,23 +149,6 @@
     q = qkv[:, 0:128]
     kvn[0] = qkv[:, 128:256]
     kvn[1] = qkv[:, 256:384]
-    sub16 = lax.broadcasted_iota(jnp.int32, (16, 128), 0)
-
-    @pl.loop(0, nblk)
-    def _(s):
-        t_in(s, 0).wait()
-        t_in(s, 1).wait()
-        for i in range(RB):
-            r = s * RB + i
-            length = tl_s[r]
-            base = pl.multiple_of((length >> 4) << 4, 16)
-            for kv in range(2):
-                w = buf[kv, r, pl.ds(base, 16), :].astype(F32)
-                row = kvn[kv, pl.ds(r, 1), :]
-                buf[kv, r, pl.ds(base, 16), :] = jnp.where(sub16 == length - base, row, w).astype(BF16)
-        t_out(s, 0).start()
-        t_out(s, 1).start()
-
     lane = lax.broadcasted_iota(jnp.int32, (nb, 2, 8, 128), 3)
     head = lax.broadcasted_iota(jnp.int32, (nb, 2, 8, 128), 1)
     qh = jnp.broadcast_to((q * 0.125).reshape(nb, 1, 8, 128), (nb, 2, 8, 128))
@@ -205,8 +169,7 @@
     sub = lax.broadcasted_iota(jnp.int32, (8, 128), 0)
     mine = (ln >> 6) == (sub & 1)
 
-    @pl.loop(0, nb // UB)
-    def _(i):
+    def prompt_softmax(i):
         at = [i * UB + n for n in range(UB)]
         pos = [posb[pl.ds(b * 8, 8), :] for b in at]
         pb = [plb[pl.ds(b * 8, 8), :] for b in at]
@@ -250,6 +213,27 @@
                     [out[n * 2][2][c], out[n * 2 + 1][2][c]], axis=0
                 ).astype(BF16)
 
+    half = nb // UB // 2
+    pl.loop(0, half)(prompt_softmax)
+
+    sub16 = lax.broadcasted_iota(jnp.int32, (16, 128), 0)
+
+    @pl.loop(0, nblk)
+    def _(s):
+        t_in(s, 0).wait()
+        t_in(s, 1).wait()
+        for i in range(RB):
+            r = s * RB + i
+            length = tl_s[r]
+            base = pl.multiple_of((length >> 4) << 4, 16)
+            for kv in range(2):
+                w = buf[kv, r, pl.ds(base, 16), :].astype(F32)
+                row = kvn[kv, pl.ds(r, 1), :]
+                buf[kv, r, pl.ds(base, 16), :] = jnp.where(sub16 == length - base, row, w).astype(BF16)
+        t_out(s, 0).start()
+        t_out(s, 1).start()
+
+    pl.loop(half, nb // UB)(prompt_softmax)
     loads[5].wait()
     acc = jnp.zeros((2 * rows, 128), F32)
     for i in range(0, groups, 2):
@@ -271,7 +255,7 @@
 
 
 def attention_call(
-    hidden_in, gain, wq, wk, wv, group_of, prompt_len, tail_len, bucket_of, table_t, new_slot, ids_t, prompt_kv, tail_kv
+    hidden_in, gain, wq, wk, wv, group_of, prompt_len, tail_len, bucket_of, table_t, new_slot, prompt_kv, tail_kv
 ):
     rows, width = hidden_in.shape
     smem = pl.BlockSpec(memory_space=pltpu.SMEM)
@@ -287,13 +271,12 @@
         out_shape=(
             jax.ShapeDtypeStruct(tail_kv.shape, BF16),
             jax.ShapeDtypeStruct((MIG, 2, tail_rows, wd), BF16),
-            jax.ShapeDtypeStruct((2, rows, 128), F32),
             jax.ShapeDtypeStruct((8, 128), jnp.int32),
             jax.ShapeDtypeStruct((2 * rows, wd), BF16),
         )
         + (jax.ShapeDtypeStruct((2 * rows, 128), F32),) * 4,
-        in_specs=[smem] * 4 + [vmem] * 5 + [anym] * 6,
-        out_specs=(anym,) + (vmem,) * 8,
+        in_specs=[smem] * 4 + [vmem] * 4 + [anym] * 6,
+        out_specs=(anym,) + (vmem,) * 7,
         scratch_shapes=[
             pltpu.VMEM((rows, width), BF16),
             pltpu.VMEM((width, 3 * wd), BF16),
@@ -319,7 +302,7 @@
         name="attention_tails",
     )(
         tail_len, table_t, prompt_len, bucket_of,
-        gain.reshape(1, -1), group_of.reshape(1, -1), tail_len.reshape(1, -1), ids_t, new_slot.reshape(-1, 128),
+        gain.reshape(1, -1), group_of.reshape(1, -1), tail_len.reshape(1, -1), new_slot.reshape(-1, 128),
         hidden_in, wq, wk, wv, prompt_kv, tail_kv,
     )
 
@@ -330,10 +313,10 @@
 
 def moe_kernel(
     meta_s,
-    q16, tbias, mpart, lpart, opart, gain_ref, router_ref, ids_ref, slot_ref, tail_ref, kv_any, hid_any, wout_any, wg_any, wu_any, wd_any,
+    q16, tbias, mpart, lpart, opart, gain_ref, router_ref, ids_ref, tail_ref, kv_any, hid_any, wout_any, wg_any, wu_any, wd_any,
     mix, came, got,
     buf, head_v, hid_v, wout_v, wg_v, wu_v, wd_v,
-    t1, t2, part, psib, psend, precv, stat, statr, dsend, drecv, xall, ypart, ysib, ysend, yrecv, rsend, rrecv, mvs, mvr,
+    t1, t2, part, psib, psend, precv, stat, statr, dsend, drecv, xall, ypart, ysib, ysend, yrecv, rsend, rrecv, mvs, mvr, pickt, pick0, pick1,
     s_in, s_kv, s_t1, r_t1, s_t2, r_t2, s_ps, r_ps, s_px, r_px, s_st, r_st, s_d, r_d, s_gx, r_gx, s_gs, r_gs,
     s_ys, r_ys, s_yx, r_yx, s_r, r_r, s_mv, r_mv, s_ox, r_ox, s_os, r_os, s_cm, r_cm,
 ):
@@ -489,6 +472,10 @@
             ag_x(d, buf, ss1, rs1).start()
         ag_s(0, buf, ss2, rs2).start()
 
+    def ag_left(buf, ss1, rs1, ss2, rs2):
+        for d in (2, 1, 3):
+            ag_x(d, buf, ss1, rs1).wait_send()
+
     def ag_pass(buf, ss1, rs1, ss2, rs2):
         for d in (1, 3, 2):
             who = xfrom(d)
@@ -501,9 +488,9 @@
             other = lax.rem(x + n_x - d, n_x) * 2 + 1 - c
             tp_copy(buf.at[mine], buf.at[other], ss2.at[d], rs2.at[d], sib).wait_recv()
 
-    def ag_finish(buf, ss1, rs1, ss2, rs2):
-        for d in (1, 2, 3):
-            ag_x(d, buf, ss1, rs1).wait_send()
+    def ag_finish(buf, ss1, rs1, ss2, rs2, left=False):
+        if not left:
+            ag_left(buf, ss1, rs1, ss2, rs2)
         for d in (0, 1, 2, 3):
             ag_s(d, buf, ss2, rs2).wait_send()
 
@@ -515,17 +502,30 @@
         j = lax.rem(r + d, n_req)
         return req_copy(tail_ref.at[j], t1.at[r], s_t1.at[d], r_t1.at[d], j)
 
+    lnf = lax.broadcasted_iota(jnp.int32, (rows, 128), 1).astype(F32)
+    e0 = col_form(ids_ref[0:1, :])
+    e1 = col_form(ids_ref[1:2, :])
+    hit0 = lnf == e0
+    hit1 = lnf == e1
+    lower = lax.broadcasted_iota(jnp.int32, (rows, rows), 1) < lax.broadcasted_iota(jnp.int32, (rows, rows), 0)
+    lower = lower.astype(F32).astype(BF16)
+    o0 = hit0.astype(F32)
+    o1 = hit1.astype(F32)
+    cum0 = jnp.dot(lower, o0.astype(BF16), preferred_element_type=F32)
+    cum1 = jnp.dot(lower, o1.astype(BF16), preferred_element_type=F32)
+    tot0 = jnp.sum(o0, axis=0, keepdims=True)
+    s0 = e0 * float(capp) + jnp.sum(jnp.where(hit0, cum0, 0.0), axis=1, keepdims=True)
+    s1 = e1 * float(capp) + jnp.sum(jnp.where(hit1, cum1 + tot0, 0.0), axis=1, keepdims=True)
+    row0 = jnp.transpose(s0)[0:1]
+    row1 = jnp.transpose(s1)[0:1]
+    sl = lax.broadcasted_iota(jnp.int32, (128, rows), 0).astype(F32)
+    for k in range(nslp // 128):
+        here = sl + float(k * 128)
+        pickt[k * 128 : (k + 1) * 128, :] = ((here == row0) | (here == row1)).astype(F32).astype(BF16)
     loads[1].wait()
     resid = (hid_v[...].astype(F32) + rs_total(*attn_rs)).astype(BF16)
 
-    s0 = slot_ref[0]
-    s1 = slot_ref[1]
-    lnf = lax.broadcasted_iota(jnp.int32, (rows, 128), 1).astype(F32)
-    for k in range(nslp // 128):
-        pick = (s0 == lnf + float(k * 128)) | (s1 == lnf + float(k * 128))
-        dsend[k * 128 : (k + 1) * 128, :] = lax.dot_general(
-            pick.astype(F32).astype(BF16), resid, (((0,), (0,)), ((), ())), preferred_element_type=F32
-        ).astype(BF16)
+    dsend[...] = jnp.dot(pickt[...], resid, preferred_element_type=F32).astype(BF16)
 
     def block(j):
         return pl.ds(pl.multiple_of(j * capp, 16), capp)
@@ -540,19 +540,12 @@
 
     drecv[block(r), :] = dsend[block(r), :]
 
-    @pl.loop(1, n_req)
-    def _(d):
-        t1_copy(d).start()
-
-    t1[r] = tail_ref[r]
 
     rf = resid.astype(F32)
     u = rf * gain_ref[:, lanes]
     lg = lax.dot_general(
         u.astype(BF16), router_ref[:, lanes], (((1,), (1,)), ((), ())), preferred_element_type=F32
     )
-    e0 = col_form(ids_ref[0:1, :])
-    e1 = col_form(ids_ref[1:2, :])
     n_e = lg.shape[1]
     ex = lnf[:, 0:n_e]
     diff = jnp.sum(
@@ -582,21 +575,9 @@
 
     @pl.loop(1, n_req)
     def _(d):
-        t1_copy(d).wait_recv()
-
-    @pl.loop(0, n_req)
-    def _(j):
-        t2[j] = t1[meta_s[1, j]]
-
-    def t2_copy(d):
-        j = lax.rem(r + d, n_req)
-        return req_copy(t2.at[j], got.at[r], s_t2.at[d], r_t2.at[d], j)
-
-    @pl.loop(1, n_req)
-    def _(d):
-        t2_copy(d).start()
-
-    got[r] = t2[r]
+        t1_copy(d).start()
+
+    t1[r] = tail_ref[r]
 
     tot = stat[...]
     for d in range(1, n_tp):
@@ -633,6 +614,24 @@
             ag_pass(*x_ag(h + 1))
         rs_send(*y_rs(h))
 
+    @pl.loop(1, n_req)
+    def _(d):
+        t1_copy(d).wait_recv()
+
+    @pl.loop(0, n_req)
+    def _(j):
+        t2[j] = t1[meta_s[1, j]]
+
+    def t2_copy(d):
+        j = lax.rem(r + d, n_req)
+        return req_copy(t2.at[j], got.at[r], s_t2.at[d], r_t2.at[d], j)
+
+    @pl.loop(1, n_req)
+    def _(d):
+        t2_copy(d).start()
+
+    got[r] = t2[r]
+
     def r_copy(d):
         j = lax.rem(r + d, n_req)
         return req_copy(rsend.at[block(j)], rrecv.at[block(r)], s_r.at[d], r_r.at[d], j)
@@ -654,16 +653,17 @@
 
     rrecv[block(r), :] = rsend[block(r), :]
 
+    for k in range(nslp // 128):
+        here = lnf + float(k * 128)
+        pick0[:, k * 128 : (k + 1) * 128] = (s0 == here).astype(F32).astype(BF16)
+        pick1[:, k * 128 : (k + 1) * 128] = (s1 == here).astype(F32).astype(BF16)
+
     @pl.loop(1, n_req)
     def _(d):
         r_copy(d).wait_recv()
 
-    p0 = jnp.zeros((rows, 128), F32)
-    p1 = jnp.zeros((rows, 128), F32)
-    for k in range(nslp // 128):
-        res = rrecv[k * 128 : (k + 1) * 128, :]
-        p0 = p0 + jnp.dot((s0 == lnf + float(k * 128)).astype(F32).astype(BF16), res, preferred_element_type=F32)
-        p1 = p1 + jnp.dot((s1 == lnf + float(k * 128)).astype(F32).astype(BF16), res, preferred_element_type=F32)
+    p0 = jnp.dot(pick0[...], rrecv[...], preferred_element_type=F32)
+    p1 = jnp.dot(pick1[...], rrecv[...], preferred_element_type=F32)
     mixed = (rf + gate * p0 + (1.0 - gate) * p1).astype(BF16)
 
     kk = lax.broadcasted_iota(jnp.int32, (16, rows), 0)
@@ -687,6 +687,20 @@
 
     mvr[r] = mvs[...]
 
+    rs_finish(*attn_rs)
+    for h in range(NCH):
+        rs_finish(*y_rs(h))
+        ag_finish(*x_ag(h), left=False)
+    for d in range(1, n_tp):
+        st_copy(d).wait_send()
+
+    @pl.loop(1, n_req)
+    def _(d):
+        t1_copy(d).wait_send()
+        d_copy(d).wait_send()
+        t2_copy(d).wait_send()
+        r_copy(d).wait_send()
+
     def cm_copy(d):
         return tp_copy(came.at[t], came.at[t], s_cm.at[d], r_cm.at[d], lax.rem(t + d, n_tp))
 
@@ -708,25 +722,16 @@
     def _(d):
         t2_copy(d).wait_recv()
 
-    rs_finish(*attn_rs)
-    for h in range(NCH):
-        rs_finish(*y_rs(h))
-        ag_finish(*x_ag(h))
     ag_finish(*o_ag)
     for d in range(1, n_tp):
-        st_copy(d).wait_send()
         cm_copy(d).wait_send()
 
     @pl.loop(1, n_req)
     def _(d):
-        t1_copy(d).wait_send()
-        d_copy(d).wait_send()
-        t2_copy(d).wait_send()
-        r_copy(d).wait_send()
         mv_copy(d).wait_send()
 
 
-def moe_call(n_req, n_tp, meta, parts, gain, router_t, ids_t, slots, send_tail, tail, hidden, w_out, wg_t, wu_t, wd):
+def moe_call(n_req, n_tp, meta, parts, gain, router_t, ids_t, send_tail, tail, hidden, w_out, wg_t, wu_t, wd):
     rows, width = hidden.shape
     cap = 5 * rows * TOP // (4 * n_req)
     nsl = n_req * cap
@@ -749,7 +754,7 @@
             jax.ShapeDtypeStruct((n_tp, 16, 128), BF16),
             jax.ShapeDtypeStruct((n_req, chunk, 128), BF16),
         ),
-        in_specs=[smem] + [vmem] * 10 + [anym] * 6,
+        in_specs=[smem] + [vmem] * 9 + [anym] * 6,
         out_specs=(vmem, vmem, vmem),
         scratch_shapes=[
             bf(*tail.shape), bf(rows, 128), bf(rows, 128), bf(*w_out.shape), bf(*wg_t.shape), bf(*wu_t.shape), bf(*wd.shape),
@@ -759,7 +764,7 @@
             bf(nslp, 128), bf(nslp, 128), bf(NCH, n_tp, crows, 128),
             bf(NCH, 2, n_x, crows, 128), bf(NCH, n_x, crows, 128), bf(NCH, n_x, crows, 128), bf(NCH, n_x, crows, 128),
             bf(nslp, 128), bf(nslp, 128),
-            bf(16, 128), bf(n_req, 16, 128),
+            bf(16, 128), bf(n_req, 16, 128), bf(nslp, rows), bf(rows, nslp), bf(rows, nslp),
         ]
         + [dma((5,))]
         + [dma((rows // (TB * 8),))]
@@ -773,7 +778,7 @@
         + [dma((n_tp,))] * 2,
         compiler_params=pltpu.CompilerParams(collective_id=0, has_side_effects=True, vmem_limit_bytes=56 << 20),
         name="moe_exchange",
-    )(meta, *parts, gain.reshape(1, -1), router_t, ids_t, slots, send_tail, tail, hidden, w_out, wg_t, wu_t, wd)
+    )(meta, *parts, gain.reshape(1, -1), router_t, ids_t, send_tail, tail, hidden, w_out, wg_t, wu_t, wd)
 
 
 def place_kernel(meta_s, mix_ref, came_ref, got_ref, tail_in, out_ref, tail_out, sems):
@@ -836,13 +841,13 @@
     n_req = lax.axis_size("req")
     n_tp = lax.axis_size("tp")
     ids_t = expert_ids.T
-    tail_new, send_tail, slots, meta, *parts = attention_call(
+    tail_new, send_tail, meta, *parts = attention_call(
         hidden_in, attn_gain, w_query, w_key, w_value, group_of, prompt_len, tail_len, bucket_of, bias_table.T,
-        new_slot, ids_t, prompt_kv, tail_kv,
+        new_slot, prompt_kv, tail_kv,
     )
     pieces = send_tail.reshape(n_req, -1, send_tail.shape[-1])
     mix, came, got = moe_call(
-        n_req, n_tp, meta, parts, ffn_gain, router_weight.T, ids_t, slots, pieces, tail_new, hidden_in, w_out,
+        n_req, n_tp, meta, parts, ffn_gain, router_weight.T, ids_t, pieces, tail_new, hidden_in, w_out,
         w_gate[0].T, w_up[0].T, w_down[0],
     )
     return place_call(meta, mix, came, got.reshape(send_tail.shape), tail_new)

time: 78.8 us -> 75.3 us (0.956)
  Pallas kernels: 77.9 us -> 74.5 us
    pallas_call x1, Pallas kernels: 14.9 us -> 11.8 us  [attention_call(): pl.pallas_call(attn_kernel, out_shape=(jax.ShapeDtypeStruct(tail_kv.shape...]
where the time goes in v6:
time: 75.3 us; the launch traced here: 75.1 us
  Pallas kernels  74.5 us (99%)
    pallas_call x1, Pallas kernels, moe_call(): pl.pallas_call(moe_kernel, out_shape=(jax.ShapeDtypeStruct((n_tp, rows, 1...  60 us
    pallas_call x1, Pallas kernels, attention_call(): pl.pallas_call(attn_kernel, out_shape=(jax.ShapeDtypeStruct(tail_kv.shape...  11.8 us
    pallas_call x1, Pallas kernels, place_call(): pl.pallas_call(place_kernel, out_shape=(jax.ShapeDtypeStruct((rows, n_tp...  2.61 us

profile of v6, /device:TPU:1, one launch (start us, length us, event | category | flops | bytes accessed | tf_op | source)
XLA Modules:
  0.0 75.1 jit_solution(7923297445968020310)
XLA Ops:
  0.6 11.8 %attention_tails.1 = (bf16[2,256,64,128]{3,2,1,0:T(8,128)(2,1)}, bf16[4,2,64,128]{3,2,1,0:T(8,128)(2,1)}, s32[8,128]{1,0:T(8,128)}, bf16[512,128]{1,0:T(8,128)(2...) custom-call(s32[256]{0:T(256)} %tl_s.1, f32[2,32]{1,0:T(2,128)} %bitcast.28, ...), custom_call_target="tpu_custom_call" | custom-call | tf_op jit(solution)/shard_map/attention_tails/pallas_call | solution.py:269
  12.5 60.0 %moe_exchange.1 = (bf16[8,256,128]{2,1,0:T(8,128)(2,1)}, bf16[8,16,128]{2,1,0:T(8,128)(2,1)}, bf16[16,32,128]{2,1,0:T(8,128)(2,1)}) custom-call(s32[8,128]{1,0:T(8,128)} %get-tuple-element.13.meta_s, bf16[512,128]{1,0:T(8,128)(2,1)} %get-tuple-element.14.q16, f32[512,128]{1,0:T(8,128)} %get-tuple-element.15.tbias, f32[512,128]{1,0:T(8,128)} %get-tuple-element.16.mpart, ...), custom_call_target="tpu_custom_call" | custom-call | tf_op jit(solution)/shard_map/moe_exchange/pallas_call | solution.py:750
  72.5 2.6 %place_rows.1 = (bf16[256,1024]{1,0:T(8,128)(2,1)}, bf16[2,256,64,128]{3,2,1,0:T(8,128)(2,1)}) custom-call(s32[8,128]{1,0:T(8,128)} %get-tuple-element.13.meta_s, bf16[8,256,128]{2,1,0:T(8,128)(2,1)} %get-tuple-element.21.mix_ref, bf16[8,16,128]{2,1,0:T(8,128)(2,1)} %get-tuple-element.22.came_ref, ...), custom_call_target="tpu_custom_call", output_to_operand_aliasing={{1}: (4, {})} | custom-call | tf_op jit(solution)/shard_map/place_rows/pallas_call | solution.py:823

commit v7 on v6

--- a/solution.py
+++ b/solution.py
@@ -387,8 +387,7 @@
     pair = lax.rem(sub16, 8) // 2
     lane4 = lax.broadcasted_iota(jnp.int32, (TB, 8, 128), 2)
 
-    @pl.loop(0, nkv)
-    def _(i):
+    def tail_attention(i):
         kv_load(i).wait()
         rs = pl.ds(pl.multiple_of(i * TB * 16, TB * 16), TB * 16)
         scs = []
@@ -419,13 +418,18 @@
         o = jnp.where(lane4 < 64, o[:, 0], o[:, 1]).reshape(TB * 8, 128)
         head_v[pl.ds(pl.multiple_of(i * TB * 8, TB * 8), TB * 8), :] = o.astype(BF16)
 
-    head = head_v[...]
+    hrows = rows // 2
+
+    def attn_part(h):
+        head = head_v[h * hrows : (h + 1) * hrows, :]
+        for tt in range(n_tp):
+            part[h, tt % 2, tt // 2] = jnp.dot(
+                head, wout_v[:, tt * 128 : (tt + 1) * 128], preferred_element_type=F32
+            ).astype(BF16)
+
+    pl.loop(0, nkv // 2)(tail_attention)
     loads[0].wait()
-    for tt in range(n_tp):
-        part[tt % 2, tt // 2] = jnp.dot(
-            head, wout_v[:, tt * 128 : (tt + 1) * 128], preferred_element_type=F32
-        ).astype(BF16)
-
+    attn_part(0)
     pl.semaphore_wait(barrier, n_tp - 1 + n_req - 1)
 
     def rs_sib(d, buf, dst, ss, rs):
@@ -494,9 +498,18 @@
         for d in (0, 1, 2, 3):
             ag_s(d, buf, ss2, rs2).wait_send()
 
-    attn_rs = (part, psib, psend, precv, s_ps, r_ps, s_px, r_px)
-    rs_start(part, psib, s_ps, r_ps)
-    rs_send(*attn_rs)
+    def attn_rs(h):
+        return (
+            part.at[h], psib.at[h], psend.at[h], precv.at[h], s_ps.at[h], r_ps.at[h], s_px.at[h], r_px.at[h]
+        )
+
+    rs_start(part.at[0], psib.at[0], s_ps.at[0], r_ps.at[0])
+    pl.loop(nkv // 2, nkv // 4 * 3)(tail_attention)
+    rs_send(*attn_rs(0))
+    pl.loop(nkv // 4 * 3, nkv)(tail_attention)
+    attn_part(1)
+    rs_start(part.at[1], psib.at[1], s_ps.at[1], r_ps.at[1])
+    rs_send(*attn_rs(1))
 
     def t1_copy(d):
         j = lax.rem(r + d, n_req)
@@ -523,7 +536,8 @@
         here = sl + float(k * 128)
         pickt[k * 128 : (k + 1) * 128, :] = ((here == row0) | (here == row1)).astype(F32).astype(BF16)
     loads[1].wait()
-    resid = (hid_v[...].astype(F32) + rs_total(*attn_rs)).astype(BF16)
+    attn = jnp.concatenate([rs_total(*attn_rs(h)) for h in range(2)], axis=0)
+    resid = (hid_v[...].astype(F32) + attn).astype(BF16)
 
     dsend[...] = jnp.dot(pickt[...], resid, preferred_element_type=F32).astype(BF16)
 
@@ -687,7 +701,8 @@
 
     mvr[r] = mvs[...]
 
-    rs_finish(*attn_rs)
+    for h in range(2):
+        rs_finish(*attn_rs(h))
     for h in range(NCH):
         rs_finish(*y_rs(h))
         ag_finish(*x_ag(h), left=False)
@@ -759,7 +774,8 @@
         scratch_shapes=[
             bf(*tail.shape), bf(rows, 128), bf(rows, 128), bf(*w_out.shape), bf(*wg_t.shape), bf(*wu_t.shape), bf(*wd.shape),
             bf(n_req, chunk, 128), bf(n_req, chunk, 128),
-            bf(2, n_x, rows, 128), bf(n_x, rows, 128), bf(n_x, rows, 128), bf(n_x, rows, 128),
+            bf(2, 2, n_x, rows // 2, 128), bf(2, n_x, rows // 2, 128), bf(2, n_x, rows // 2, 128),
+            bf(2, n_x, rows // 2, 128),
             pltpu.VMEM((8, rows), F32), pltpu.VMEM((n_tp, 8, rows), F32),
             bf(nslp, 128), bf(nslp, 128), bf(NCH, n_tp, crows, 128),
             bf(NCH, 2, n_x, crows, 128), bf(NCH, n_x, crows, 128), bf(NCH, n_x, crows, 128), bf(NCH, n_x, crows, 128),
@@ -769,7 +785,7 @@
         + [dma((5,))]
         + [dma((rows // (TB * 8),))]
         + [dma((n_req,))] * 4
-        + [dma((n_x,))] * 4
+        + [dma((2, n_x))] * 4
         + [dma((n_tp,))] * 2
         + [dma((n_req,))] * 2
         + [dma((NCH, n_x))] * 8

time: 75.3 us -> 73.9 us (0.981)
  Pallas kernels: 74.5 us -> 73 us
    pallas_call x1, Pallas kernels: 60 us -> 58.6 us  [moe_call(): pl.pallas_call(moe_kernel, out_shape=(jax.ShapeDtypeStruct((n_tp, rows, 1...]
where the time goes in v7:
time: 73.9 us; the launch traced here: 73.7 us
  Pallas kernels  73 us (99%)
    pallas_call x1, Pallas kernels, moe_call(): pl.pallas_call(moe_kernel, out_shape=(jax.ShapeDtypeStruct((n_tp, rows, 1...  58.6 us
    pallas_call x1, Pallas kernels, attention_call(): pl.pallas_call(attn_kernel, out_shape=(jax.ShapeDtypeStruct(tail_kv.shape...  11.8 us
    pallas_call x1, Pallas kernels, place_call(): pl.pallas_call(place_kernel, out_shape=(jax.ShapeDtypeStruct((rows, n_tp...  2.61 us

profile of v7, /device:TPU:1, one launch (start us, length us, event | category | flops | bytes accessed | tf_op | source)
XLA Modules:
  0.0 73.7 jit_solution(14779473589259551613)
XLA Ops:
  0.6 11.8 %attention_tails.1 = (bf16[2,256,64,128]{3,2,1,0:T(8,128)(2,1)}, bf16[4,2,64,128]{3,2,1,0:T(8,128)(2,1)}, s32[8,128]{1,0:T(8,128)}, bf16[512,128]{1,0:T(8,128)(2...) custom-call(s32[256]{0:T(256)} %tl_s.1, f32[2,32]{1,0:T(2,128)} %bitcast.28, ...), custom_call_target="tpu_custom_call" | custom-call | tf_op jit(solution)/shard_map/attention_tails/pallas_call | solution.py:269
  12.5 58.6 %moe_exchange.1 = (bf16[8,256,128]{2,1,0:T(8,128)(2,1)}, bf16[8,16,128]{2,1,0:T(8,128)(2,1)}, bf16[16,32,128]{2,1,0:T(8,128)(2,1)}) custom-call(s32[8,128]{1,0:T(8,128)} %get-tuple-element.13.meta_s, bf16[512,128]{1,0:T(8,128)(2,1)} %get-tuple-element.14.q16, f32[512,128]{1,0:T(8,128)} %get-tuple-element.15.tbias, f32[512,128]{1,0:T(8,128)} %get-tuple-element.16.mpart, ...), custom_call_target="tpu_custom_call" | custom-call | tf_op jit(solution)/shard_map/moe_exchange/pallas_call | solution.py:765
  71.0 2.6 %place_rows.1 = (bf16[256,1024]{1,0:T(8,128)(2,1)}, bf16[2,256,64,128]{3,2,1,0:T(8,128)(2,1)}) custom-call(s32[8,128]{1,0:T(8,128)} %get-tuple-element.13.meta_s, bf16[8,256,128]{2,1,0:T(8,128)(2,1)} %get-tuple-element.21.mix_ref, bf16[8,16,128]{2,1,0:T(8,128)(2,1)} %get-tuple-element.22.came_ref, ...), custom_call_target="tpu_custom_call", output_to_operand_aliasing={{1}: (4, {})} | custom-call | tf_op jit(solution)/shard_map/place_rows/pallas_call | solution.py:839
